TPU v7x, 32 devices: a whole 2x2x4 slice. The times are simulated.
32 devices in a mesh: groups: 2 (over y), rows: 4 (over z), cols: 2 (over x), sub: 2 (over core).
Axes of the slice: x: 2, y: 2, z: 4, core: 2. Of those that a mesh axis runs over, the one named last changes fastest.
Arguments:
- diagonal_tiles: float32 [256, 128, 128], P(('groups', 'rows', 'sub')), parts along dimension 0
- coupling_tiles: float32 [256, 6, 128, 128], P(('groups', 'rows', 'sub'), 'cols'), parts along dimension 0, may hold values from -0.0625 to 0.0625
- column_part: int32 [256, 6], P(('groups', 'rows', 'sub'), 'cols'), parts along dimension 0, may hold values from 0 to 4
- column_tile: int32 [256, 6], P(('groups', 'rows', 'sub'), 'cols'), parts along dimension 0, may hold values from 0 to 31
- neighbours: int32 [8, 4], P('groups'), parts along dimension 0, may hold values from 0 to 3, as said below
- right_side: float32 [256, 128], P(('groups', 'rows', 'sub')), parts along dimension 0, may hold values from -6 to 6
- jacobi_inverse: float32 [256, 128, 128], P(('groups', 'rows', 'sub')), parts along dimension 0, as said below
Outputs:
- solution: float32 [256, 128], P(('groups', 'rows', 'sub')), parts along dimension 0
- residual: float32 [256, 128], P(('groups', 'rows', 'sub')), parts along dimension 0
There are 2 independent parts, one for each index of `groups`. A program takes and returns all parts, laid end to end along the dimension named above; each array names one. Nothing has to cross between parts.
Inputs may be any that keep to these rules, and one draw needn't show every extreme that they name: `neighbours`: entry 0 of partition p's list is (p + 4 // 2) mod 4, the opposite partition on the cycle; every other entry names a partition whose index differs from p by 1 to 2 (without wrapping round); entries may repeat. `jacobi_inverse`: block-diagonal: each group of 5 consecutive variables, from the first on, forms one 5 x 5 block, and each variable left over after the last whole group of 5 is a 1 x 1 block of its own.
All inputs are finite; a program needn't handle non-finite values.
Results may differ from a plain program's by a relative error of at most 0.00019.
Values sent between devices are 32-bit elements; how exact they have to be, the bound alone decides.
No kernel may reach another device: no remote copies, remote signals or barrier semaphores. Data moves between devices by JAX's collectives and lax.ppermute only.
A program may use at most 64 MiB of HBM per device.

v0:
```python
import jax
import jax.numpy as jnp
from jax import lax
from jax.sharding import PartitionSpec as P

ITERS = 2


def transpose_apply(vector, diagonal_tiles, coupling_tiles, column_part, column_tile, neighbours):
    highest = lax.Precision.HIGHEST
    diagonal_part = jnp.einsum("rij,ri->rj", diagonal_tiles, vector, precision=highest)
    partial_value = jnp.einsum("rkij,ri->rkj", coupling_tiles, vector, precision=highest)
    tile_width = vector.shape[1]
    partial_value = partial_value.reshape(-1, tile_width)
    rows_dev = vector.shape[0]
    sub_count = lax.axis_size("sub")
    part_rows = rows_dev * sub_count
    own_part = lax.axis_index("rows")
    listed = neighbours[own_part]
    chosen = listed[jnp.maximum(column_part - 1, 0)]
    target = jnp.where(column_part == 0, own_part, chosen)
    landing = (target * part_rows + column_tile).reshape(-1)
    row_ids = lax.iota(jnp.int32, rows_dev * lax.axis_size(("rows", "sub")))
    one_hot = (row_ids[:, None] == landing[None, :]).astype(jnp.float32)
    owned = lax.psum_scatter(
        jnp.dot(one_hot, partial_value, precision=highest, preferred_element_type=jnp.float32),
        ("rows", "sub"),
        scatter_dimension=0,
        tiled=True,
    )
    owned = lax.psum(owned, "cols")
    return diagonal_part + owned


def precondition(jacobi_inverse, vector):
    return jnp.einsum("rij,ri->rj", jacobi_inverse, vector, precision=lax.Precision.HIGHEST)


def on_device(
    diagonal_tiles, coupling_tiles, column_part, column_tile, neighbours, right_side, jacobi_inverse
):

    def apply_a(vector):
        return transpose_apply(
            vector, diagonal_tiles, coupling_tiles, column_part, column_tile, neighbours
        )

    solution = jnp.zeros_like(right_side)
    residual = right_side
    search = right_side
    rho_now = lax.psum(jnp.sum(right_side * residual), ("rows", "sub"))
    for step in range(ITERS):
        search_hat = precondition(jacobi_inverse, search)
        image = apply_a(search_hat)
        alpha = rho_now / lax.psum(jnp.sum(right_side * image), ("rows", "sub"))
        half = residual - alpha * image
        half_hat = precondition(jacobi_inverse, half)
        twice = apply_a(half_hat)
        cross, square, shadow_half, shadow_twice = lax.psum(
            (
                jnp.sum(twice * half),
                jnp.sum(twice * twice),
                jnp.sum(right_side * half),
                jnp.sum(right_side * twice),
            ),
            ("rows", "sub"),
        )
        omega = cross / square
        solution = solution + alpha * search_hat + omega * half_hat
        residual = half - omega * twice
        if step + 1 < ITERS:
            rho_next = shadow_half - omega * shadow_twice
            search = residual + rho_next / rho_now * (alpha / omega) * (search - omega * image)
            rho_now = rho_next
    return (solution, residual)


def solution(mesh):
    in_specs = (
        P(("groups", "rows", "sub"), None, None),
        P(("groups", "rows", "sub"), "cols", None, None),
        P(("groups", "rows", "sub"), "cols"),
        P(("groups", "rows", "sub"), "cols"),
        P("groups", None),
        P(("groups", "rows", "sub"), None),
        P(("groups", "rows", "sub"), None, None),
    )
    out_specs = (P(("groups", "rows", "sub"), None), P(("groups", "rows", "sub"), None))
    return jax.shard_map(
        on_device, mesh=mesh, in_specs=in_specs, out_specs=out_specs, check_vma=False
    )
```

profile of v0, /device:TPU:0, one launch (start us, length us, event | category | flops | bytes accessed | tf_op | source)
XLA Modules:
  0.0 245.4 jit_solution(2506493067648481065)
XLA Ops:
  10.0 2.2 fusion.24
  12.2 1.9 fusion.20
  15.0 2.2 fusion.22
  17.2 31.2 %reduce-scatter.5.cloned.1.call-done = f32[16,128]{1,0:T(8,128)} async-done(((f32[128,128]{1,0:T(8,128)}), f32[16,128]{1,0:T(8,128)}) %reduce-scatter.5.cloned.1.call-update) | async-done | bytes 8208 | tf_op jit(solution)/shard_map/reduce_scatter | solution.py:25
  48.4 5.1 %psum.92 = f32[16,128]{1,0:T(8,128)S(1)} all-reduce(f32[16,128]{1,0:T(8,128)} %reduce-scatter.5.cloned.1.call-done), channel_id=1, replica_groups=mesh['groups'=2,'rows'=4,'cols'=2,'sub'=2] {'cols'}, use_global_device_ids=true, to_apply=%region_3.4 | all-reduce | flops 2048 | bytes 16384 | tf_op jit(solution)/shard_map/psum | solution.py:31
  54.1 14.2 %all-reduce.2 = (f32[]{:T(128)}, f32[]{:T(128)}) all-reduce(f32[]{:T(128)} %get-tuple-element.9, f32[]{:T(128)} %get-tuple-element.8), channel_id=1, replica_groups=mesh['groups'=2,'rows'=4,'cols'=2,'sub'=2] {'rows','sub'}, use_global_device_ids=true, to_apply=%region_1.0 | all-reduce | flops 2 | bytes 16 | tf_op jit(solution)/shard_map/psum | solution.py:51
  69.6 2.2 fusion.25
  71.8 1.9 fusion.16
  74.6 2.2 fusion.18
  76.8 26.5 %reduce-scatter.7.cloned.1.call-done = f32[16,128]{1,0:T(8,128)} async-done(((f32[128,128]{1,0:T(8,128)}), f32[16,128]{1,0:T(8,128)}) %reduce-scatter.7.cloned.1.call-update) | async-done | bytes 8208 | tf_op jit(solution)/shard_map/reduce_scatter | solution.py:25
  103.2 5.1 %psum.94 = f32[16,128]{1,0:T(8,128)S(1)} all-reduce(f32[16,128]{1,0:T(8,128)} %reduce-scatter.7.cloned.1.call-done), channel_id=1, replica_groups=mesh['groups'=2,'rows'=4,'cols'=2,'sub'=2] {'cols'}, use_global_device_ids=true, to_apply=%region_7.8 | all-reduce | flops 2048 | bytes 16384 | tf_op jit(solution)/shard_map/psum | solution.py:31
  109.0 14.3 %all-reduce.1 = (f32[]{:T(128)}, f32[]{:T(128)}, f32[]{:T(128)}, f32[]{:T(128)}) all-reduce(f32[]{:T(128)} %get-tuple-element.7, f32[]{:T(128)} %get-tuple-element.6, f32[]{:T(128)} %get-tuple-element.5, f32[]{:T(128)} %get-tuple-element.4), channel_id=1, replica_groups=mesh['groups'=2,'rows'=4,'cols'=2,'sub'=2] {'rows','sub'}, use_global_device_ids=true, to_apply=%region_13.14 | all-reduce | flops 4 | bytes 32 | tf_op jit(solution)/shard_map/psum | solution.py:59
  129.0 2.2 fusion.26
  131.2 1.9 fusion.12
  134.2 2.2 fusion.14
  136.3 26.4 %reduce-scatter.9.cloned.1.call-done = f32[16,128]{1,0:T(8,128)} async-done(((f32[128,128]{1,0:T(8,128)}), f32[16,128]{1,0:T(8,128)}) %reduce-scatter.9.cloned.1.call-update) | async-done | bytes 8208 | tf_op jit(solution)/shard_map/reduce_scatter | solution.py:25
  162.7 5.1 %psum.99 = f32[16,128]{1,0:T(8,128)S(1)} all-reduce(f32[16,128]{1,0:T(8,128)} %reduce-scatter.9.cloned.1.call-done), channel_id=1, replica_groups=mesh['groups'=2,'rows'=4,'cols'=2,'sub'=2] {'cols'}, use_global_device_ids=true, to_apply=%region_17.18 | all-reduce | flops 2048 | bytes 16384 | tf_op jit(solution)/shard_map/psum | solution.py:31
  168.4 14.2 %psum.100 = f32[]{:T(128)} all-reduce(f32[]{:T(128)} %get-tuple-element.19), channel_id=1, replica_groups=mesh['groups'=2,'rows'=4,'cols'=2,'sub'=2] {'rows','sub'}, use_global_device_ids=true, to_apply=%region_19.20 | all-reduce | flops 1 | bytes 8 | tf_op jit(solution)/shard_map/psum | solution.py:55
  183.3 2.2 fusion.27
  185.5 1.9 fusion.8
  188.2 2.2 fusion.10
  190.4 26.6 %reduce-scatter.11.cloned.1.call-done = f32[16,128]{1,0:T(8,128)} async-done(((f32[128,128]{1,0:T(8,128)}), f32[16,128]{1,0:T(8,128)}) %reduce-scatter.11.cloned.1.call-update) | async-done | bytes 8208 | tf_op jit(solution)/shard_map/reduce_scatter | solution.py:25
  217.0 5.1 %psum.101 = f32[16,128]{1,0:T(8,128)S(1)} all-reduce(f32[16,128]{1,0:T(8,128)} %reduce-scatter.11.cloned.1.call-done), channel_id=1, replica_groups=mesh['groups'=2,'rows'=4,'cols'=2,'sub'=2] {'cols'}, use_global_device_ids=true, to_apply=%region_21.22 | all-reduce | flops 2048 | bytes 16384 | tf_op jit(solution)/shard_map/psum | solution.py:31
  222.7 14.2 %all-reduce = (f32[]{:T(128)}, f32[]{:T(128)}) all-reduce(f32[]{:T(128)} %get-tuple-element.3, f32[]{:T(128)} %get-tuple-element.2), channel_id=1, replica_groups=mesh['groups'=2,'rows'=4,'cols'=2,'sub'=2] {'rows','sub'}, use_global_device_ids=true, to_apply=%region_23.24 | all-reduce | flops 2 | bytes 16 | tf_op jit(solution)/shard_map/psum | solution.py:59
  (44 shorter events, 9.5 us)
Async XLA Ops:
  7.2 5.1 %copy-start = (f32[16,3,128,128]{3,2,1,0:T(8,128)S(1)}, f32[16,3,128,128]{3,2,1,0:T(8,128)}, u32[]{:S(2)}) copy-start(f32[16,3,128,128]{3,2,1,0:T(8,128)} %param.8) | copy-start | bytes 9437188
  7.2 41.2 %reduce-scatter.5.cloned.1.call-start = ((), (), s32[]{:S(2)}) async-start(), calls=%async_computation.4 | async-start | bytes 73728 | tf_op jit(solution)/shard_map/reduce_scatter | solution.py:25
  8.9 0.9 copy-start.2
  8.9 1.1 copy-start.1
  14.9 88.3 %reduce-scatter.7.cloned.1.call-start = ((), (), s32[]{:S(2)}) async-start(), calls=%async_computation.5 | async-start | bytes 73728 | tf_op jit(solution)/shard_map/reduce_scatter | solution.py:25
  74.5 88.2 %reduce-scatter.9.cloned.1.call-start = ((), (), s32[]{:S(2)}) async-start(), calls=%async_computation.6 | async-start | bytes 73728 | tf_op jit(solution)/shard_map/reduce_scatter | solution.py:25
  133.9 83.1 %reduce-scatter.11.cloned.1.call-start = ((), (), s32[]{:S(2)}) async-start(), calls=%async_computation.7 | async-start | bytes 73728 | tf_op jit(solution)/shard_map/reduce_scatter | solution.py:25
Sparse Core Ops, SparseCore 0:
  15.1 33.2 reduce-scatter.4
  74.7 28.5 reduce-scatter.6
  134.0 28.6 reduce-scatter.8
  188.4 28.6 reduce-scatter.10
where the time goes:
time: 246 us; the launch traced here: 245 us
  waiting for transfers between devices  111 us (45%)
  blocking collectives  77.3 us (31%)
  matrix products  28.1 us (11%)
  between operations  23 us (9%)
  other arithmetic  3.16 us (1%)
  local copies, waits for them, and re-layouts  2.84 us (1%)
    reduce_scatter x4, waiting for transfers between devices, transpose_apply(): lax.psum_scatter(jnp.dot(one_hot, partial_value, precision=highest, prefe...  111 us
    psum x2, blocking collectives, on_device(): lax.psum((jnp.sum(twice * half), jnp.sum(twice * twice), jnp.sum(right_si...  28.5 us
    psum x4, blocking collectives, transpose_apply(): owned = lax.psum(owned, 'cols')  20.3 us
    psum x1, blocking collectives, on_device(): rho_now = lax.psum(jnp.sum(right_side * residual), ('rows', 'sub'))  14.2 us
    psum x1, blocking collectives, on_device(): alpha = rho_now / lax.psum(jnp.sum(right_side * image), ('rows', 'sub'))  14.2 us
    dot_general x4, matrix products, precondition(): jnp.einsum('rij,ri->rj', jacobi_inverse, vector, precision=lax.Precision....  8.77 us
    dot_general x4, matrix products, transpose_apply(): jnp.einsum('rij,ri->rj', diagonal_tiles, vector, precision=highest)  8.74 us
    dot_general x4, matrix products, transpose_apply(): jnp.einsum('rkij,ri->rkj', coupling_tiles, vector, precision=highest)  7.46 us
  transfers between devices with their start and end apart: 4, of which 4 were waited for; matrix products, arithmetic and copies ran while one was open for 4% of the time, Pallas kernels for 0%

commit v1 on v0

v1 whole, which is shorter than its diff:
```python
import functools

import jax
import jax.numpy as jnp
from jax import lax
from jax.experimental import pallas as pl
from jax.experimental.pallas import tpu as pltpu
from jax.sharding import PartitionSpec as P

BLOCK = 5
BAND = BLOCK - 1
LANES = 128
PART = ("rows", "cols", "sub")


def apply_m(band_ref, v):
    width = v.shape[1]
    z = band_ref[BAND] * v
    for d in range(-BAND, BAND + 1):
        if d:
            z = z + band_ref[d + BAND] * pltpu.roll(v, (-d) % width, 1)
    return z


def split3(x):
    hi = x.astype(jnp.bfloat16)
    rest = x - hi.astype(jnp.float32)
    mid = rest.astype(jnp.bfloat16)
    low = (rest - mid.astype(jnp.float32)).astype(jnp.bfloat16)
    return jnp.concatenate([hi, mid, low], axis=0)


def products(z, coupling_ref, diagonal_ref, partial_ref, own_ref):
    rows, slots = coupling_ref.shape[0], coupling_ref.shape[1]
    z_t = z.T
    for r in range(rows):
        column = jnp.broadcast_to(z_t[:, r : r + 1], coupling_ref.shape[2:])
        for k in range(slots):
            partial_ref[pl.ds(k * rows + r, 1), :] = jnp.sum(column * coupling_ref[r, k], axis=0, keepdims=True)
        own_ref[pl.ds(r, 1), :] = jnp.sum(column * diagonal_ref[r], axis=0, keepdims=True)


def emit(z, tail, spread_ref, coupling_ref, diagonal_ref, partial_ref, own_ref, send_ref):
    rows = z.shape[0]
    products(z, coupling_ref, diagonal_ref, partial_ref, own_ref)
    send_ref[...] = jnp.dot(spread_ref[...], split3(partial_ref[...]), preferred_element_type=jnp.float32)
    for d in range(send_ref.shape[0] // (rows + 1)):
        send_ref[pl.ds(d * (rows + 1) + rows, 1), :] = tail


def pack(scalars, width):
    lane = lax.broadcasted_iota(jnp.int32, (1, width), 1)
    tail = jnp.zeros((1, width), jnp.float32)
    for at, value in enumerate(scalars):
        tail = jnp.where(lane == at, value, tail)
    return tail


def total(x):
    return jnp.sum(jnp.sum(x, axis=0, keepdims=True), axis=1, keepdims=True)


def peak(x):
    return jnp.max(jnp.max(jnp.abs(x), axis=0, keepdims=True), axis=1, keepdims=True)


def level(x, like):
    size, aim = peak(x), peak(like)
    good = (size > 0) & (aim > 0)
    return jnp.where(good, aim / size, 1.0), jnp.where(good, size / aim, 1.0)


def gather_tails(recv_ref, rows):
    count = recv_ref.shape[0] // (rows + 1)
    return [recv_ref[pl.ds(d * (rows + 1) + rows, 1), :] for d in range(count)]


def chunk(recv_ref, d, rows):
    return recv_ref[pl.ds(d * (rows + 1), rows), :]


def first_kernel(
    b_ref, jacobi_ref, part_ref, tile_ref, near_ref, coupling_ref, diagonal_ref,
    send_ref, own_ref, band_ref, spread_ref, partial_ref, *, sizes,
):
    n_rows, n_cols, n_sub = sizes
    rows, slots = coupling_ref.shape[0], coupling_ref.shape[1]
    width = b_ref.shape[1]
    folded = jnp.sum(jacobi_ref[...].reshape(rows, width // 8, 8, width), axis=1)
    m = lax.broadcasted_iota(jnp.int32, (1, 8, width), 1)
    j = lax.broadcasted_iota(jnp.int32, (1, 8, width), 2)
    last = width // BLOCK * BLOCK
    for d in range(-BAND, BAND + 1):
        i = j + d
        inside = (i // BLOCK == j // BLOCK) & (j < last) if d else j >= 0
        picked = inside & (i >= 0) & (lax.rem(i + 8, 8) == m)
        band_ref[d + BAND] = jnp.sum(jnp.where(picked, folded, 0.0), axis=1)
    own = lax.axis_index("rows")
    part, tile = part_ref[...], tile_ref[...]
    near = near_ref[...]
    near_row = lax.broadcasted_iota(jnp.int32, near.shape, 0)
    mine = jnp.sum(jnp.where(near_row == own, near, 0), axis=0, keepdims=True)
    target = jnp.where(part == 0, own, 0)
    for n in range(near.shape[1]):
        target = target + jnp.where(part == n + 1, mine[:, n : n + 1], 0)
    landing = target * (rows * n_sub) + tile
    lanes = -(-spread_ref.shape[0] // LANES) * LANES
    at = lax.broadcasted_iota(jnp.int32, (rows, lanes), 1)
    device, line = at // (rows + 1), at % (rows + 1)
    row, sub = device // (n_cols * n_sub), device % n_sub
    wanted = jnp.where((line < rows) & (row < n_rows), row * (rows * n_sub) + sub * rows + line, -1)
    hits = jnp.concatenate(
        [(landing[:, k : k + 1] == wanted).astype(jnp.float32) for k in range(slots)], axis=0
    )
    one_hot = hits.T[: spread_ref.shape[0]].astype(jnp.bfloat16)
    spread_ref[...] = jnp.concatenate([one_hot] * 3, axis=1)
    z = apply_m(band_ref, b_ref[...])
    emit(z, jnp.zeros((1, width), jnp.float32), spread_ref, coupling_ref, diagonal_ref, partial_ref, own_ref, send_ref)


def second_kernel(
    recv_ref, own_in, b_ref, band_ref, spread_ref, coupling_ref, diagonal_ref,
    send_ref, own_ref, q_ref, partial_ref,
):
    b = b_ref[...]
    rows, width = b.shape
    q = own_in[...]
    for d in range(recv_ref.shape[0] // (rows + 1)):
        q = q + chunk(recv_ref, d, rows)
    q_ref[...] = q
    up, down = level(q, b)
    tail = pack([total(b * b), total(b * q), down], width)
    z = apply_m(band_ref, q * up)
    emit(z, tail, spread_ref, coupling_ref, diagonal_ref, partial_ref, own_ref, send_ref)


def scalars_of(recv_ref, rows, count, repeats):
    tails = gather_tails(recv_ref, rows)
    summed = functools.reduce(jnp.add, tails)
    return tails, [summed[:, n : n + 1] / repeats for n in range(count)]


def weighted(recv_ref, own_in, own_down, tails, at, factor):
    rows = own_in.shape[0]
    out = own_in[...] * (factor * own_down)
    for d, tail in enumerate(tails):
        out = out + chunk(recv_ref, d, rows) * (factor * tail[:, at : at + 1])
    return out


def third_kernel(
    recv_ref, own_in, b_ref, q_ref, band_ref, spread_ref, coupling_ref, diagonal_ref,
    send_ref, own_ref, twice_ref, half_ref, u_ref, keep_ref, partial_ref, *, n_cols,
):
    b, q = b_ref[...], q_ref[...]
    rows, width = b.shape
    tails, (rho, cross) = scalars_of(recv_ref, rows, 2, n_cols)
    alpha = rho / cross
    _, down = level(q, b)
    u = weighted(recv_ref, own_in, down, tails, 2, alpha)
    twice = q - u
    half = b - alpha * q
    up, down = level(twice, half)
    tail = pack([total(twice * half), total(twice * twice), total(b * half), total(b * twice), down], width)
    twice_ref[...], half_ref[...], u_ref[...] = twice, half, u
    keep_ref[...] = pack([rho, alpha], width)
    z = apply_m(band_ref, twice * up)
    emit(z, tail, spread_ref, coupling_ref, diagonal_ref, partial_ref, own_ref, send_ref)


def fourth_kernel(
    recv_ref, own_in, b_ref, q_ref, twice_ref, half_ref, u_ref, keep_ref, band_ref, spread_ref, coupling_ref,
    diagonal_ref, send_ref, own_ref, a_ref, residual_ref, image_ref, search_ref, done_ref, kept_ref, partial_ref,
    *, n_cols,
):
    b, q, twice, half = b_ref[...], q_ref[...], twice_ref[...], half_ref[...]
    rows, width = b.shape
    rho, alpha = keep_ref[:, 0:1], keep_ref[:, 1:2]
    tails, (cross, square, b_half, b_twice) = scalars_of(recv_ref, rows, 4, n_cols)
    omega = cross / square
    rho_next = b_half - omega * b_twice
    ratio = rho_next / rho
    beta = ratio * (alpha / omega)
    _, down = level(twice, half)
    a = twice - weighted(recv_ref, own_in, down, tails, 4, omega)
    residual = half - omega * twice
    image = a + beta * q - ratio * u_ref[...]
    up, down = level(image, residual)
    tail = pack([total(b * image), down], width)
    a_ref[...], residual_ref[...], image_ref[...] = a, residual, image
    search_ref[...] = residual + beta * (b - omega * q)
    done_ref[...] = alpha * b + omega * half
    kept_ref[...] = pack([rho_next], width)
    z = apply_m(band_ref, image * up)
    emit(z, tail, spread_ref, coupling_ref, diagonal_ref, partial_ref, own_ref, send_ref)


def fifth_kernel(
    recv_ref, own_in, a_ref, residual_ref, image_ref, search_ref, done_ref, kept_ref,
    twice_ref, half_ref, sum_ref, dots_ref, *, n_cols,
):
    residual, image = residual_ref[...], image_ref[...]
    rows, width = residual.shape
    tails, (cross,) = scalars_of(recv_ref, rows, 1, n_cols)
    alpha = kept_ref[:, 0:1] / cross
    _, down = level(image, residual)
    twice = a_ref[...] - weighted(recv_ref, own_in, down, tails, 1, alpha)
    half = residual - alpha * image
    twice_ref[...], half_ref[...] = twice, half
    sum_ref[...] = done_ref[...] + alpha * search_ref[...]
    dots_ref[...] = pack([total(twice * half), total(twice * twice)], width)


def last_kernel(dots_ref, twice_ref, half_ref, sum_ref, band_ref, solution_ref, residual_ref):
    dots = dots_ref[...]
    omega = dots[:, 0:1] / dots[:, 1:2]
    half = half_ref[...]
    residual_ref[...] = half - omega * twice_ref[...]
    solution_ref[...] = apply_m(band_ref, sum_ref[...] + omega * half)


def partners(count, step):
    if count & (count - 1) == 0:
        return [(i, i ^ step) for i in range(count)]
    return [(i, (i + step) % count) for i in range(count)]


def sum_over(x, axis):
    count = lax.axis_size(axis)
    out = x
    for step in range(1, count):
        out = out + lax.ppermute(x, axis, partners(count, step))
    return out


def call(kernel, outs, args, scratch=()):
    spec = pl.BlockSpec(memory_space=pltpu.VMEM)
    return pl.pallas_call(
        kernel,
        out_shape=[jax.ShapeDtypeStruct(shape, kind) for shape, kind in outs],
        in_specs=[spec] * len(args),
        out_specs=[spec] * len(outs),
        scratch_shapes=list(scratch),
        compiler_params=pltpu.CompilerParams(vmem_limit_bytes=48 << 20),
    )(*args)


def on_device(diagonal, coupling, column_part, column_tile, neighbours, b, jacobi):
    f32 = jnp.float32
    rows, width = b.shape
    slots = coupling.shape[1]
    sizes = tuple(lax.axis_size(axis) for axis in PART)
    n_cols = sizes[1]
    devices = sizes[0] * sizes[1] * sizes[2]
    vec, line = ((rows, width), f32), ((1, width), f32)
    message = ((devices * (rows + 1), width), f32)
    band_shape = ((2 * BAND + 1, rows, width), f32)
    spread_shape = ((devices * (rows + 1), 3 * slots * rows), jnp.bfloat16)
    scratch = [pltpu.VMEM((slots * rows, width), f32)]

    def exchange(send):
        send = send.reshape(devices, rows + 1, 1, width)
        return lax.all_to_all(send, PART, 0, 0, tiled=True).reshape(devices * (rows + 1), width)

    send, own, band, spread = call(
        functools.partial(first_kernel, sizes=sizes), [message, vec, band_shape, spread_shape],
        (b, jacobi, column_part, column_tile, neighbours, coupling, diagonal), scratch,
    )
    fixed = (band, spread, coupling, diagonal)
    send, own, q = call(second_kernel, [message, vec, vec], (exchange(send), own, b) + fixed, scratch)
    send, own, twice, half, u, keep = call(
        functools.partial(third_kernel, n_cols=n_cols), [message] + [vec] * 4 + [line],
        (exchange(send), own, b, q) + fixed, scratch,
    )
    send, own, a, residual, image, search, done, kept = call(
        functools.partial(fourth_kernel, n_cols=n_cols), [message] + [vec] * 6 + [line],
        (exchange(send), own, b, q, twice, half, u, keep) + fixed, scratch,
    )
    twice, half, summed, dots = call(
        functools.partial(fifth_kernel, n_cols=n_cols), [vec] * 3 + [line],
        (exchange(send), own, a, residual, image, search, done, kept),
    )
    dots = sum_over(sum_over(dots, "sub"), "rows")
    return tuple(call(last_kernel, [vec, vec], (dots, twice, half, summed, band)))


def solution(mesh):
    lines = P(("groups", "rows", "sub"), None)
    tiles = P(("groups", "rows", "sub"), None, None)
    slots = P(("groups", "rows", "sub"), "cols")
    in_specs = (
        tiles, P(("groups", "rows", "sub"), "cols", None, None), slots, slots, P("groups", None), lines, tiles,
    )
    return jax.shard_map(on_device, mesh=mesh, in_specs=in_specs, out_specs=(lines, lines), check_vma=False)
```

time: 246 us -> 68.8 us (0.28)
  waiting for transfers between devices: 111 us -> 2.7 us
  blocking collectives: 77.3 us -> 47.2 us
  matrix products: 28.1 us -> 0 us
  between operations: 23 us -> 0.68 us
  Pallas kernels: 0 us -> 6.03 us
  local copies, waits for them, and re-layouts: 2.84 us -> 7.24 us
  starting transfers between devices: 0.34 us -> 4.39 us
  other arithmetic: 3.16 us -> 0.01 us
    reduce_scatter x4 -> x0, waiting for transfers between devices: 111 us -> none  [transpose_apply(): lax.psum_scatter(jnp.dot(one_hot, partial_value, precision=highest, prefe...]
    psum x8 -> x0, blocking collectives: 77.3 us -> none  [the longest x2 28.5 us: on_device(): lax.psum((jnp.sum(twice * half), jnp.sum(twice * twice), jnp.sum(right_si...]
    all_to_all x0 -> x4, blocking collectives: none -> 47.2 us  [exchange(): lax.all_to_all(send, PART, 0, 0, tiled=True)]
    dot_general x16 -> x0, matrix products: 28.1 us -> none  [the longest x4 8.77 us: precondition(): jnp.einsum('rij,ri->rj', jacobi_inverse, vector, precision=lax.Precision....]
    unnamed x8 -> x16, local copies, waits for them, and re-layouts: 1.01 us -> 7.24 us
    pallas_call x0 -> x6, Pallas kernels: none -> 6.03 us  [call(): pl.pallas_call(kernel, out_shape=[jax.ShapeDtypeStruct(shape, kind) for s...]
    ppermute x0 -> x4, starting transfers between devices: none -> 4.39 us  [sum_over(): out = out + lax.ppermute(x, axis, partners(count, step))]
    ppermute x0 -> x4, waiting for transfers between devices: none -> 2.7 us  [sum_over(): out = out + lax.ppermute(x, axis, partners(count, step))]
  transfers between devices with their start and end apart: 4 -> 4, of which waited for: 4 -> 3; matrix products, arithmetic and copies ran while one was open for 4% -> 0% of each run, Pallas kernels for 0% -> 0%
where the time goes in v1:
time: 68.8 us; the launch traced here: 68.3 us
  blocking collectives  47.2 us (69%)
  local copies, waits for them, and re-layouts  7.24 us (11%)
  Pallas kernels  6.03 us (9%)
  starting transfers between devices  4.39 us (6%)
  waiting for transfers between devices  2.7 us (4%)
    all_to_all x4, blocking collectives, exchange(): lax.all_to_all(send, PART, 0, 0, tiled=True)  47.2 us
    unnamed x16, local copies, waits for them, and re-layouts  7.24 us
    pallas_call x6, Pallas kernels, call(): pl.pallas_call(kernel, out_shape=[jax.ShapeDtypeStruct(shape, kind) for s...  6.03 us
    ppermute x4, starting transfers between devices, sum_over(): out = out + lax.ppermute(x, axis, partners(count, step))  4.39 us
    ppermute x4, waiting for transfers between devices, sum_over(): out = out + lax.ppermute(x, axis, partners(count, step))  2.7 us
  transfers between devices with their start and end apart: 4, of which 3 were waited for; matrix products, arithmetic and copies ran while one was open for 0% of the time, Pallas kernels for 0%

profile of v1, /device:TPU:0, one launch (start us, length us, event | category | flops | bytes accessed | tf_op | source)
XLA Modules:
  0.0 68.3 jit_solution(9280779630092010304)
XLA Ops:
  0.6 0.8 %copy.13.part_ref = s32[16,3]{1,0:T(8,128)S(1)} copy(s32[16,3]{0,1:T(4,128)} %param.9) | data formatting | bytes 384 | tf_op args[2]
  1.4 0.8 %copy.14.tile_ref = s32[16,3]{1,0:T(8,128)S(1)} copy(s32[16,3]{0,1:T(4,128)} %param.10) | data formatting | bytes 384 | tf_op args[3]
  2.1 1.9 %copy-done = f32[16,3,128,128]{3,2,1,0:T(8,128)S(1)} copy-done((f32[16,3,128,128]{3,2,1,0:T(8,128)S(1)}, f32[16,3,128,128]{3,2,1,0:T(8,128)}, u32[]{:S(2)}) %copy-start) | copy-done | bytes 3145752
  4.0 1.2 %copy-done.2 = f32[16,128,128]{2,1,0:T(8,128)S(1)} copy-done((f32[16,128,128]{2,1,0:T(8,128)S(1)}, f32[16,128,128]{2,1,0:T(8,128)}, u32[]{:S(2)}) %copy-start.2) | copy-done | bytes 1048600
  5.3 1.2 %copy-done.4 = f32[16,128,128]{2,1,0:T(8,128)S(1)} copy-done((f32[16,128,128]{2,1,0:T(8,128)S(1)}, f32[16,128,128]{2,1,0:T(8,128)}, u32[]{:S(2)}) %copy-start.4) | copy-done | bytes 1048600
  6.5 0.7 %copy-done.5 = f32[16,128]{1,0:T(8,128)S(1)} copy-done((f32[16,128]{1,0:T(8,128)S(1)}, f32[16,128]{1,0:T(8,128)}, u32[]{:S(2)}) %copy-start.5) | copy-done | bytes 8216
  7.2 0.7 copy-done.6
  7.9 1.1 %shard_map.86 = (f32[272,128]{1,0:T(8,128)S(1)}, f32[16,128]{1,0:T(8,128)S(1)}, f32[9,16,128]{2,1,0:T(8,128)S(1)}, bf16[272,144]{1,0:T(8,128)(2,1)S(1)}) custom-call(f32[16,128]{1,0:T(8,128)S(1)} %copy-done.5, f32[16,128,128]{2,1,0:T(8,128)S(1)} %copy-done.4, s32[16,3]{1,0:T(8,128)S(1)} %copy.13.part_ref, s32[16,3]{1,0:T(8,128)S(1)} %copy.14.tile_ref, ...), custom_call_target="tpu_custom_call" | custom-call | tf_op jit(solution)/shard_map/pallas_call | solution.py:238
  9.0 15.4 %all_to_all.20 = f32[16,17,1,128]{3,2,1,0:T(1,128)S(1)} all-to-all(f32[16,17,1,128]{3,2,1,0:T(1,128)S(1)} %bitcast.14), channel_id=1, replica_groups=mesh['groups'=2,'rows'=4,'cols'=2,'sub'=2] {'rows','cols','sub'}, dimensions={0} | all-to-all | bytes 278528 | tf_op jit(solution)/shard_map/all_to_all | solution.py:263
  24.4 1.1 %shard_map.87 = (f32[272,128]{1,0:T(8,128)S(1)}, f32[16,128]{1,0:T(8,128)S(1)}, f32[16,128]{1,0:T(8,128)S(1)}) custom-call(f32[272,128]{1,0:T(8,128)S(1)} %bitcast.10, f32[16,128]{1,0:T(8,128)S(1)} %get-tuple-element.28.own_in, f32[16,128]{1,0:T(8,128)S(1)} %copy-done.5, f32[9,16,128]{2,1,0:T(8,128)S(1)} %get-tuple-element.29.band_ref, ...), custom_call_target="tpu_custom_call" | custom-call | tf_op jit(solution)/shard_map/pallas_call | solution.py:238
  25.5 10.6 %all_to_all.21 = f32[16,17,1,128]{3,2,1,0:T(1,128)S(1)} all-to-all(f32[16,17,1,128]{3,2,1,0:T(1,128)S(1)} %bitcast.15), channel_id=1, replica_groups=mesh['groups'=2,'rows'=4,'cols'=2,'sub'=2] {'rows','cols','sub'}, dimensions={0} | all-to-all | bytes 278528 | tf_op jit(solution)/shard_map/all_to_all | solution.py:263
  36.1 1.3 %shard_map.88 = (f32[272,128]{1,0:T(8,128)S(1)}, f32[16,128]{1,0:T(8,128)S(1)}, f32[16,128]{1,0:T(8,128)S(1)}, f32[16,128]{1,0:T(8,128)S(1)}, f32[16,128]{1,0:T(8,128)S(1)}, /*index=5*/f32[1,128]{1,0:T(1,128)S(1)}) custom-call(f32[272,128]{1,0:T(8,128)S(1)} %bitcast.9, f32[16,128]{1,0:T(8,128)S(1)} %get-tuple-element.32.own_in, f32[16,128]{1,0:T(8,128)S(1)} %copy-done.5, ...), custom_call_target="tpu_custom_call" | custom-call | tf_op jit(solution)/shard_map/pallas_call | solution.py:238
  37.4 10.6 %all_to_all.22 = f32[16,17,1,128]{3,2,1,0:T(1,128)S(1)} all-to-all(f32[16,17,1,128]{3,2,1,0:T(1,128)S(1)} %bitcast.13), channel_id=1, replica_groups=mesh['groups'=2,'rows'=4,'cols'=2,'sub'=2] {'rows','cols','sub'}, dimensions={0} | all-to-all | bytes 278528 | tf_op jit(solution)/shard_map/all_to_all | solution.py:263
  48.0 1.4 %shard_map.89 = (f32[272,128]{1,0:T(8,128)S(1)}, f32[16,128]{1,0:T(8,128)S(1)}, f32[16,128]{1,0:T(8,128)S(1)}, f32[16,128]{1,0:T(8,128)S(1)}, f32[16,128]{1,0:T(...) custom-call(f32[272,128]{1,0:T(8,128)S(1)} %bitcast.8, ...), custom_call_target="tpu_custom_call" | custom-call | tf_op jit(solution)/shard_map/pallas_call | solution.py:238
  49.4 10.6 %all_to_all.23 = f32[16,17,1,128]{3,2,1,0:T(1,128)S(1)} all-to-all(f32[16,17,1,128]{3,2,1,0:T(1,128)S(1)} %bitcast.12), channel_id=1, replica_groups=mesh['groups'=2,'rows'=4,'cols'=2,'sub'=2] {'rows','cols','sub'}, dimensions={0} | all-to-all | bytes 278528 | tf_op jit(solution)/shard_map/all_to_all | solution.py:263
  60.1 0.3 shard_map.90
  60.3 0.0 collective-permute-start
  60.4 1.2 %collective-permute-done = f32[1,128]{1,0:T(1,128)S(1)} collective-permute-done((f32[1,128]{1,0:T(1,128)S(1)}, f32[1,128]{1,0:T(1,128)S(1)}, u32[]{:S(2)}, u32[]{:S(2)}) %collective-permute-start) | collective-permute-done | bytes 544 | tf_op jit(solution)/shard_map/ppermute | solution.py:232
  61.5 0.7 %collective-permute-start.3 = (f32[1,128]{1,0:T(1,128)S(1)}, f32[1,128]{1,0:T(1,128)S(1)}, u32[]{:S(2)}, u32[]{:S(2)}) collective-permute-start(f32[1,128]{1,0:T(1,128)S(1)} %add.12), channel_id=1, source_target_pairs={{0,12},{4,8},{8,4},{12,0},{1,13},{5,9},{9,5},{13,1},{2,14},{6,10},... | collective-permute-start | bytes 1544 | tf_op jit(solution)/shard_map/ppermute | solution.py:232
  62.2 0.4 collective-permute-start.2
  62.6 3.3 %collective-permute-start.1 = (f32[1,128]{1,0:T(1,128)S(1)}, f32[1,128]{1,0:T(1,128)S(1)}, u32[]{:S(2)}, u32[]{:S(2)}) collective-permute-start(f32[1,128]{1,0:T(1,128)S(1)} %add.12), channel_id=1, source_target_pairs={{0,4},{4,0},{8,12},{12,8},{1,5},{5,1},{9,13},{13,9},{2,6},{6,2},{1... | collective-permute-start | bytes 1544 | tf_op jit(solution)/shard_map/ppermute | solution.py:232
  65.9 1.0 %collective-permute-done.3 = f32[1,128]{1,0:T(1,128)S(1)} collective-permute-done((f32[1,128]{1,0:T(1,128)S(1)}, f32[1,128]{1,0:T(1,128)S(1)}, u32[]{:S(2)}, u32[]{:S(2)}) %collective-permute-start.3) | collective-permute-done | bytes 544 | tf_op jit(solution)/shard_map/ppermute | solution.py:232
  66.9 0.6 collective-permute-done.1
  67.5 0.8 %shard_map.91 = (f32[16,128]{1,0:T(8,128)}, f32[16,128]{1,0:T(8,128)}) custom-call(f32[1,128]{1,0:T(1,128)S(1)} %add_add_fusion.dots_ref, f32[16,128]{1,0:T(8,128)S(1)} %get-tuple-element.49.twice_ref, f32[16,128]{1,0:T(8,128)S(1)} %get-tuple-element.50.half_ref, f32[16,128]{1,0:T(8,128)S(1)} %get-tuple-element.51.sum_ref, ...), custom_call_target="tpu_custom_call" | custom-call | tf_op jit(solution)/shard_map/pallas_call | solution.py:238
  (12 shorter events, 0.0 us)
Async XLA Ops:
  2.1 1.9 %copy-start = (f32[16,3,128,128]{3,2,1,0:T(8,128)S(1)}, f32[16,3,128,128]{3,2,1,0:T(8,128)}, u32[]{:S(2)}) copy-start(f32[16,3,128,128]{3,2,1,0:T(8,128)} %coupling_ref.7) | copy-start | bytes 9437188
  4.0 1.2 %copy-start.2 = (f32[16,128,128]{2,1,0:T(8,128)S(1)}, f32[16,128,128]{2,1,0:T(8,128)}, u32[]{:S(2)}) copy-start(f32[16,128,128]{2,1,0:T(8,128)} %diagonal_ref.7) | copy-start | bytes 3145732
  5.3 1.2 %copy-start.4 = (f32[16,128,128]{2,1,0:T(8,128)S(1)}, f32[16,128,128]{2,1,0:T(8,128)}, u32[]{:S(2)}) copy-start(f32[16,128,128]{2,1,0:T(8,128)} %jacobi_ref.1) | copy-start | bytes 3145732
  6.5 0.7 %copy-start.5 = (f32[16,128]{1,0:T(8,128)S(1)}, f32[16,128]{1,0:T(8,128)}, u32[]{:S(2)}) copy-start(f32[16,128]{1,0:T(8,128)} %b_ref.7) | copy-start | bytes 24580
  7.2 0.7 copy-start.6
  7.9 16.5 %copy-start.1 = (f32[16,3,128,128]{3,2,1,0:T(8,128)S(1)}, f32[16,3,128,128]{3,2,1,0:T(8,128)}, u32[]{:S(2)}) copy-start(f32[16,3,128,128]{3,2,1,0:T(8,128)} %coupling_ref.7) | copy-start | bytes 9437188
  7.9 16.5 %copy-start.3 = (f32[16,128,128]{2,1,0:T(8,128)S(1)}, f32[16,128,128]{2,1,0:T(8,128)}, u32[]{:S(2)}) copy-start(f32[16,128,128]{2,1,0:T(8,128)} %diagonal_ref.7) | copy-start | bytes 3145732
  60.3 1.2 %collective-permute-start = (f32[1,128]{1,0:T(1,128)S(1)}, f32[1,128]{1,0:T(1,128)S(1)}, u32[]{:S(2)}, u32[]{:S(2)}) collective-permute-start(f32[1,128]{1,0:T(1,128)S(1)} %get-tuple-element.48), channel_id=1, source_target_pairs={{0,1},{1,0},{2,3},{3,2},{4,5},{5,4},{6,7},{7,6},{8,9},{9,8},{10,11... | collective-permute-start | bytes 1544 | tf_op jit(solution)/shard_map/ppermute | solution.py:232
  61.5 5.4 %collective-permute-start.3 = (f32[1,128]{1,0:T(1,128)S(1)}, f32[1,128]{1,0:T(1,128)S(1)}, u32[]{:S(2)}, u32[]{:S(2)}) collective-permute-start(f32[1,128]{1,0:T(1,128)S(1)} %add.12), channel_id=1, source_target_pairs={{0,12},{4,8},{8,4},{12,0},{1,13},{5,9},{9,5},{13,1},{2,14},{6,10},... | collective-permute-start | bytes 1544 | tf_op jit(solution)/shard_map/ppermute | solution.py:232
  62.2 4.7 %collective-permute-start.2 = (f32[1,128]{1,0:T(1,128)S(1)}, f32[1,128]{1,0:T(1,128)S(1)}, u32[]{:S(2)}, u32[]{:S(2)}) collective-permute-start(f32[1,128]{1,0:T(1,128)S(1)} %add.12), channel_id=1, source_target_pairs={{0,8},{4,12},{8,0},{12,4},{1,9},{5,13},{9,1},{13,5},{2,10},{6,14},... | collective-permute-start | bytes 1544 | tf_op jit(solution)/shard_map/ppermute | solution.py:232
  62.6 4.8 %collective-permute-start.1 = (f32[1,128]{1,0:T(1,128)S(1)}, f32[1,128]{1,0:T(1,128)S(1)}, u32[]{:S(2)}, u32[]{:S(2)}) collective-permute-start(f32[1,128]{1,0:T(1,128)S(1)} %add.12), channel_id=1, source_target_pairs={{0,4},{4,0},{8,12},{12,8},{1,5},{5,1},{9,13},{13,9},{2,6},{6,2},{1... | collective-permute-start | bytes 1544 | tf_op jit(solution)/shard_map/ppermute | solution.py:232

commit v2 on v1

--- a/solution.py
+++ b/solution.py
@@ -30,19 +30,40 @@
     return jnp.concatenate([hi, mid, low], axis=0)
 
 
-def products(z, coupling_ref, diagonal_ref, partial_ref, own_ref):
-    rows, slots = coupling_ref.shape[0], coupling_ref.shape[1]
-    z_t = z.T
-    for r in range(rows):
-        column = jnp.broadcast_to(z_t[:, r : r + 1], coupling_ref.shape[2:])
+def sum_lines(parts):
+    line = lax.broadcasted_iota(jnp.int32, parts[0].shape, 0)
+    step = 1
+    while len(parts) > 1:
+        low = (line // step) % 2 == 0
+        parts = [
+            jnp.where(low, one, two) + pltpu.roll(jnp.where(low, two, one), step, 0)
+            for one, two in zip(parts[::2], parts[1::2])
+        ]
+        step *= 2
+    return parts[0]
+
+
+def products(z, coupling_ref, diagonal_ref, partial_ref, own_ref, column_ref, before=None):
+    rows, slots, width = coupling_ref.shape[:3]
+    for g in range(rows // 8):
+        if before is not None:
+            before(g)
+        first = g * 8
+        sums = [[] for _ in range(slots + 1)]
+        for r in range(first, first + 8):
+            column = jnp.broadcast_to(z[r : r + 1], (width, width)).T
+            for k in range(slots):
+                sums[k].append(jnp.sum((column * coupling_ref[r, k]).reshape(width // 8, 8, width), axis=0))
+            sums[slots].append(jnp.sum((column * diagonal_ref[r]).reshape(width // 8, 8, width), axis=0))
         for k in range(slots):
-            partial_ref[pl.ds(k * rows + r, 1), :] = jnp.sum(column * coupling_ref[r, k], axis=0, keepdims=True)
-        own_ref[pl.ds(r, 1), :] = jnp.sum(column * diagonal_ref[r], axis=0, keepdims=True)
-
-
-def emit(z, tail, spread_ref, coupling_ref, diagonal_ref, partial_ref, own_ref, send_ref):
+            partial_ref[pl.ds(k * rows + first, 8), :] = sum_lines(sums[k])
+        own_ref[pl.ds(first, 8), :] = sum_lines(sums[slots])
+
+
+def emit(z, tail, spread_ref, coupling_ref, diagonal_ref, scratch, own_ref, send_ref, before=None):
     rows = z.shape[0]
-    products(z, coupling_ref, diagonal_ref, partial_ref, own_ref)
+    partial_ref, column_ref = scratch
+    products(z, coupling_ref, diagonal_ref, partial_ref, own_ref, column_ref, before)
     send_ref[...] = jnp.dot(spread_ref[...], split3(partial_ref[...]), preferred_element_type=jnp.float32)
     for d in range(send_ref.shape[0] // (rows + 1)):
         send_ref[pl.ds(d * (rows + 1) + rows, 1), :] = tail
@@ -80,47 +101,75 @@
 
 
 def first_kernel(
-    b_ref, jacobi_ref, part_ref, tile_ref, near_ref, coupling_ref, diagonal_ref,
-    send_ref, own_ref, band_ref, spread_ref, partial_ref, *, sizes,
+    b_hbm, jacobi_hbm, part_hbm, tile_hbm, near_hbm, coupling_hbm, diagonal_hbm,
+    send_ref, own_ref, band_ref, spread_ref, b_ref, coupling_ref, diagonal_ref,
+    partial_ref, column_ref, jacobi_ref, part_ref, tile_ref, near_ref, small_sem, jacobi_sem, coupling_sem, diagonal_sem,
+    *, sizes,
 ):
     n_rows, n_cols, n_sub = sizes
     rows, slots = coupling_ref.shape[0], coupling_ref.shape[1]
     width = b_ref.shape[1]
-    folded = jnp.sum(jacobi_ref[...].reshape(rows, width // 8, 8, width), axis=1)
-    m = lax.broadcasted_iota(jnp.int32, (1, 8, width), 1)
-    j = lax.broadcasted_iota(jnp.int32, (1, 8, width), 2)
-    last = width // BLOCK * BLOCK
-    for d in range(-BAND, BAND + 1):
-        i = j + d
-        inside = (i // BLOCK == j // BLOCK) & (j < last) if d else j >= 0
-        picked = inside & (i >= 0) & (lax.rem(i + 8, 8) == m)
-        band_ref[d + BAND] = jnp.sum(jnp.where(picked, folded, 0.0), axis=1)
+    groups = rows // 8
+
+    def some(ref, g):
+        return ref.at[pl.ds(g * 8, 8)]
+
+    def copy_of(g, source, target, sem):
+        return pltpu.make_async_copy(some(source, g), some(target, g), sem.at[g])
+
+    small = [
+        pltpu.make_async_copy(source, target, small_sem.at[n])
+        for n, (source, target) in enumerate(
+            ((b_hbm, b_ref), (part_hbm, part_ref), (tile_hbm, tile_ref), (near_hbm, near_ref))
+        )
+    ]
+    for copy in small:
+        copy.start()
+    for g in range(groups):
+        copy_of(g, jacobi_hbm, jacobi_ref, jacobi_sem).start()
+    for g in range(groups):
+        copy_of(g, coupling_hbm, coupling_ref, coupling_sem).start()
+        copy_of(g, diagonal_hbm, diagonal_ref, diagonal_sem).start()
+    for copy in small:
+        copy.wait()
     own = lax.axis_index("rows")
-    part, tile = part_ref[...], tile_ref[...]
-    near = near_ref[...]
+    part, tile, near = part_ref[...], tile_ref[...], near_ref[...]
     near_row = lax.broadcasted_iota(jnp.int32, near.shape, 0)
     mine = jnp.sum(jnp.where(near_row == own, near, 0), axis=0, keepdims=True)
     target = jnp.where(part == 0, own, 0)
     for n in range(near.shape[1]):
         target = target + jnp.where(part == n + 1, mine[:, n : n + 1], 0)
     landing = target * (rows * n_sub) + tile
-    lanes = -(-spread_ref.shape[0] // LANES) * LANES
-    at = lax.broadcasted_iota(jnp.int32, (rows, lanes), 1)
+    landing = jnp.concatenate([landing[k : k + 1] for k in range(slots)] * 3, axis=1)
+    at = lax.broadcasted_iota(jnp.int32, (spread_ref.shape[0], 1), 0)
     device, line = at // (rows + 1), at % (rows + 1)
     row, sub = device // (n_cols * n_sub), device % n_sub
-    wanted = jnp.where((line < rows) & (row < n_rows), row * (rows * n_sub) + sub * rows + line, -1)
-    hits = jnp.concatenate(
-        [(landing[:, k : k + 1] == wanted).astype(jnp.float32) for k in range(slots)], axis=0
-    )
-    one_hot = hits.T[: spread_ref.shape[0]].astype(jnp.bfloat16)
-    spread_ref[...] = jnp.concatenate([one_hot] * 3, axis=1)
+    wanted = jnp.where(line < rows, row * (rows * n_sub) + sub * rows + line, -1)
+    spread_ref[...] = jnp.where(landing == wanted, 1.0, 0.0).astype(jnp.bfloat16)
+    m = lax.broadcasted_iota(jnp.int32, (1, 8, width), 1)
+    j = lax.broadcasted_iota(jnp.int32, (1, 8, width), 2)
+    last = width // BLOCK * BLOCK
+    for g in range(groups):
+        copy_of(g, jacobi_hbm, jacobi_ref, jacobi_sem).wait()
+        folded = jnp.sum(some(jacobi_ref, g)[...].reshape(8, width // 8, 8, width), axis=1)
+        for d in range(-BAND, BAND + 1):
+            i = j + d
+            inside = (i // BLOCK == j // BLOCK) & (j < last) if d else j >= 0
+            picked = inside & (i >= 0) & (lax.rem(i + 8, 8) == m)
+            band_ref[d + BAND, pl.ds(g * 8, 8)] = jnp.sum(jnp.where(picked, folded, 0.0), axis=1)
     z = apply_m(band_ref, b_ref[...])
-    emit(z, jnp.zeros((1, width), jnp.float32), spread_ref, coupling_ref, diagonal_ref, partial_ref, own_ref, send_ref)
+
+    def before(g):
+        copy_of(g, coupling_hbm, coupling_ref, coupling_sem).wait()
+        copy_of(g, diagonal_hbm, diagonal_ref, diagonal_sem).wait()
+
+    tail = jnp.zeros((1, width), jnp.float32)
+    emit(z, tail, spread_ref, coupling_ref, diagonal_ref, (partial_ref, column_ref), own_ref, send_ref, before)
 
 
 def second_kernel(
     recv_ref, own_in, b_ref, band_ref, spread_ref, coupling_ref, diagonal_ref,
-    send_ref, own_ref, q_ref, partial_ref,
+    send_ref, own_ref, q_ref, partial_ref, column_ref,
 ):
     b = b_ref[...]
     rows, width = b.shape
@@ -131,7 +180,7 @@
     up, down = level(q, b)
     tail = pack([total(b * b), total(b * q), down], width)
     z = apply_m(band_ref, q * up)
-    emit(z, tail, spread_ref, coupling_ref, diagonal_ref, partial_ref, own_ref, send_ref)
+    emit(z, tail, spread_ref, coupling_ref, diagonal_ref, (partial_ref, column_ref), own_ref, send_ref)
 
 
 def scalars_of(recv_ref, rows, count, repeats):
@@ -150,7 +199,7 @@
 
 def third_kernel(
     recv_ref, own_in, b_ref, q_ref, band_ref, spread_ref, coupling_ref, diagonal_ref,
-    send_ref, own_ref, twice_ref, half_ref, u_ref, keep_ref, partial_ref, *, n_cols,
+    send_ref, own_ref, twice_ref, half_ref, u_ref, keep_ref, partial_ref, column_ref, *, n_cols,
 ):
     b, q = b_ref[...], q_ref[...]
     rows, width = b.shape
@@ -165,12 +214,12 @@
     twice_ref[...], half_ref[...], u_ref[...] = twice, half, u
     keep_ref[...] = pack([rho, alpha], width)
     z = apply_m(band_ref, twice * up)
-    emit(z, tail, spread_ref, coupling_ref, diagonal_ref, partial_ref, own_ref, send_ref)
+    emit(z, tail, spread_ref, coupling_ref, diagonal_ref, (partial_ref, column_ref), own_ref, send_ref)
 
 
 def fourth_kernel(
     recv_ref, own_in, b_ref, q_ref, twice_ref, half_ref, u_ref, keep_ref, band_ref, spread_ref, coupling_ref,
-    diagonal_ref, send_ref, own_ref, a_ref, residual_ref, image_ref, search_ref, done_ref, kept_ref, partial_ref,
+    diagonal_ref, send_ref, own_ref, a_ref, residual_ref, image_ref, search_ref, done_ref, kept_ref, partial_ref, column_ref,
     *, n_cols,
 ):
     b, q, twice, half = b_ref[...], q_ref[...], twice_ref[...], half_ref[...]
@@ -192,7 +241,7 @@
     done_ref[...] = alpha * b + omega * half
     kept_ref[...] = pack([rho_next], width)
     z = apply_m(band_ref, image * up)
-    emit(z, tail, spread_ref, coupling_ref, diagonal_ref, partial_ref, own_ref, send_ref)
+    emit(z, tail, spread_ref, coupling_ref, diagonal_ref, (partial_ref, column_ref), own_ref, send_ref)
 
 
 def fifth_kernel(
@@ -233,15 +282,17 @@
     return out
 
 
-def call(kernel, outs, args, scratch=()):
+def call(kernel, outs, args, scratch=(), space=pltpu.VMEM):
     spec = pl.BlockSpec(memory_space=pltpu.VMEM)
+    if space == pltpu.HBM:
+        args = [pltpu.with_memory_space_constraint(x, space) for x in args]
     return pl.pallas_call(
         kernel,
-        out_shape=[jax.ShapeDtypeStruct(shape, kind) for shape, kind in outs],
-        in_specs=[spec] * len(args),
+        out_shape=[pltpu.VMEM(shape, kind) if space == pltpu.HBM else jax.ShapeDtypeStruct(shape, kind) for shape, kind in outs],
+        in_specs=[pl.BlockSpec(memory_space=space)] * len(args),
         out_specs=[spec] * len(outs),
         scratch_shapes=list(scratch),
-        compiler_params=pltpu.CompilerParams(vmem_limit_bytes=48 << 20),
+        compiler_params=pltpu.CompilerParams(vmem_limit_bytes=24 << 20),
     )(*args)
 
 
@@ -256,15 +307,23 @@
     message = ((devices * (rows + 1), width), f32)
     band_shape = ((2 * BAND + 1, rows, width), f32)
     spread_shape = ((devices * (rows + 1), 3 * slots * rows), jnp.bfloat16)
-    scratch = [pltpu.VMEM((slots * rows, width), f32)]
+    scratch = [pltpu.VMEM((slots * rows, width), f32), pltpu.VMEM((rows, width, width), f32)]
 
     def exchange(send):
         send = send.reshape(devices, rows + 1, 1, width)
         return lax.all_to_all(send, PART, 0, 0, tiled=True).reshape(devices * (rows + 1), width)
 
-    send, own, band, spread = call(
-        functools.partial(first_kernel, sizes=sizes), [message, vec, band_shape, spread_shape],
-        (b, jacobi, column_part, column_tile, neighbours, coupling, diagonal), scratch,
+    part, tile = column_part.T, column_tile.T
+    sems = [pltpu.SemaphoreType.DMA((n,)) for n in (4, rows // 8, rows // 8, rows // 8)]
+    send, own, band, spread, b, coupling, diagonal = call(
+        functools.partial(first_kernel, sizes=sizes),
+        [message, vec, band_shape, spread_shape, vec, (coupling.shape, f32), (diagonal.shape, f32)],
+        (b, jacobi, part, tile, neighbours, coupling, diagonal),
+        scratch
+        + [pltpu.VMEM(jacobi.shape, f32)]
+        + [pltpu.VMEM(x.shape, x.dtype) for x in (part, tile, neighbours)]
+        + sems,
+        pltpu.HBM,
     )
     fixed = (band, spread, coupling, diagonal)
     send, own, q = call(second_kernel, [message, vec, vec], (exchange(send), own, b) + fixed, scratch)

time: 68.8 us -> 62 us (0.901)
  local copies, waits for them, and re-layouts: 7.24 us -> 0 us
  Pallas kernels: 6.03 us -> 6.79 us
    unnamed x16 -> x0, local copies, waits for them, and re-layouts: 7.24 us -> none
    pallas_call x6, Pallas kernels: 6.03 us -> 6.79 us  [call(): pl.pallas_call(kernel, out_shape=[pltpu.VMEM(shape, kind) if space == plt...]
where the time goes in v2:
time: 62 us; the launch traced here: 61.7 us
  blocking collectives  47.1 us (76%)
  Pallas kernels  6.79 us (11%)
  starting transfers between devices  4.39 us (7%)
  waiting for transfers between devices  2.7 us (4%)
  between operations  0.68 us (1%)
    all_to_all x4, blocking collectives, exchange(): lax.all_to_all(send, PART, 0, 0, tiled=True)  47.1 us
    pallas_call x6, Pallas kernels, call(): pl.pallas_call(kernel, out_shape=[pltpu.VMEM(shape, kind) if space == plt...  6.79 us
    ppermute x4, starting transfers between devices, sum_over(): out = out + lax.ppermute(x, axis, partners(count, step))  4.39 us
    ppermute x4, waiting for transfers between devices, sum_over(): out = out + lax.ppermute(x, axis, partners(count, step))  2.7 us
  transfers between devices with their start and end apart: 4, of which 3 were waited for; matrix products, arithmetic and copies ran while one was open for 0% of the time, Pallas kernels for 0%

profile of v2, /device:TPU:0, one launch (start us, length us, event | category | flops | bytes accessed | tf_op | source)
XLA Modules:
  0.0 61.7 jit_solution(14192350036641274130)
XLA Ops:
  0.6 3.0 %shard_map.86 = (f32[272,128]{1,0:T(8,128)S(1)}, f32[16,128]{1,0:T(8,128)S(1)}, f32[9,16,128]{2,1,0:T(8,128)S(1)}, bf16[272,144]{1,0:T(8,128)(2,1)S(1)}, f32[16,...) custom-call(f32[16,128]{1,0:T(8,128)} %b_hbm.1, f32[16,128,128]{2,1,0:T(8,128)} %jacobi_hbm.1, ...), custom_call_target="tpu_custom_call" | custom-call | tf_op jit(solution)/shard_map/pallas_call | solution.py:289
  3.6 15.2 %all_to_all.20 = f32[16,17,1,128]{3,2,1,0:T(1,128)S(1)} all-to-all(f32[16,17,1,128]{3,2,1,0:T(1,128)S(1)} %bitcast.16), channel_id=1, replica_groups=mesh['groups'=2,'rows'=4,'cols'=2,'sub'=2] {'rows','cols','sub'}, dimensions={0} | all-to-all | bytes 278528 | tf_op jit(solution)/shard_map/all_to_all | solution.py:314
  18.9 0.7 %shard_map.87 = (f32[272,128]{1,0:T(8,128)S(1)}, f32[16,128]{1,0:T(8,128)S(1)}, f32[16,128]{1,0:T(8,128)S(1)}) custom-call(f32[272,128]{1,0:T(8,128)S(1)} %bitcast.12, f32[16,128]{1,0:T(8,128)S(1)} %get-tuple-element.31.own_in, f32[16,128]{1,0:T(8,128)S(1)} %get-tuple-element.32.b_ref, f32[9,16,128]{2,1,0:T(8,128)S(1)} %get-tuple-element.33.band_ref, ...), custom_call_target="tpu_custom_call" | custom-call | tf_op jit(solution)/shard_map/pallas_call | solution.py:289
  19.6 10.6 %all_to_all.21 = f32[16,17,1,128]{3,2,1,0:T(1,128)S(1)} all-to-all(f32[16,17,1,128]{3,2,1,0:T(1,128)S(1)} %bitcast.17), channel_id=1, replica_groups=mesh['groups'=2,'rows'=4,'cols'=2,'sub'=2] {'rows','cols','sub'}, dimensions={0} | all-to-all | bytes 278528 | tf_op jit(solution)/shard_map/all_to_all | solution.py:314
  30.2 0.9 %shard_map.88 = (f32[272,128]{1,0:T(8,128)S(1)}, f32[16,128]{1,0:T(8,128)S(1)}, f32[16,128]{1,0:T(8,128)S(1)}, f32[16,128]{1,0:T(8,128)S(1)}, f32[16,128]{1,0:T(8,128)S(1)}, /*index=5*/f32[1,128]{1,0:T(1,128)S(1)}) custom-call(f32[272,128]{1,0:T(8,128)S(1)} %bitcast.11, f32[16,128]{1,0:T(8,128)S(1)} %get-tuple-element.38.own_in, ...), custom_call_target="tpu_custom_call" | custom-call | tf_op jit(solution)/shard_map/pallas_call | solution.py:289
  31.1 10.6 %all_to_all.22 = f32[16,17,1,128]{3,2,1,0:T(1,128)S(1)} all-to-all(f32[16,17,1,128]{3,2,1,0:T(1,128)S(1)} %bitcast.15), channel_id=1, replica_groups=mesh['groups'=2,'rows'=4,'cols'=2,'sub'=2] {'rows','cols','sub'}, dimensions={0} | all-to-all | bytes 278528 | tf_op jit(solution)/shard_map/all_to_all | solution.py:314
  41.7 1.1 %shard_map.89 = (f32[272,128]{1,0:T(8,128)S(1)}, f32[16,128]{1,0:T(8,128)S(1)}, f32[16,128]{1,0:T(8,128)S(1)}, f32[16,128]{1,0:T(8,128)S(1)}, f32[16,128]{1,0:T(...) custom-call(f32[272,128]{1,0:T(8,128)S(1)} %bitcast.10, ...), custom_call_target="tpu_custom_call" | custom-call | tf_op jit(solution)/shard_map/pallas_call | solution.py:289
  42.8 10.6 %all_to_all.23 = f32[16,17,1,128]{3,2,1,0:T(1,128)S(1)} all-to-all(f32[16,17,1,128]{3,2,1,0:T(1,128)S(1)} %bitcast.14), channel_id=1, replica_groups=mesh['groups'=2,'rows'=4,'cols'=2,'sub'=2] {'rows','cols','sub'}, dimensions={0} | all-to-all | bytes 278528 | tf_op jit(solution)/shard_map/all_to_all | solution.py:314
  53.4 0.3 shard_map.90
  53.7 0.0 collective-permute-start
  53.7 1.2 %collective-permute-done = f32[1,128]{1,0:T(1,128)S(1)} collective-permute-done((f32[1,128]{1,0:T(1,128)S(1)}, f32[1,128]{1,0:T(1,128)S(1)}, u32[]{:S(2)}, u32[]{:S(2)}) %collective-permute-start) | collective-permute-done | bytes 544 | tf_op jit(solution)/shard_map/ppermute | solution.py:281
  54.9 0.7 %collective-permute-start.3 = (f32[1,128]{1,0:T(1,128)S(1)}, f32[1,128]{1,0:T(1,128)S(1)}, u32[]{:S(2)}, u32[]{:S(2)}) collective-permute-start(f32[1,128]{1,0:T(1,128)S(1)} %add.12), channel_id=1, source_target_pairs={{0,12},{4,8},{8,4},{12,0},{1,13},{5,9},{9,5},{13,1},{2,14},{6,10},... | collective-permute-start | bytes 1544 | tf_op jit(solution)/shard_map/ppermute | solution.py:281
  55.6 0.4 collective-permute-start.2
  56.0 3.3 %collective-permute-start.1 = (f32[1,128]{1,0:T(1,128)S(1)}, f32[1,128]{1,0:T(1,128)S(1)}, u32[]{:S(2)}, u32[]{:S(2)}) collective-permute-start(f32[1,128]{1,0:T(1,128)S(1)} %add.12), channel_id=1, source_target_pairs={{0,4},{4,0},{8,12},{12,8},{1,5},{5,1},{9,13},{13,9},{2,6},{6,2},{1... | collective-permute-start | bytes 1544 | tf_op jit(solution)/shard_map/ppermute | solution.py:281
  59.3 1.0 %collective-permute-done.3 = f32[1,128]{1,0:T(1,128)S(1)} collective-permute-done((f32[1,128]{1,0:T(1,128)S(1)}, f32[1,128]{1,0:T(1,128)S(1)}, u32[]{:S(2)}, u32[]{:S(2)}) %collective-permute-start.3) | collective-permute-done | bytes 544 | tf_op jit(solution)/shard_map/ppermute | solution.py:281
  60.3 0.0 collective-permute-done.2
  60.3 0.6 collective-permute-done.1
  60.8 0.8 %shard_map.91 = (f32[16,128]{1,0:T(8,128)}, f32[16,128]{1,0:T(8,128)}) custom-call(f32[1,128]{1,0:T(1,128)S(1)} %add_add_fusion.dots_ref, f32[16,128]{1,0:T(8,128)S(1)} %get-tuple-element.55.twice_ref, f32[16,128]{1,0:T(8,128)S(1)} %get-tuple-element.56.half_ref, f32[16,128]{1,0:T(8,128)S(1)} %get-tuple-element.57.sum_ref, ...), custom_call_target="tpu_custom_call" | custom-call | tf_op jit(solution)/shard_map/pallas_call | solution.py:289
  (2 shorter events, 0.0 us)
Async XLA Ops:
  53.7 1.2 %collective-permute-start = (f32[1,128]{1,0:T(1,128)S(1)}, f32[1,128]{1,0:T(1,128)S(1)}, u32[]{:S(2)}, u32[]{:S(2)}) collective-permute-start(f32[1,128]{1,0:T(1,128)S(1)} %get-tuple-element.54), channel_id=1, source_target_pairs={{0,1},{1,0},{2,3},{3,2},{4,5},{5,4},{6,7},{7,6},{8,9},{9,8},{10,11... | collective-permute-start | bytes 1544 | tf_op jit(solution)/shard_map/ppermute | solution.py:281
  54.9 5.4 %collective-permute-start.3 = (f32[1,128]{1,0:T(1,128)S(1)}, f32[1,128]{1,0:T(1,128)S(1)}, u32[]{:S(2)}, u32[]{:S(2)}) collective-permute-start(f32[1,128]{1,0:T(1,128)S(1)} %add.12), channel_id=1, source_target_pairs={{0,12},{4,8},{8,4},{12,0},{1,13},{5,9},{9,5},{13,1},{2,14},{6,10},... | collective-permute-start | bytes 1544 | tf_op jit(solution)/shard_map/ppermute | solution.py:281
  55.6 4.7 %collective-permute-start.2 = (f32[1,128]{1,0:T(1,128)S(1)}, f32[1,128]{1,0:T(1,128)S(1)}, u32[]{:S(2)}, u32[]{:S(2)}) collective-permute-start(f32[1,128]{1,0:T(1,128)S(1)} %add.12), channel_id=1, source_target_pairs={{0,8},{4,12},{8,0},{12,4},{1,9},{5,13},{9,1},{13,5},{2,10},{6,14},... | collective-permute-start | bytes 1544 | tf_op jit(solution)/shard_map/ppermute | solution.py:281
  56.0 4.8 %collective-permute-start.1 = (f32[1,128]{1,0:T(1,128)S(1)}, f32[1,128]{1,0:T(1,128)S(1)}, u32[]{:S(2)}, u32[]{:S(2)}) collective-permute-start(f32[1,128]{1,0:T(1,128)S(1)} %add.12), channel_id=1, source_target_pairs={{0,4},{4,0},{8,12},{12,8},{1,5},{5,1},{9,13},{13,9},{2,6},{6,2},{1... | collective-permute-start | bytes 1544 | tf_op jit(solution)/shard_map/ppermute | solution.py:281

commit v3 on v2

--- a/solution.py
+++ b/solution.py
@@ -43,7 +43,7 @@
     return parts[0]
 
 
-def products(z, coupling_ref, diagonal_ref, partial_ref, own_ref, column_ref, before=None):
+def products(z, coupling_ref, diagonal_ref, partial_ref, own_ref, before=None):
     rows, slots, width = coupling_ref.shape[:3]
     for g in range(rows // 8):
         if before is not None:
@@ -60,10 +60,9 @@
         own_ref[pl.ds(first, 8), :] = sum_lines(sums[slots])
 
 
-def emit(z, tail, spread_ref, coupling_ref, diagonal_ref, scratch, own_ref, send_ref, before=None):
+def emit(z, tail, spread_ref, coupling_ref, diagonal_ref, partial_ref, own_ref, send_ref, before=None):
     rows = z.shape[0]
-    partial_ref, column_ref = scratch
-    products(z, coupling_ref, diagonal_ref, partial_ref, own_ref, column_ref, before)
+    products(z, coupling_ref, diagonal_ref, partial_ref, own_ref, before)
     send_ref[...] = jnp.dot(spread_ref[...], split3(partial_ref[...]), preferred_element_type=jnp.float32)
     for d in range(send_ref.shape[0] // (rows + 1)):
         send_ref[pl.ds(d * (rows + 1) + rows, 1), :] = tail
@@ -102,8 +101,8 @@
 
 def first_kernel(
     b_hbm, jacobi_hbm, part_hbm, tile_hbm, near_hbm, coupling_hbm, diagonal_hbm,
-    send_ref, own_ref, band_ref, spread_ref, b_ref, coupling_ref, diagonal_ref,
-    partial_ref, column_ref, jacobi_ref, part_ref, tile_ref, near_ref, small_sem, jacobi_sem, coupling_sem, diagonal_sem,
+    send_ref, own_ref, band_ref, spread_ref, halves_ref, b_ref, coupling_ref, diagonal_ref,
+    partial_ref, jacobi_ref, part_ref, tile_ref, near_ref, small_sem, jacobi_sem, coupling_sem, diagonal_sem,
     *, sizes,
 ):
     n_rows, n_cols, n_sub = sizes
@@ -146,6 +145,11 @@
     row, sub = device // (n_cols * n_sub), device % n_sub
     wanted = jnp.where(line < rows, row * (rows * n_sub) + sub * rows + line, -1)
     spread_ref[...] = jnp.where(landing == wanted, 1.0, 0.0).astype(jnp.bfloat16)
+    at = lax.broadcasted_iota(jnp.int32, (halves_ref.shape[0], 1), 0)
+    size = halves_ref.shape[0] // n_sub
+    sub, at = partner(lax.axis_index("sub"), at // size, n_sub), at % size
+    wanted = jnp.where(at < n_rows * rows, at // rows * (rows * n_sub) + sub * rows + at % rows, -1)
+    halves_ref[...] = jnp.where(landing == wanted, 1.0, 0.0).astype(jnp.bfloat16)
     m = lax.broadcasted_iota(jnp.int32, (1, 8, width), 1)
     j = lax.broadcasted_iota(jnp.int32, (1, 8, width), 2)
     last = width // BLOCK * BLOCK
@@ -164,12 +168,12 @@
         copy_of(g, diagonal_hbm, diagonal_ref, diagonal_sem).wait()
 
     tail = jnp.zeros((1, width), jnp.float32)
-    emit(z, tail, spread_ref, coupling_ref, diagonal_ref, (partial_ref, column_ref), own_ref, send_ref, before)
+    emit(z, tail, spread_ref, coupling_ref, diagonal_ref, partial_ref, own_ref, send_ref, before)
 
 
 def second_kernel(
     recv_ref, own_in, b_ref, band_ref, spread_ref, coupling_ref, diagonal_ref,
-    send_ref, own_ref, q_ref, partial_ref, column_ref,
+    send_ref, own_ref, q_ref, partial_ref,
 ):
     b = b_ref[...]
     rows, width = b.shape
@@ -180,7 +184,7 @@
     up, down = level(q, b)
     tail = pack([total(b * b), total(b * q), down], width)
     z = apply_m(band_ref, q * up)
-    emit(z, tail, spread_ref, coupling_ref, diagonal_ref, (partial_ref, column_ref), own_ref, send_ref)
+    emit(z, tail, spread_ref, coupling_ref, diagonal_ref, partial_ref, own_ref, send_ref)
 
 
 def scalars_of(recv_ref, rows, count, repeats):
@@ -199,7 +203,7 @@
 
 def third_kernel(
     recv_ref, own_in, b_ref, q_ref, band_ref, spread_ref, coupling_ref, diagonal_ref,
-    send_ref, own_ref, twice_ref, half_ref, u_ref, keep_ref, partial_ref, column_ref, *, n_cols,
+    send_ref, own_ref, twice_ref, half_ref, u_ref, keep_ref, partial_ref, *, n_cols,
 ):
     b, q = b_ref[...], q_ref[...]
     rows, width = b.shape
@@ -209,55 +213,77 @@
     u = weighted(recv_ref, own_in, down, tails, 2, alpha)
     twice = q - u
     half = b - alpha * q
-    up, down = level(twice, half)
-    tail = pack([total(twice * half), total(twice * twice), total(b * half), total(b * twice), down], width)
+    tail = pack([total(twice * half), total(twice * twice), total(b * half), total(b * twice)], width)
     twice_ref[...], half_ref[...], u_ref[...] = twice, half, u
     keep_ref[...] = pack([rho, alpha], width)
-    z = apply_m(band_ref, twice * up)
-    emit(z, tail, spread_ref, coupling_ref, diagonal_ref, (partial_ref, column_ref), own_ref, send_ref)
+    z = apply_m(band_ref, alpha * twice)
+    emit(z, tail, spread_ref, coupling_ref, diagonal_ref, partial_ref, own_ref, send_ref)
 
 
 def fourth_kernel(
-    recv_ref, own_in, b_ref, q_ref, twice_ref, half_ref, u_ref, keep_ref, band_ref, spread_ref, coupling_ref,
-    diagonal_ref, send_ref, own_ref, a_ref, residual_ref, image_ref, search_ref, done_ref, kept_ref, partial_ref, column_ref,
-    *, n_cols,
+    recv_ref, own_in, b_ref, q_ref, twice_ref, half_ref, u_ref, keep_ref, band_ref, halves_ref, coupling_ref,
+    diagonal_ref, *refs, n_rows, n_cols, n_sub,
 ):
+    parts, (three_ref, search_ref, done_ref, kept_ref, partial_ref, own_ref) = refs[:n_sub], refs[n_sub:]
     b, q, twice, half = b_ref[...], q_ref[...], twice_ref[...], half_ref[...]
     rows, width = b.shape
     rho, alpha = keep_ref[:, 0:1], keep_ref[:, 1:2]
-    tails, (cross, square, b_half, b_twice) = scalars_of(recv_ref, rows, 4, n_cols)
+    _, (cross, square, b_half, b_twice) = scalars_of(recv_ref, rows, 4, n_cols)
     omega = cross / square
     rho_next = b_half - omega * b_twice
     ratio = rho_next / rho
     beta = ratio * (alpha / omega)
-    _, down = level(twice, half)
-    a = twice - weighted(recv_ref, own_in, down, tails, 4, omega)
+    a = own_in[...]
+    for d in range(recv_ref.shape[0] // (rows + 1)):
+        a = a + chunk(recv_ref, d, rows)
+    a = twice - (omega / alpha) * a
     residual = half - omega * twice
     image = a + beta * q - ratio * u_ref[...]
-    up, down = level(image, residual)
-    tail = pack([total(b * image), down], width)
-    a_ref[...], residual_ref[...], image_ref[...] = a, residual, image
+    three_ref[...] = jnp.concatenate([a, residual, image], axis=0)
     search_ref[...] = residual + beta * (b - omega * q)
     done_ref[...] = alpha * b + omega * half
-    kept_ref[...] = pack([rho_next], width)
-    z = apply_m(band_ref, image * up)
-    emit(z, tail, spread_ref, coupling_ref, diagonal_ref, (partial_ref, column_ref), own_ref, send_ref)
-
-
-def fifth_kernel(
-    recv_ref, own_in, a_ref, residual_ref, image_ref, search_ref, done_ref, kept_ref,
-    twice_ref, half_ref, sum_ref, dots_ref, *, n_cols,
-):
-    residual, image = residual_ref[...], image_ref[...]
-    rows, width = residual.shape
-    tails, (cross,) = scalars_of(recv_ref, rows, 1, n_cols)
-    alpha = kept_ref[:, 0:1] / cross
-    _, down = level(image, residual)
-    twice = a_ref[...] - weighted(recv_ref, own_in, down, tails, 1, alpha)
-    half = residual - alpha * image
-    twice_ref[...], half_ref[...] = twice, half
+    kept_ref[...] = pack([rho_next, alpha], width)
+    first = lax.axis_index("cols") == 0
+    tail = pack([jnp.where(first, total(b * image), 0.0)], width)
+    z = apply_m(band_ref, alpha * image)
+    products(z, coupling_ref, diagonal_ref, partial_ref, own_ref)
+    out = jnp.dot(halves_ref[...], split3(partial_ref[...]), preferred_element_type=jnp.float32)
+    size = parts[0].shape[0]
+    for t, part_ref in enumerate(parts):
+        part_ref[...] = out[t * size : (t + 1) * size]
+        part_ref[pl.ds(n_rows * rows, 1), :] = tail
+    here = pl.ds(pl.multiple_of(lax.axis_index("rows") * rows, rows), rows)
+    parts[0][here, :] = parts[0][here, :] + jnp.where(first, own_ref[...], 0.0)
+
+
+def fifth_kernel(mine_ref, *refs, n_rows):
+    others, (kept_ref, search_ref, done_ref, twice_ref, half_ref, sum_ref, dots_ref, full_ref) = (
+        refs[: n_rows - 1],
+        refs[n_rows - 1 :],
+    )
+    rows, width = search_ref.shape
+    size = full_ref.shape[0]
+    full = mine_ref[pl.ds(0, size), :]
+    for other in others:
+        full = full + other[pl.ds(0, size), :]
+    full_ref[...] = full
+    tail = full[n_rows * rows : n_rows * rows + 1]
+    alpha = kept_ref[:, 0:1] / tail[:, 0:1]
+    factor = alpha / kept_ref[:, 1:2]
+    own = lax.axis_index("rows")
+    cross = square = None
+    for step, source in enumerate((mine_ref,) + tuple(others)):
+        at = own if step == 0 else sender(own, step, n_rows)
+        a, residual, image = (source[pl.ds(size + n * rows, rows), :] for n in range(3))
+        twice = a - factor * full_ref[pl.ds(pl.multiple_of(at * rows, rows), rows), :]
+        half = residual - alpha * image
+        if step == 0:
+            twice_ref[...], half_ref[...] = twice, half
+            cross, square = twice * half, twice * twice
+        else:
+            cross, square = cross + twice * half, square + twice * twice
     sum_ref[...] = done_ref[...] + alpha * search_ref[...]
-    dots_ref[...] = pack([total(twice * half), total(twice * twice)], width)
+    dots_ref[...] = pack([total(cross), total(square)], width)
 
 
 def last_kernel(dots_ref, twice_ref, half_ref, sum_ref, band_ref, solution_ref, residual_ref):
@@ -268,17 +294,23 @@
     solution_ref[...] = apply_m(band_ref, sum_ref[...] + omega * half)
 
 
-def partners(count, step):
-    if count & (count - 1) == 0:
-        return [(i, i ^ step) for i in range(count)]
-    return [(i, (i + step) % count) for i in range(count)]
+def partner(at, step, count):
+    return at ^ step if count & (count - 1) == 0 else (at + step) % count
+
+
+def sender(at, step, count):
+    return at ^ step if count & (count - 1) == 0 else (at + count - step) % count
+
+
+def shifted(x, axis, step):
+    count = lax.axis_size(axis)
+    return lax.ppermute(x, axis, [(i, partner(i, step, count)) for i in range(count)])
 
 
 def sum_over(x, axis):
-    count = lax.axis_size(axis)
     out = x
-    for step in range(1, count):
-        out = out + lax.ppermute(x, axis, partners(count, step))
+    for step in range(1, lax.axis_size(axis)):
+        out = out + shifted(x, axis, step)
     return out
 
 
@@ -301,13 +333,16 @@
     rows, width = b.shape
     slots = coupling.shape[1]
     sizes = tuple(lax.axis_size(axis) for axis in PART)
-    n_cols = sizes[1]
-    devices = sizes[0] * sizes[1] * sizes[2]
+    n_rows, n_cols, n_sub = sizes
+    devices = n_rows * n_cols * n_sub
     vec, line = ((rows, width), f32), ((1, width), f32)
     message = ((devices * (rows + 1), width), f32)
+    part_size = n_rows * rows + 8
+    part_shape = ((part_size, width), f32)
     band_shape = ((2 * BAND + 1, rows, width), f32)
     spread_shape = ((devices * (rows + 1), 3 * slots * rows), jnp.bfloat16)
-    scratch = [pltpu.VMEM((slots * rows, width), f32), pltpu.VMEM((rows, width, width), f32)]
+    halves_shape = ((n_sub * part_size, 3 * slots * rows), jnp.bfloat16)
+    scratch = [pltpu.VMEM((slots * rows, width), f32)]
 
     def exchange(send):
         send = send.reshape(devices, rows + 1, 1, width)
@@ -315,9 +350,9 @@
 
     part, tile = column_part.T, column_tile.T
     sems = [pltpu.SemaphoreType.DMA((n,)) for n in (4, rows // 8, rows // 8, rows // 8)]
-    send, own, band, spread, b, coupling, diagonal = call(
+    send, own, band, spread, halves, b, coupling, diagonal = call(
         functools.partial(first_kernel, sizes=sizes),
-        [message, vec, band_shape, spread_shape, vec, (coupling.shape, f32), (diagonal.shape, f32)],
+        [message, vec, band_shape, spread_shape, halves_shape, vec, (coupling.shape, f32), (diagonal.shape, f32)],
         (b, jacobi, part, tile, neighbours, coupling, diagonal),
         scratch
         + [pltpu.VMEM(jacobi.shape, f32)]
@@ -325,22 +360,32 @@
         + sems,
         pltpu.HBM,
     )
-    fixed = (band, spread, coupling, diagonal)
-    send, own, q = call(second_kernel, [message, vec, vec], (exchange(send), own, b) + fixed, scratch)
+    tiles = (coupling, diagonal)
+    send, own, q = call(
+        second_kernel, [message, vec, vec], (exchange(send), own, b, band, spread) + tiles, scratch
+    )
     send, own, twice, half, u, keep = call(
         functools.partial(third_kernel, n_cols=n_cols), [message] + [vec] * 4 + [line],
-        (exchange(send), own, b, q) + fixed, scratch,
-    )
-    send, own, a, residual, image, search, done, kept = call(
-        functools.partial(fourth_kernel, n_cols=n_cols), [message] + [vec] * 6 + [line],
-        (exchange(send), own, b, q, twice, half, u, keep) + fixed, scratch,
-    )
-    twice, half, summed, dots = call(
-        functools.partial(fifth_kernel, n_cols=n_cols), [vec] * 3 + [line],
-        (exchange(send), own, a, residual, image, search, done, kept),
-    )
-    dots = sum_over(sum_over(dots, "sub"), "rows")
-    return tuple(call(last_kernel, [vec, vec], (dots, twice, half, summed, band)))
+        (exchange(send), own, b, q, band, spread) + tiles, scratch,
+    )
+    *parts, three, search, done, kept = call(
+        functools.partial(fourth_kernel, n_rows=n_rows, n_cols=n_cols, n_sub=n_sub),
+        [part_shape] * n_sub + [((3 * rows, width), f32), vec, vec, line],
+        (exchange(send), own, b, q, twice, half, u, keep, band, halves) + tiles,
+        scratch + [pltpu.VMEM((rows, width), f32)],
+    )
+    summed = parts[0]
+    for step in range(1, n_sub):
+        summed = summed + shifted(parts[step], "sub", step)
+    summed = sum_over(summed, "cols")
+    mine = jnp.concatenate([summed, three])
+    others = [shifted(mine, "rows", step) for step in range(1, n_rows)]
+    twice, half, total_search, dots = call(
+        functools.partial(fifth_kernel, n_rows=n_rows), [vec] * 3 + [line],
+        (mine, *others, kept, search, done), [pltpu.VMEM((part_size, width), f32)],
+    )
+    dots = sum_over(dots, "sub")
+    return tuple(call(last_kernel, [vec, vec], (dots, twice, half, total_search, band)))
 
 
 def solution(mesh):

time: 62 us -> 57.9 us (0.934)
  blocking collectives: 47.1 us -> 36.5 us
  waiting for transfers between devices: 2.7 us -> 9.19 us
    all_to_all x4 -> x3, blocking collectives: 47.1 us -> 36.5 us  [exchange(): lax.all_to_all(send, PART, 0, 0, tiled=True)]
    ppermute x4 -> x6, waiting for transfers between devices: 2.7 us -> 9.19 us  [shifted(): lax.ppermute(x, axis, [(i, partner(i, step, count)) for i in range(count)])]
    ppermute x4 -> x6, starting transfers between devices: 4.39 us -> 4.53 us  [shifted(): lax.ppermute(x, axis, [(i, partner(i, step, count)) for i in range(count)])]
  transfers between devices with their start and end apart: 4 -> 6, of which waited for: 3 -> 5; matrix products, arithmetic and copies ran while one was open for 0% -> 0% of each run, Pallas kernels for 0% -> 0%
where the time goes in v3:
time: 57.9 us; the launch traced here: 57.6 us
  blocking collectives  36.5 us (63%)
  waiting for transfers between devices  9.19 us (16%)
  Pallas kernels  6.68 us (12%)
  starting transfers between devices  4.53 us (8%)
  between operations  0.69 us (1%)
    all_to_all x3, blocking collectives, exchange(): lax.all_to_all(send, PART, 0, 0, tiled=True)  36.5 us
    ppermute x6, waiting for transfers between devices, shifted(): lax.ppermute(x, axis, [(i, partner(i, step, count)) for i in range(count)])  9.19 us
    pallas_call x6, Pallas kernels, call(): pl.pallas_call(kernel, out_shape=[pltpu.VMEM(shape, kind) if space == plt...  6.68 us
    ppermute x6, starting transfers between devices, shifted(): lax.ppermute(x, axis, [(i, partner(i, step, count)) for i in range(count)])  4.53 us
  transfers between devices with their start and end apart: 6, of which 5 were waited for; matrix products, arithmetic and copies ran while one was open for 0% of the time, Pallas kernels for 0%

profile of v3, /device:TPU:0, one launch (start us, length us, event | category | flops | bytes accessed | tf_op | source)
XLA Modules:
  0.0 57.6 jit_solution(12902716345514217889)
XLA Ops:
  0.6 3.0 %shard_map.86 = (f32[272,128]{1,0:T(8,128)S(1)}, f32[16,128]{1,0:T(8,128)S(1)}, f32[9,16,128]{2,1,0:T(8,128)S(1)}, bf16[272,144]{1,0:T(8,128)(2,1)S(1)}, bf16[14...) custom-call(f32[16,128]{1,0:T(8,128)} %b_hbm.1, ...), custom_call_target="tpu_custom_call" | custom-call | tf_op jit(solution)/shard_map/pallas_call | solution.py:321
  3.7 15.2 %all_to_all.15 = f32[16,17,1,128]{3,2,1,0:T(1,128)S(1)} all-to-all(f32[16,17,1,128]{3,2,1,0:T(1,128)S(1)} %bitcast.12), channel_id=1, replica_groups=mesh['groups'=2,'rows'=4,'cols'=2,'sub'=2] {'rows','cols','sub'}, dimensions={0} | all-to-all | bytes 278528 | tf_op jit(solution)/shard_map/all_to_all | solution.py:349
  18.9 0.8 %shard_map.87 = (f32[272,128]{1,0:T(8,128)S(1)}, f32[16,128]{1,0:T(8,128)S(1)}, f32[16,128]{1,0:T(8,128)S(1)}) custom-call(f32[272,128]{1,0:T(8,128)S(1)} %bitcast.10, f32[16,128]{1,0:T(8,128)S(1)} %get-tuple-element.30.own_in, f32[16,128]{1,0:T(8,128)S(1)} %get-tuple-element.31.b_ref, f32[9,16,128]{2,1,0:T(8,128)S(1)} %get-tuple-element.32.band_ref, ...), custom_call_target="tpu_custom_call" | custom-call | tf_op jit(solution)/shard_map/pallas_call | solution.py:321
  19.7 10.6 %all_to_all.16 = f32[16,17,1,128]{3,2,1,0:T(1,128)S(1)} all-to-all(f32[16,17,1,128]{3,2,1,0:T(1,128)S(1)} %bitcast.13), channel_id=1, replica_groups=mesh['groups'=2,'rows'=4,'cols'=2,'sub'=2] {'rows','cols','sub'}, dimensions={0} | all-to-all | bytes 278528 | tf_op jit(solution)/shard_map/all_to_all | solution.py:349
  30.3 0.8 %shard_map.88 = (f32[272,128]{1,0:T(8,128)S(1)}, f32[16,128]{1,0:T(8,128)S(1)}, f32[16,128]{1,0:T(8,128)S(1)}, f32[16,128]{1,0:T(8,128)S(1)}, f32[16,128]{1,0:T(8,128)S(1)}, /*index=5*/f32[1,128]{1,0:T(1,128)S(1)}) custom-call(f32[272,128]{1,0:T(8,128)S(1)} %bitcast.9, f32[16,128]{1,0:T(8,128)S(1)} %get-tuple-element.37.own_in, ...), custom_call_target="tpu_custom_call" | custom-call | tf_op jit(solution)/shard_map/pallas_call | solution.py:321
  31.1 10.6 %all_to_all.17 = f32[16,17,1,128]{3,2,1,0:T(1,128)S(1)} all-to-all(f32[16,17,1,128]{3,2,1,0:T(1,128)S(1)} %bitcast.11), channel_id=1, replica_groups=mesh['groups'=2,'rows'=4,'cols'=2,'sub'=2] {'rows','cols','sub'}, dimensions={0} | all-to-all | bytes 278528 | tf_op jit(solution)/shard_map/all_to_all | solution.py:349
  41.8 1.0 %shard_map.89 = (f32[72,128]{1,0:T(8,128)S(1)}, f32[72,128]{1,0:T(8,128)S(1)}, f32[48,128]{1,0:T(8,128)S(1)}, f32[16,128]{1,0:T(8,128)S(1)}, f32[16,128]{1,0:T(8,128)S(1)}, /*index=5*/f32[1,128]{1,0:T(1,128)S(1)}) custom-call(f32[272,128]{1,0:T(8,128)S(1)} %bitcast.8, f32[16,128]{1,0:T(8,128)S(1)} %get-tuple-element.40.own_in, ...), custom_call_target="tpu_custom_call" | custom-call | tf_op jit(solution)/shard_map/pallas_call | solution.py:321
  42.8 0.1 collective-permute-start
  42.8 1.2 %collective-permute-done = f32[72,128]{1,0:T(8,128)S(1)} collective-permute-done((f32[72,128]{1,0:T(8,128)S(1)}, f32[72,128]{1,0:T(8,128)S(1)}, u32[]{:S(2)}, u32[]{:S(2)}) %collective-permute-start) | collective-permute-done | bytes 36896 | tf_op jit(solution)/shard_map/ppermute | solution.py:307
  44.0 0.0 collective-permute-start.1
  44.1 3.9 %collective-permute-done.1 = f32[72,128]{1,0:T(8,128)S(1)} collective-permute-done((f32[72,128]{1,0:T(8,128)S(1)}, f32[72,128]{1,0:T(8,128)S(1)}, u32[]{:S(2)}, u32[]{:S(2)}) %collective-permute-start.1) | collective-permute-done | bytes 36896 | tf_op jit(solution)/shard_map/ppermute | solution.py:307
  48.0 0.7 %collective-permute-start.4 = (f32[120,128]{1,0:T(8,128)S(1)}, f32[120,128]{1,0:T(8,128)S(1)}, u32[]{:S(2)}, u32[]{:S(2)}) collective-permute-start(f32[120,128]{1,0:T(8,128)S(1)} %pad_maximum_fusion.mine_ref), channel_id=1, source_target_pairs={{0,12},{4,8},{8,4},{12,0},{1,13},{5,9},{9,5},{13,1},{2,14},{6,10},... | collective-permute-start | bytes 184328 | tf_op jit(solution)/shard_map/ppermute | solution.py:307
  48.8 0.4 collective-permute-start.3
  49.2 3.3 %collective-permute-start.2 = (f32[120,128]{1,0:T(8,128)S(1)}, f32[120,128]{1,0:T(8,128)S(1)}, u32[]{:S(2)}, u32[]{:S(2)}) collective-permute-start(f32[120,128]{1,0:T(8,128)S(1)} %pad_maximum_fusion.mine_ref), channel_id=1, source_target_pairs={{0,4},{4,0},{8,12},{12,8},{1,5},{5,1},{9,13},{13,9},{2,6},{6,2},{1... | collective-permute-start | bytes 184328 | tf_op jit(solution)/shard_map/ppermute | solution.py:307
  52.5 1.8 %collective-permute-done.4.refs_2_ = f32[120,128]{1,0:T(8,128)S(1)} collective-permute-done((f32[120,128]{1,0:T(8,128)S(1)}, f32[120,128]{1,0:T(8,128)S(1)}, u32[]{:S(2)}, u32[]{:S(2)}) %collective-permute-start.4) | collective-permute-done | bytes 61472 | tf_op jit(solution)/shard_map/ppermute | solution.py:307
  54.3 1.1 %collective-permute-done.3.refs_1_ = f32[120,128]{1,0:T(8,128)S(1)} collective-permute-done((f32[120,128]{1,0:T(8,128)S(1)}, f32[120,128]{1,0:T(8,128)S(1)}, u32[]{:S(2)}, u32[]{:S(2)}) %collective-permute-start.3) | collective-permute-done | bytes 61472 | tf_op jit(solution)/shard_map/ppermute | solution.py:307
  55.4 0.0 collective-permute-done.2.refs_0_
  55.4 0.2 shard_map.90
  55.6 0.0 collective-permute-start.5
  55.6 1.2 %collective-permute-done.5 = f32[1,128]{1,0:T(1,128)S(1)} collective-permute-done((f32[1,128]{1,0:T(1,128)S(1)}, f32[1,128]{1,0:T(1,128)S(1)}, u32[]{:S(2)}, u32[]{:S(2)}) %collective-permute-start.5) | collective-permute-done | bytes 544 | tf_op jit(solution)/shard_map/ppermute | solution.py:307
  56.8 0.8 %shard_map.91 = (f32[16,128]{1,0:T(8,128)}, f32[16,128]{1,0:T(8,128)}) custom-call(f32[1,128]{1,0:T(1,128)S(1)} %add.11.dots_ref, f32[16,128]{1,0:T(8,128)S(1)} %get-tuple-element.53.twice_ref, f32[16,128]{1,0:T(8,128)S(1)} %get-tuple-element.54.half_ref, f32[16,128]{1,0:T(8,128)S(1)} %get-tuple-element.55.sum_ref, f32[9,16,128]{2,1,0:T(8,128)S(1)} %get-tuple-element.32.band_ref), custom_call_target="tpu_custom_call" | custom-call | tf_op jit(solution)/shard_map/pallas_call | solution.py:321
  (4 shorter events, 0.0 us)
Async XLA Ops:
  42.8 1.3 %collective-permute-start = (f32[72,128]{1,0:T(8,128)S(1)}, f32[72,128]{1,0:T(8,128)S(1)}, u32[]{:S(2)}, u32[]{:S(2)}) collective-permute-start(f32[72,128]{1,0:T(8,128)S(1)} %get-tuple-element.47), channel_id=1, source_target_pairs={{0,1},{1,0},{2,3},{3,2},{4,5},{5,4},{6,7},{7,6},{8,9},{9,8},{10,11... | collective-permute-start | bytes 110600 | tf_op jit(solution)/shard_map/ppermute | solution.py:307
  44.0 4.0 %collective-permute-start.1 = (f32[72,128]{1,0:T(8,128)S(1)}, f32[72,128]{1,0:T(8,128)S(1)}, u32[]{:S(2)}, u32[]{:S(2)}) collective-permute-start(f32[72,128]{1,0:T(8,128)S(1)} %add.9), channel_id=1, source_target_pairs={{0,2},{2,0},{1,3},{3,1},{4,6},{6,4},{5,7},{7,5},{8,10},{10,8},{9,1... | collective-permute-start | bytes 110600 | tf_op jit(solution)/shard_map/ppermute | solution.py:307
  48.0 6.3 %collective-permute-start.4 = (f32[120,128]{1,0:T(8,128)S(1)}, f32[120,128]{1,0:T(8,128)S(1)}, u32[]{:S(2)}, u32[]{:S(2)}) collective-permute-start(f32[120,128]{1,0:T(8,128)S(1)} %pad_maximum_fusion.mine_ref), channel_id=1, source_target_pairs={{0,12},{4,8},{8,4},{12,0},{1,13},{5,9},{9,5},{13,1},{2,14},{6,10},... | collective-permute-start | bytes 184328 | tf_op jit(solution)/shard_map/ppermute | solution.py:307
  48.8 6.6 %collective-permute-start.3 = (f32[120,128]{1,0:T(8,128)S(1)}, f32[120,128]{1,0:T(8,128)S(1)}, u32[]{:S(2)}, u32[]{:S(2)}) collective-permute-start(f32[120,128]{1,0:T(8,128)S(1)} %pad_maximum_fusion.mine_ref), channel_id=1, source_target_pairs={{0,8},{4,12},{8,0},{12,4},{1,9},{5,13},{9,1},{13,5},{2,10},{6,14},... | collective-permute-start | bytes 184328 | tf_op jit(solution)/shard_map/ppermute | solution.py:307
  49.2 6.1 %collective-permute-start.2 = (f32[120,128]{1,0:T(8,128)S(1)}, f32[120,128]{1,0:T(8,128)S(1)}, u32[]{:S(2)}, u32[]{:S(2)}) collective-permute-start(f32[120,128]{1,0:T(8,128)S(1)} %pad_maximum_fusion.mine_ref), channel_id=1, source_target_pairs={{0,4},{4,0},{8,12},{12,8},{1,5},{5,1},{9,13},{13,9},{2,6},{6,2},{1... | collective-permute-start | bytes 184328 | tf_op jit(solution)/shard_map/ppermute | solution.py:307
  55.6 1.2 %collective-permute-start.5 = (f32[1,128]{1,0:T(1,128)S(1)}, f32[1,128]{1,0:T(1,128)S(1)}, u32[]{:S(2)}, u32[]{:S(2)}) collective-permute-start(f32[1,128]{1,0:T(1,128)S(1)} %get-tuple-element.52), channel_id=1, source_target_pairs={{0,1},{1,0},{2,3},{3,2},{4,5},{5,4},{6,7},{7,6},{8,9},{9,8},{10,11... | collective-permute-start | bytes 1544 | tf_op jit(solution)/shard_map/ppermute | solution.py:307

commit v4 on v3

--- a/solution.py
+++ b/solution.py
@@ -256,7 +256,7 @@
     parts[0][here, :] = parts[0][here, :] + jnp.where(first, own_ref[...], 0.0)
 
 
-def fifth_kernel(mine_ref, *refs, n_rows):
+def fifth_kernel(mine_ref, *refs, order, n_rows):
     others, (kept_ref, search_ref, done_ref, twice_ref, half_ref, sum_ref, dots_ref, full_ref) = (
         refs[: n_rows - 1],
         refs[n_rows - 1 :],
@@ -272,7 +272,7 @@
     factor = alpha / kept_ref[:, 1:2]
     own = lax.axis_index("rows")
     cross = square = None
-    for step, source in enumerate((mine_ref,) + tuple(others)):
+    for step, source in [(0, mine_ref)] + [(n + 1, other) for n, other in zip(order, others)]:
         at = own if step == 0 else sender(own, step, n_rows)
         a, residual, image = (source[pl.ds(size + n * rows, rows), :] for n in range(3))
         twice = a - factor * full_ref[pl.ds(pl.multiple_of(at * rows, rows), rows), :]
@@ -286,12 +286,17 @@
     dots_ref[...] = pack([total(cross), total(square)], width)
 
 
-def last_kernel(dots_ref, twice_ref, half_ref, sum_ref, band_ref, solution_ref, residual_ref):
-    dots = dots_ref[...]
+def map_kernel(half_ref, sum_ref, band_ref, half_hat_ref, sum_hat_ref):
+    half_hat_ref[...] = apply_m(band_ref, half_ref[...])
+    sum_hat_ref[...] = apply_m(band_ref, sum_ref[...])
+
+
+def last_kernel(twice_ref, half_ref, half_hat_ref, sum_hat_ref, *refs):
+    *shares, solution_ref, residual_ref = refs
+    dots = functools.reduce(jnp.add, [share[...] for share in shares])
     omega = dots[:, 0:1] / dots[:, 1:2]
-    half = half_ref[...]
-    residual_ref[...] = half - omega * twice_ref[...]
-    solution_ref[...] = apply_m(band_ref, sum_ref[...] + omega * half)
+    residual_ref[...] = half_ref[...] - omega * twice_ref[...]
+    solution_ref[...] = sum_hat_ref[...] + omega * half_hat_ref[...]
 
 
 def partner(at, step, count):
@@ -380,12 +385,14 @@
     summed = sum_over(summed, "cols")
     mine = jnp.concatenate([summed, three])
     others = [shifted(mine, "rows", step) for step in range(1, n_rows)]
+    order = [1, 0, *range(2, n_rows - 1)]
     twice, half, total_search, dots = call(
-        functools.partial(fifth_kernel, n_rows=n_rows), [vec] * 3 + [line],
-        (mine, *others, kept, search, done), [pltpu.VMEM((part_size, width), f32)],
-    )
-    dots = sum_over(dots, "sub")
-    return tuple(call(last_kernel, [vec, vec], (dots, twice, half, total_search, band)))
+        functools.partial(fifth_kernel, order=order, n_rows=n_rows), [vec] * 3 + [line],
+        (mine, *(others[n] for n in order), kept, search, done), [pltpu.VMEM((part_size, width), f32)],
+    )
+    half_hat, sum_hat = call(map_kernel, [vec, vec], (half, total_search, band))
+    shares = [dots] + [shifted(dots, "sub", step) for step in range(1, n_sub)]
+    return tuple(call(last_kernel, [vec, vec], (twice, half, half_hat, sum_hat, *shares)))
 
 
 def solution(mesh):

time: 57.9 us -> 57.3 us (0.990)
  waiting for transfers between devices: 9.19 us -> 8.5 us
    ppermute x6, waiting for transfers between devices: 9.19 us -> 8.5 us  [shifted(): lax.ppermute(x, axis, [(i, partner(i, step, count)) for i in range(count)])]
    pallas_call x6 -> x7, Pallas kernels: 6.68 us -> 6.7 us  [call(): pl.pallas_call(kernel, out_shape=[pltpu.VMEM(shape, kind) if space == plt...]
where the time goes in v4:
time: 57.3 us; the launch traced here: 56.9 us
  blocking collectives  36.5 us (64%)
  waiting for transfers between devices  8.5 us (15%)
  Pallas kernels  6.7 us (12%)
  starting transfers between devices  4.53 us (8%)
  between operations  0.7 us (1%)
    all_to_all x3, blocking collectives, exchange(): lax.all_to_all(send, PART, 0, 0, tiled=True)  36.5 us
    ppermute x6, waiting for transfers between devices, shifted(): lax.ppermute(x, axis, [(i, partner(i, step, count)) for i in range(count)])  8.5 us
    pallas_call x7, Pallas kernels, call(): pl.pallas_call(kernel, out_shape=[pltpu.VMEM(shape, kind) if space == plt...  6.7 us
    ppermute x6, starting transfers between devices, shifted(): lax.ppermute(x, axis, [(i, partner(i, step, count)) for i in range(count)])  4.53 us
  transfers between devices with their start and end apart: 6, of which 5 were waited for; matrix products, arithmetic and copies ran while one was open for 0% of the time, Pallas kernels for 0%

profile of v4, /device:TPU:0, one launch (start us, length us, event | category | flops | bytes accessed | tf_op | source)
XLA Modules:
  0.0 56.9 jit_solution(9024334279411793828)
XLA Ops:
  0.6 3.0 %shard_map.86 = (f32[272,128]{1,0:T(8,128)S(1)}, f32[16,128]{1,0:T(8,128)S(1)}, f32[9,16,128]{2,1,0:T(8,128)S(1)}, bf16[272,144]{1,0:T(8,128)(2,1)S(1)}, bf16[14...) custom-call(f32[16,128]{1,0:T(8,128)} %b_hbm.1, ...), custom_call_target="tpu_custom_call" | custom-call | tf_op jit(solution)/shard_map/pallas_call | solution.py:326
  3.7 15.2 %all_to_all.15 = f32[16,17,1,128]{3,2,1,0:T(1,128)S(1)} all-to-all(f32[16,17,1,128]{3,2,1,0:T(1,128)S(1)} %bitcast.12), channel_id=1, replica_groups=mesh['groups'=2,'rows'=4,'cols'=2,'sub'=2] {'rows','cols','sub'}, dimensions={0} | all-to-all | bytes 278528 | tf_op jit(solution)/shard_map/all_to_all | solution.py:354
  18.9 0.8 %shard_map.87 = (f32[272,128]{1,0:T(8,128)S(1)}, f32[16,128]{1,0:T(8,128)S(1)}, f32[16,128]{1,0:T(8,128)S(1)}) custom-call(f32[272,128]{1,0:T(8,128)S(1)} %bitcast.10, f32[16,128]{1,0:T(8,128)S(1)} %get-tuple-element.32.own_in, f32[16,128]{1,0:T(8,128)S(1)} %get-tuple-element.33.b_ref, f32[9,16,128]{2,1,0:T(8,128)S(1)} %get-tuple-element.34.band_ref, ...), custom_call_target="tpu_custom_call" | custom-call | tf_op jit(solution)/shard_map/pallas_call | solution.py:326
  19.7 10.6 %all_to_all.16 = f32[16,17,1,128]{3,2,1,0:T(1,128)S(1)} all-to-all(f32[16,17,1,128]{3,2,1,0:T(1,128)S(1)} %bitcast.13), channel_id=1, replica_groups=mesh['groups'=2,'rows'=4,'cols'=2,'sub'=2] {'rows','cols','sub'}, dimensions={0} | all-to-all | bytes 278528 | tf_op jit(solution)/shard_map/all_to_all | solution.py:354
  30.3 0.8 %shard_map.88 = (f32[272,128]{1,0:T(8,128)S(1)}, f32[16,128]{1,0:T(8,128)S(1)}, f32[16,128]{1,0:T(8,128)S(1)}, f32[16,128]{1,0:T(8,128)S(1)}, f32[16,128]{1,0:T(8,128)S(1)}, /*index=5*/f32[1,128]{1,0:T(1,128)S(1)}) custom-call(f32[272,128]{1,0:T(8,128)S(1)} %bitcast.9, f32[16,128]{1,0:T(8,128)S(1)} %get-tuple-element.39.own_in, ...), custom_call_target="tpu_custom_call" | custom-call | tf_op jit(solution)/shard_map/pallas_call | solution.py:326
  31.1 10.6 %all_to_all.17 = f32[16,17,1,128]{3,2,1,0:T(1,128)S(1)} all-to-all(f32[16,17,1,128]{3,2,1,0:T(1,128)S(1)} %bitcast.11), channel_id=1, replica_groups=mesh['groups'=2,'rows'=4,'cols'=2,'sub'=2] {'rows','cols','sub'}, dimensions={0} | all-to-all | bytes 278528 | tf_op jit(solution)/shard_map/all_to_all | solution.py:354
  41.8 1.0 %shard_map.89 = (f32[72,128]{1,0:T(8,128)S(1)}, f32[72,128]{1,0:T(8,128)S(1)}, f32[48,128]{1,0:T(8,128)S(1)}, f32[16,128]{1,0:T(8,128)S(1)}, f32[16,128]{1,0:T(8,128)S(1)}, /*index=5*/f32[1,128]{1,0:T(1,128)S(1)}) custom-call(f32[272,128]{1,0:T(8,128)S(1)} %bitcast.8, f32[16,128]{1,0:T(8,128)S(1)} %get-tuple-element.42.own_in, ...), custom_call_target="tpu_custom_call" | custom-call | tf_op jit(solution)/shard_map/pallas_call | solution.py:326
  42.8 0.1 collective-permute-start
  42.8 1.2 %collective-permute-done = f32[72,128]{1,0:T(8,128)S(1)} collective-permute-done((f32[72,128]{1,0:T(8,128)S(1)}, f32[72,128]{1,0:T(8,128)S(1)}, u32[]{:S(2)}, u32[]{:S(2)}) %collective-permute-start) | collective-permute-done | bytes 36896 | tf_op jit(solution)/shard_map/ppermute | solution.py:312
  44.0 0.0 collective-permute-start.1
  44.1 3.9 %collective-permute-done.1 = f32[72,128]{1,0:T(8,128)S(1)} collective-permute-done((f32[72,128]{1,0:T(8,128)S(1)}, f32[72,128]{1,0:T(8,128)S(1)}, u32[]{:S(2)}, u32[]{:S(2)}) %collective-permute-start.1) | collective-permute-done | bytes 36896 | tf_op jit(solution)/shard_map/ppermute | solution.py:312
  48.0 0.7 %collective-permute-start.4 = (f32[120,128]{1,0:T(8,128)S(1)}, f32[120,128]{1,0:T(8,128)S(1)}, u32[]{:S(2)}, u32[]{:S(2)}) collective-permute-start(f32[120,128]{1,0:T(8,128)S(1)} %pad_maximum_fusion.mine_ref), channel_id=1, source_target_pairs={{0,12},{4,8},{8,4},{12,0},{1,13},{5,9},{9,5},{13,1},{2,14},{6,10},... | collective-permute-start | bytes 184328 | tf_op jit(solution)/shard_map/ppermute | solution.py:312
  48.8 0.3 collective-permute-start.3
  49.1 3.4 %collective-permute-start.2 = (f32[120,128]{1,0:T(8,128)S(1)}, f32[120,128]{1,0:T(8,128)S(1)}, u32[]{:S(2)}, u32[]{:S(2)}) collective-permute-start(f32[120,128]{1,0:T(8,128)S(1)} %pad_maximum_fusion.mine_ref), channel_id=1, source_target_pairs={{0,8},{4,12},{8,0},{12,4},{1,9},{5,13},{9,1},{13,5},{2,10},{6,14},... | collective-permute-start | bytes 184328 | tf_op jit(solution)/shard_map/ppermute | solution.py:312
  52.5 1.7 %collective-permute-done.4.refs_2_ = f32[120,128]{1,0:T(8,128)S(1)} collective-permute-done((f32[120,128]{1,0:T(8,128)S(1)}, f32[120,128]{1,0:T(8,128)S(1)}, u32[]{:S(2)}, u32[]{:S(2)}) %collective-permute-start.4) | collective-permute-done | bytes 61472 | tf_op jit(solution)/shard_map/ppermute | solution.py:312
  54.1 0.0 collective-permute-done.3.refs_1_
  54.1 0.6 %collective-permute-done.2.refs_0_ = f32[120,128]{1,0:T(8,128)S(1)} collective-permute-done((f32[120,128]{1,0:T(8,128)S(1)}, f32[120,128]{1,0:T(8,128)S(1)}, u32[]{:S(2)}, u32[]{:S(2)}) %collective-permute-start.2) | collective-permute-done | bytes 61472 | tf_op jit(solution)/shard_map/ppermute | solution.py:312
  54.8 0.2 shard_map.90
  55.0 0.0 collective-permute-start.5
  55.0 0.1 shard_map.91
  55.1 1.0 %collective-permute-done.5.refs_1_ = f32[1,128]{1,0:T(1,128)S(1)} collective-permute-done((f32[1,128]{1,0:T(1,128)S(1)}, f32[1,128]{1,0:T(1,128)S(1)}, u32[]{:S(2)}, u32[]{:S(2)}) %collective-permute-start.5) | collective-permute-done | bytes 544 | tf_op jit(solution)/shard_map/ppermute | solution.py:312
  56.2 0.8 %shard_map.92 = (f32[16,128]{1,0:T(8,128)}, f32[16,128]{1,0:T(8,128)}) custom-call(f32[16,128]{1,0:T(8,128)S(1)} %get-tuple-element.54.twice_ref, f32[16,128]{1,0:T(8,128)S(1)} %get-tuple-element.55.half_ref, f32[16,128]{1,0:T(8,128)S(1)} %get-tuple-element.57.half_hat_ref, f32[16,128]{1,0:T(8,128)S(1)} %get-tuple-element.58.sum_hat_ref, ...), custom_call_target="tpu_custom_call" | custom-call | tf_op jit(solution)/shard_map/pallas_call | solution.py:326
  (3 shorter events, 0.0 us)
Async XLA Ops:
  42.8 1.3 %collective-permute-start = (f32[72,128]{1,0:T(8,128)S(1)}, f32[72,128]{1,0:T(8,128)S(1)}, u32[]{:S(2)}, u32[]{:S(2)}) collective-permute-start(f32[72,128]{1,0:T(8,128)S(1)} %get-tuple-element.49), channel_id=1, source_target_pairs={{0,1},{1,0},{2,3},{3,2},{4,5},{5,4},{6,7},{7,6},{8,9},{9,8},{10,11... | collective-permute-start | bytes 110600 | tf_op jit(solution)/shard_map/ppermute | solution.py:312
  44.0 4.0 %collective-permute-start.1 = (f32[72,128]{1,0:T(8,128)S(1)}, f32[72,128]{1,0:T(8,128)S(1)}, u32[]{:S(2)}, u32[]{:S(2)}) collective-permute-start(f32[72,128]{1,0:T(8,128)S(1)} %add.6), channel_id=1, source_target_pairs={{0,2},{2,0},{1,3},{3,1},{4,6},{6,4},{5,7},{7,5},{8,10},{10,8},{9,1... | collective-permute-start | bytes 110600 | tf_op jit(solution)/shard_map/ppermute | solution.py:312
  48.0 6.1 %collective-permute-start.4 = (f32[120,128]{1,0:T(8,128)S(1)}, f32[120,128]{1,0:T(8,128)S(1)}, u32[]{:S(2)}, u32[]{:S(2)}) collective-permute-start(f32[120,128]{1,0:T(8,128)S(1)} %pad_maximum_fusion.mine_ref), channel_id=1, source_target_pairs={{0,12},{4,8},{8,4},{12,0},{1,13},{5,9},{9,5},{13,1},{2,14},{6,10},... | collective-permute-start | bytes 184328 | tf_op jit(solution)/shard_map/ppermute | solution.py:312
  48.8 5.4 %collective-permute-start.3 = (f32[120,128]{1,0:T(8,128)S(1)}, f32[120,128]{1,0:T(8,128)S(1)}, u32[]{:S(2)}, u32[]{:S(2)}) collective-permute-start(f32[120,128]{1,0:T(8,128)S(1)} %pad_maximum_fusion.mine_ref), channel_id=1, source_target_pairs={{0,4},{4,0},{8,12},{12,8},{1,5},{5,1},{9,13},{13,9},{2,6},{6,2},{1... | collective-permute-start | bytes 184328 | tf_op jit(solution)/shard_map/ppermute | solution.py:312
  49.1 5.7 %collective-permute-start.2 = (f32[120,128]{1,0:T(8,128)S(1)}, f32[120,128]{1,0:T(8,128)S(1)}, u32[]{:S(2)}, u32[]{:S(2)}) collective-permute-start(f32[120,128]{1,0:T(8,128)S(1)} %pad_maximum_fusion.mine_ref), channel_id=1, source_target_pairs={{0,8},{4,12},{8,0},{12,4},{1,9},{5,13},{9,1},{13,5},{2,10},{6,14},... | collective-permute-start | bytes 184328 | tf_op jit(solution)/shard_map/ppermute | solution.py:312
  55.0 1.2 %collective-permute-start.5 = (f32[1,128]{1,0:T(1,128)S(1)}, f32[1,128]{1,0:T(1,128)S(1)}, u32[]{:S(2)}, u32[]{:S(2)}) collective-permute-start(f32[1,128]{1,0:T(1,128)S(1)} %get-tuple-element.59.refs_0_), channel_id=1, source_target_pairs={{0,1},{1,0},{2,3},{3,2},{4,5},{5,4},{6,7},{7,6},{8,9},{9,8},{10,11... | collective-permute-start | bytes 1544 | tf_op jit(solution)/shard_map/ppermute | solution.py:312

commit v5 on v4

--- a/solution.py
+++ b/solution.py
@@ -10,7 +10,7 @@
 BLOCK = 5
 BAND = BLOCK - 1
 LANES = 128
-PART = ("rows", "cols", "sub")
+PART = ("rows", "sub", "cols")
 
 
 def apply_m(band_ref, v):
@@ -64,6 +64,8 @@
     rows = z.shape[0]
     products(z, coupling_ref, diagonal_ref, partial_ref, own_ref, before)
     send_ref[...] = jnp.dot(spread_ref[...], split3(partial_ref[...]), preferred_element_type=jnp.float32)
+    if callable(tail):
+        tail = tail()
     for d in range(send_ref.shape[0] // (rows + 1)):
         send_ref[pl.ds(d * (rows + 1) + rows, 1), :] = tail
 
@@ -84,19 +86,25 @@
     return jnp.max(jnp.max(jnp.abs(x), axis=0, keepdims=True), axis=1, keepdims=True)
 
 
-def level(x, like):
-    size, aim = peak(x), peak(like)
-    good = (size > 0) & (aim > 0)
-    return jnp.where(good, aim / size, 1.0), jnp.where(good, size / aim, 1.0)
-
-
-def gather_tails(recv_ref, rows):
+def pairwise(join, items):
+    items = list(items)
+    while len(items) > 1:
+        items = [join(*items[n : n + 2]) if n + 1 < len(items) else items[n] for n in range(0, len(items), 2)]
+    return items[0]
+
+
+def tails_of(recv_ref, rows):
     count = recv_ref.shape[0] // (rows + 1)
     return [recv_ref[pl.ds(d * (rows + 1) + rows, 1), :] for d in range(count)]
 
 
 def chunk(recv_ref, d, rows):
     return recv_ref[pl.ds(d * (rows + 1), rows), :]
+
+
+def chunks_of(recv_ref, own_in):
+    rows = own_in.shape[0]
+    return pairwise(jnp.add, [own_in[...]] + [chunk(recv_ref, d, rows) for d in range(recv_ref.shape[0] // (rows + 1))])
 
 
 def first_kernel(
@@ -142,7 +150,7 @@
     landing = jnp.concatenate([landing[k : k + 1] for k in range(slots)] * 3, axis=1)
     at = lax.broadcasted_iota(jnp.int32, (spread_ref.shape[0], 1), 0)
     device, line = at // (rows + 1), at % (rows + 1)
-    row, sub = device // (n_cols * n_sub), device % n_sub
+    row, sub = device // (n_cols * n_sub), device // n_cols % n_sub
     wanted = jnp.where(line < rows, row * (rows * n_sub) + sub * rows + line, -1)
     spread_ref[...] = jnp.where(landing == wanted, 1.0, 0.0).astype(jnp.bfloat16)
     at = lax.broadcasted_iota(jnp.int32, (halves_ref.shape[0], 1), 0)
@@ -167,50 +175,43 @@
         copy_of(g, coupling_hbm, coupling_ref, coupling_sem).wait()
         copy_of(g, diagonal_hbm, diagonal_ref, diagonal_sem).wait()
 
-    tail = jnp.zeros((1, width), jnp.float32)
+    def tail():
+        return pack([peak(b_ref[...]), jnp.maximum(peak(partial_ref[...]), peak(own_ref[...]))], width)
+
     emit(z, tail, spread_ref, coupling_ref, diagonal_ref, partial_ref, own_ref, send_ref, before)
 
 
 def second_kernel(
     recv_ref, own_in, b_ref, band_ref, spread_ref, coupling_ref, diagonal_ref,
-    send_ref, own_ref, q_ref, partial_ref,
+    send_ref, own_ref, q_ref, scale_ref, partial_ref,
 ):
     b = b_ref[...]
     rows, width = b.shape
-    q = own_in[...]
-    for d in range(recv_ref.shape[0] // (rows + 1)):
-        q = q + chunk(recv_ref, d, rows)
+    top = pairwise(jnp.maximum, tails_of(recv_ref, rows))
+    size, reach = top[:, 0:1], top[:, 1:2]
+    scale = jnp.where((size > 0) & (reach > 0), size / reach, 1.0)
+    q = chunks_of(recv_ref, own_in)
     q_ref[...] = q
-    up, down = level(q, b)
-    tail = pack([total(b * b), total(b * q), down], width)
-    z = apply_m(band_ref, q * up)
+    scale_ref[...] = jnp.broadcast_to(scale, (1, width))
+    tail = pack([total(b * b), total(b * q)], width)
+    z = apply_m(band_ref, scale * q)
     emit(z, tail, spread_ref, coupling_ref, diagonal_ref, partial_ref, own_ref, send_ref)
 
 
 def scalars_of(recv_ref, rows, count, repeats):
-    tails = gather_tails(recv_ref, rows)
-    summed = functools.reduce(jnp.add, tails)
-    return tails, [summed[:, n : n + 1] / repeats for n in range(count)]
-
-
-def weighted(recv_ref, own_in, own_down, tails, at, factor):
-    rows = own_in.shape[0]
-    out = own_in[...] * (factor * own_down)
-    for d, tail in enumerate(tails):
-        out = out + chunk(recv_ref, d, rows) * (factor * tail[:, at : at + 1])
-    return out
+    summed = pairwise(jnp.add, tails_of(recv_ref, rows)) * (1.0 / repeats)
+    return [summed[:, n : n + 1] for n in range(count)]
 
 
 def third_kernel(
-    recv_ref, own_in, b_ref, q_ref, band_ref, spread_ref, coupling_ref, diagonal_ref,
+    recv_ref, own_in, b_ref, q_ref, scale_ref, band_ref, spread_ref, coupling_ref, diagonal_ref,
     send_ref, own_ref, twice_ref, half_ref, u_ref, keep_ref, partial_ref, *, n_cols,
 ):
     b, q = b_ref[...], q_ref[...]
     rows, width = b.shape
-    tails, (rho, cross) = scalars_of(recv_ref, rows, 2, n_cols)
+    rho, cross = scalars_of(recv_ref, rows, 2, n_cols)
     alpha = rho / cross
-    _, down = level(q, b)
-    u = weighted(recv_ref, own_in, down, tails, 2, alpha)
+    u = (alpha / scale_ref[:, 0:1]) * chunks_of(recv_ref, own_in)
     twice = q - u
     half = b - alpha * q
     tail = pack([total(twice * half), total(twice * twice), total(b * half), total(b * twice)], width)
@@ -228,15 +229,12 @@
     b, q, twice, half = b_ref[...], q_ref[...], twice_ref[...], half_ref[...]
     rows, width = b.shape
     rho, alpha = keep_ref[:, 0:1], keep_ref[:, 1:2]
-    _, (cross, square, b_half, b_twice) = scalars_of(recv_ref, rows, 4, n_cols)
+    cross, square, b_half, b_twice = scalars_of(recv_ref, rows, 4, n_cols)
     omega = cross / square
     rho_next = b_half - omega * b_twice
     ratio = rho_next / rho
     beta = ratio * (alpha / omega)
-    a = own_in[...]
-    for d in range(recv_ref.shape[0] // (rows + 1)):
-        a = a + chunk(recv_ref, d, rows)
-    a = twice - (omega / alpha) * a
+    a = twice - (omega / alpha) * chunks_of(recv_ref, own_in)
     residual = half - omega * twice
     image = a + beta * q - ratio * u_ref[...]
     three_ref[...] = jnp.concatenate([a, residual, image], axis=0)
@@ -337,7 +335,7 @@
     f32 = jnp.float32
     rows, width = b.shape
     slots = coupling.shape[1]
-    sizes = tuple(lax.axis_size(axis) for axis in PART)
+    sizes = tuple(lax.axis_size(axis) for axis in ("rows", "cols", "sub"))
     n_rows, n_cols, n_sub = sizes
     devices = n_rows * n_cols * n_sub
     vec, line = ((rows, width), f32), ((1, width), f32)
@@ -366,12 +364,12 @@
         pltpu.HBM,
     )
     tiles = (coupling, diagonal)
-    send, own, q = call(
-        second_kernel, [message, vec, vec], (exchange(send), own, b, band, spread) + tiles, scratch
+    send, own, q, scale = call(
+        second_kernel, [message, vec, vec, line], (exchange(send), own, b, band, spread) + tiles, scratch
     )
     send, own, twice, half, u, keep = call(
         functools.partial(third_kernel, n_cols=n_cols), [message] + [vec] * 4 + [line],
-        (exchange(send), own, b, q, band, spread) + tiles, scratch,
+        (exchange(send), own, b, q, scale, band, spread) + tiles, scratch,
     )
     *parts, three, search, done, kept = call(
         functools.partial(fourth_kernel, n_rows=n_rows, n_cols=n_cols, n_sub=n_sub),

time: 57.3 us -> 56.8 us (level)
  blocking collectives: 36.5 us -> 35.6 us
  starting transfers between devices: 4.53 us -> 5.2 us
    all_to_all x3, blocking collectives: 36.5 us -> 35.6 us  [exchange(): lax.all_to_all(send, PART, 0, 0, tiled=True)]
    ppermute x6, starting transfers between devices: 4.53 us -> 5.2 us  [shifted(): lax.ppermute(x, axis, [(i, partner(i, step, count)) for i in range(count)])]
  transfers between devices with their start and end apart: 6 -> 6, of which waited for: 5 -> 6; matrix products, arithmetic and copies ran while one was open for 0% -> 0% of each run, Pallas kernels for 0% -> 0%
where the time goes in v5:
time: 56.8 us; the launch traced here: 56.5 us
  blocking collectives  35.6 us (63%)
  waiting for transfers between devices  8.51 us (15%)
  Pallas kernels  6.5 us (11%)
  starting transfers between devices  5.2 us (9%)
  between operations  0.69 us (1%)
    all_to_all x3, blocking collectives, exchange(): lax.all_to_all(send, PART, 0, 0, tiled=True)  35.6 us
    ppermute x6, waiting for transfers between devices, shifted(): lax.ppermute(x, axis, [(i, partner(i, step, count)) for i in range(count)])  8.51 us
    pallas_call x7, Pallas kernels, call(): pl.pallas_call(kernel, out_shape=[pltpu.VMEM(shape, kind) if space == plt...  6.5 us
    ppermute x6, starting transfers between devices, shifted(): lax.ppermute(x, axis, [(i, partner(i, step, count)) for i in range(count)])  5.2 us
  transfers between devices with their start and end apart: 6, of which 6 were waited for; matrix products, arithmetic and copies ran while one was open for 0% of the time, Pallas kernels for 0%

profile of v5, /device:TPU:0, one launch (start us, length us, event | category | flops | bytes accessed | tf_op | source)
XLA Modules:
  0.0 56.5 jit_solution(1131567602835828496)
XLA Ops:
  0.6 3.0 %shard_map.86 = (f32[272,128]{1,0:T(8,128)S(1)}, f32[16,128]{1,0:T(8,128)S(1)}, f32[9,16,128]{2,1,0:T(8,128)S(1)}, bf16[272,144]{1,0:T(8,128)(2,1)S(1)}, bf16[14...) custom-call(f32[16,128]{1,0:T(8,128)} %b_hbm.1, ...), custom_call_target="tpu_custom_call" | custom-call | tf_op jit(solution)/shard_map/pallas_call | solution.py:324
  3.7 14.8 %all_to_all.15 = f32[16,17,1,128]{3,2,1,0:T(1,128)S(1)} all-to-all(f32[16,17,1,128]{3,2,1,0:T(1,128)S(1)} %bitcast.12), channel_id=1, replica_groups=mesh['groups'=2,'rows'=4,'cols'=2,'sub'=2] {'rows','sub','cols'}, dimensions={0} | all-to-all | bytes 278528 | tf_op jit(solution)/shard_map/all_to_all | solution.py:352
  18.4 0.7 %shard_map.87 = (f32[272,128]{1,0:T(8,128)S(1)}, f32[16,128]{1,0:T(8,128)S(1)}, f32[16,128]{1,0:T(8,128)S(1)}, f32[1,128]{1,0:T(1,128)S(1)}) custom-call(f32[272,128]{1,0:T(8,128)S(1)} %bitcast.10, f32[16,128]{1,0:T(8,128)S(1)} %get-tuple-element.33.own_in, f32[16,128]{1,0:T(8,128)S(1)} %get-tuple-element.34.b_ref, ...), custom_call_target="tpu_custom_call" | custom-call | tf_op jit(solution)/shard_map/pallas_call | solution.py:324
  19.1 10.4 %all_to_all.16 = f32[16,17,1,128]{3,2,1,0:T(1,128)S(1)} all-to-all(f32[16,17,1,128]{3,2,1,0:T(1,128)S(1)} %bitcast.13), channel_id=1, replica_groups=mesh['groups'=2,'rows'=4,'cols'=2,'sub'=2] {'rows','sub','cols'}, dimensions={0} | all-to-all | bytes 278528 | tf_op jit(solution)/shard_map/all_to_all | solution.py:352
  29.6 0.7 %shard_map.88 = (f32[272,128]{1,0:T(8,128)S(1)}, f32[16,128]{1,0:T(8,128)S(1)}, f32[16,128]{1,0:T(8,128)S(1)}, f32[16,128]{1,0:T(8,128)S(1)}, f32[16,128]{1,0:T(8,128)S(1)}, /*index=5*/f32[1,128]{1,0:T(1,128)S(1)}) custom-call(f32[272,128]{1,0:T(8,128)S(1)} %bitcast.9, f32[16,128]{1,0:T(8,128)S(1)} %get-tuple-element.40.own_in, ...), custom_call_target="tpu_custom_call" | custom-call | tf_op jit(solution)/shard_map/pallas_call | solution.py:324
  30.3 10.4 %all_to_all.17 = f32[16,17,1,128]{3,2,1,0:T(1,128)S(1)} all-to-all(f32[16,17,1,128]{3,2,1,0:T(1,128)S(1)} %bitcast.11), channel_id=1, replica_groups=mesh['groups'=2,'rows'=4,'cols'=2,'sub'=2] {'rows','sub','cols'}, dimensions={0} | all-to-all | bytes 278528 | tf_op jit(solution)/shard_map/all_to_all | solution.py:352
  40.8 0.9 %shard_map.89 = (f32[72,128]{1,0:T(8,128)S(1)}, f32[72,128]{1,0:T(8,128)S(1)}, f32[48,128]{1,0:T(8,128)S(1)}, f32[16,128]{1,0:T(8,128)S(1)}, f32[16,128]{1,0:T(8,128)S(1)}, /*index=5*/f32[1,128]{1,0:T(1,128)S(1)}) custom-call(f32[272,128]{1,0:T(8,128)S(1)} %bitcast.8, f32[16,128]{1,0:T(8,128)S(1)} %get-tuple-element.44.own_in, ...), custom_call_target="tpu_custom_call" | custom-call | tf_op jit(solution)/shard_map/pallas_call | solution.py:324
  41.7 0.2 collective-permute-start
  41.9 1.1 %collective-permute-done = f32[72,128]{1,0:T(8,128)S(1)} collective-permute-done((f32[72,128]{1,0:T(8,128)S(1)}, f32[72,128]{1,0:T(8,128)S(1)}, u32[]{:S(2)}, u32[]{:S(2)}) %collective-permute-start) | collective-permute-done | bytes 36896 | tf_op jit(solution)/shard_map/ppermute | solution.py:310
  43.0 0.6 collective-permute-start.1
  43.5 3.4 %collective-permute-done.1 = f32[72,128]{1,0:T(8,128)S(1)} collective-permute-done((f32[72,128]{1,0:T(8,128)S(1)}, f32[72,128]{1,0:T(8,128)S(1)}, u32[]{:S(2)}, u32[]{:S(2)}) %collective-permute-start.1) | collective-permute-done | bytes 36896 | tf_op jit(solution)/shard_map/ppermute | solution.py:310
  47.0 1.7 %collective-permute-start.4 = (f32[120,128]{1,0:T(8,128)S(1)}, f32[120,128]{1,0:T(8,128)S(1)}, u32[]{:S(2)}, u32[]{:S(2)}) collective-permute-start(f32[120,128]{1,0:T(8,128)S(1)} %pad_maximum_fusion.mine_ref), channel_id=1, source_target_pairs={{0,12},{4,8},{8,4},{12,0},{1,13},{5,9},{9,5},{13,1},{2,14},{6,10},... | collective-permute-start | bytes 184328 | tf_op jit(solution)/shard_map/ppermute | solution.py:310
  48.7 0.0 collective-permute-start.3
  48.7 2.7 %collective-permute-start.2 = (f32[120,128]{1,0:T(8,128)S(1)}, f32[120,128]{1,0:T(8,128)S(1)}, u32[]{:S(2)}, u32[]{:S(2)}) collective-permute-start(f32[120,128]{1,0:T(8,128)S(1)} %pad_maximum_fusion.mine_ref), channel_id=1, source_target_pairs={{0,8},{4,12},{8,0},{12,4},{1,9},{5,13},{9,1},{13,5},{2,10},{6,14},... | collective-permute-start | bytes 184328 | tf_op jit(solution)/shard_map/ppermute | solution.py:310
  51.4 2.1 %collective-permute-done.4.refs_2_ = f32[120,128]{1,0:T(8,128)S(1)} collective-permute-done((f32[120,128]{1,0:T(8,128)S(1)}, f32[120,128]{1,0:T(8,128)S(1)}, u32[]{:S(2)}, u32[]{:S(2)}) %collective-permute-start.4) | collective-permute-done | bytes 61472 | tf_op jit(solution)/shard_map/ppermute | solution.py:310
  53.5 0.1 collective-permute-done.3.refs_1_
  53.6 0.7 %collective-permute-done.2.refs_0_ = f32[120,128]{1,0:T(8,128)S(1)} collective-permute-done((f32[120,128]{1,0:T(8,128)S(1)}, f32[120,128]{1,0:T(8,128)S(1)}, u32[]{:S(2)}, u32[]{:S(2)}) %collective-permute-start.2) | collective-permute-done | bytes 61472 | tf_op jit(solution)/shard_map/ppermute | solution.py:310
  54.4 0.2 shard_map.90
  54.6 0.0 collective-permute-start.5
  54.6 0.1 shard_map.91
  54.7 1.0 %collective-permute-done.5.refs_1_ = f32[1,128]{1,0:T(1,128)S(1)} collective-permute-done((f32[1,128]{1,0:T(1,128)S(1)}, f32[1,128]{1,0:T(1,128)S(1)}, u32[]{:S(2)}, u32[]{:S(2)}) %collective-permute-start.5) | collective-permute-done | bytes 544 | tf_op jit(solution)/shard_map/ppermute | solution.py:310
  55.8 0.8 %shard_map.92 = (f32[16,128]{1,0:T(8,128)}, f32[16,128]{1,0:T(8,128)}) custom-call(f32[16,128]{1,0:T(8,128)S(1)} %get-tuple-element.56.twice_ref, f32[16,128]{1,0:T(8,128)S(1)} %get-tuple-element.57.half_ref, f32[16,128]{1,0:T(8,128)S(1)} %get-tuple-element.59.half_hat_ref, f32[16,128]{1,0:T(8,128)S(1)} %get-tuple-element.60.sum_hat_ref, ...), custom_call_target="tpu_custom_call" | custom-call | tf_op jit(solution)/shard_map/pallas_call | solution.py:324
  (3 shorter events, 0.0 us)
Async XLA Ops:
  41.7 1.3 %collective-permute-start = (f32[72,128]{1,0:T(8,128)S(1)}, f32[72,128]{1,0:T(8,128)S(1)}, u32[]{:S(2)}, u32[]{:S(2)}) collective-permute-start(f32[72,128]{1,0:T(8,128)S(1)} %get-tuple-element.51), channel_id=1, source_target_pairs={{0,1},{1,0},{2,3},{3,2},{4,5},{5,4},{6,7},{7,6},{8,9},{9,8},{10,11... | collective-permute-start | bytes 110600 | tf_op jit(solution)/shard_map/ppermute | solution.py:310
  43.0 4.0 %collective-permute-start.1 = (f32[72,128]{1,0:T(8,128)S(1)}, f32[72,128]{1,0:T(8,128)S(1)}, u32[]{:S(2)}, u32[]{:S(2)}) collective-permute-start(f32[72,128]{1,0:T(8,128)S(1)} %add.6), channel_id=1, source_target_pairs={{0,2},{2,0},{1,3},{3,1},{4,6},{6,4},{5,7},{7,5},{8,10},{10,8},{9,1... | collective-permute-start | bytes 110600 | tf_op jit(solution)/shard_map/ppermute | solution.py:310
  47.0 6.6 %collective-permute-start.4 = (f32[120,128]{1,0:T(8,128)S(1)}, f32[120,128]{1,0:T(8,128)S(1)}, u32[]{:S(2)}, u32[]{:S(2)}) collective-permute-start(f32[120,128]{1,0:T(8,128)S(1)} %pad_maximum_fusion.mine_ref), channel_id=1, source_target_pairs={{0,12},{4,8},{8,4},{12,0},{1,13},{5,9},{9,5},{13,1},{2,14},{6,10},... | collective-permute-start | bytes 184328 | tf_op jit(solution)/shard_map/ppermute | solution.py:310
  48.7 4.9 %collective-permute-start.3 = (f32[120,128]{1,0:T(8,128)S(1)}, f32[120,128]{1,0:T(8,128)S(1)}, u32[]{:S(2)}, u32[]{:S(2)}) collective-permute-start(f32[120,128]{1,0:T(8,128)S(1)} %pad_maximum_fusion.mine_ref), channel_id=1, source_target_pairs={{0,4},{4,0},{8,12},{12,8},{1,5},{5,1},{9,13},{13,9},{2,6},{6,2},{1... | collective-permute-start | bytes 184328 | tf_op jit(solution)/shard_map/ppermute | solution.py:310
  48.7 5.7 %collective-permute-start.2 = (f32[120,128]{1,0:T(8,128)S(1)}, f32[120,128]{1,0:T(8,128)S(1)}, u32[]{:S(2)}, u32[]{:S(2)}) collective-permute-start(f32[120,128]{1,0:T(8,128)S(1)} %pad_maximum_fusion.mine_ref), channel_id=1, source_target_pairs={{0,8},{4,12},{8,0},{12,4},{1,9},{5,13},{9,1},{13,5},{2,10},{6,14},... | collective-permute-start | bytes 184328 | tf_op jit(solution)/shard_map/ppermute | solution.py:310
  54.6 1.2 %collective-permute-start.5 = (f32[1,128]{1,0:T(1,128)S(1)}, f32[1,128]{1,0:T(1,128)S(1)}, u32[]{:S(2)}, u32[]{:S(2)}) collective-permute-start(f32[1,128]{1,0:T(1,128)S(1)} %get-tuple-element.61.refs_0_), channel_id=1, source_target_pairs={{0,1},{1,0},{2,3},{3,2},{4,5},{5,4},{6,7},{7,6},{8,9},{9,8},{10,11... | collective-permute-start | bytes 1544 | tf_op jit(solution)/shard_map/ppermute | solution.py:310

commit v6 on v5

--- a/solution.py
+++ b/solution.py
@@ -43,27 +43,36 @@
     return parts[0]
 
 
-def products(z, coupling_ref, diagonal_ref, partial_ref, own_ref, before=None):
+def folded(column, tile):
+    width = tile.shape[1]
+    return jnp.sum((column * tile).reshape(width // 8, 8, width), axis=0)
+
+
+def spread_products(z, spread_ref, coupling_ref, diagonal_ref, scratch, own_ref, before=None):
+    partial_ref, column_ref = scratch
     rows, slots, width = coupling_ref.shape[:3]
-    for g in range(rows // 8):
+    for first in range(0, rows, 8):
         if before is not None:
-            before(g)
-        first = g * 8
-        sums = [[] for _ in range(slots + 1)]
+            before(first // 8)
+        sums = [[] for _ in range(slots)]
         for r in range(first, first + 8):
             column = jnp.broadcast_to(z[r : r + 1], (width, width)).T
+            column_ref[r] = column
             for k in range(slots):
-                sums[k].append(jnp.sum((column * coupling_ref[r, k]).reshape(width // 8, 8, width), axis=0))
-            sums[slots].append(jnp.sum((column * diagonal_ref[r]).reshape(width // 8, 8, width), axis=0))
+                sums[k].append(folded(column, coupling_ref[r, k]))
         for k in range(slots):
             partial_ref[pl.ds(k * rows + first, 8), :] = sum_lines(sums[k])
-        own_ref[pl.ds(first, 8), :] = sum_lines(sums[slots])
-
-
-def emit(z, tail, spread_ref, coupling_ref, diagonal_ref, partial_ref, own_ref, send_ref, before=None):
+    if before is not None:
+        before(rows // 8)
+    out = jnp.dot(spread_ref[...], split3(partial_ref[...]), preferred_element_type=jnp.float32)
+    for first in range(0, rows, 8):
+        own_ref[pl.ds(first, 8), :] = sum_lines([folded(column_ref[r], diagonal_ref[r]) for r in range(first, first + 8)])
+    return out
+
+
+def emit(z, tail, spread_ref, coupling_ref, diagonal_ref, scratch, own_ref, send_ref, before=None):
     rows = z.shape[0]
-    products(z, coupling_ref, diagonal_ref, partial_ref, own_ref, before)
-    send_ref[...] = jnp.dot(spread_ref[...], split3(partial_ref[...]), preferred_element_type=jnp.float32)
+    send_ref[...] = spread_products(z, spread_ref, coupling_ref, diagonal_ref, scratch, own_ref, before)
     if callable(tail):
         tail = tail()
     for d in range(send_ref.shape[0] // (rows + 1)):
@@ -110,7 +119,7 @@
 def first_kernel(
     b_hbm, jacobi_hbm, part_hbm, tile_hbm, near_hbm, coupling_hbm, diagonal_hbm,
     send_ref, own_ref, band_ref, spread_ref, halves_ref, b_ref, coupling_ref, diagonal_ref,
-    partial_ref, jacobi_ref, part_ref, tile_ref, near_ref, small_sem, jacobi_sem, coupling_sem, diagonal_sem,
+    partial_ref, column_ref, jacobi_ref, part_ref, tile_ref, near_ref, small_sem, jacobi_sem, coupling_sem, diagonal_sem,
     *, sizes,
 ):
     n_rows, n_cols, n_sub = sizes
@@ -136,7 +145,8 @@
         copy_of(g, jacobi_hbm, jacobi_ref, jacobi_sem).start()
     for g in range(groups):
         copy_of(g, coupling_hbm, coupling_ref, coupling_sem).start()
-        copy_of(g, diagonal_hbm, diagonal_ref, diagonal_sem).start()
+    diagonal_copy = pltpu.make_async_copy(diagonal_hbm, diagonal_ref, diagonal_sem)
+    diagonal_copy.start()
     for copy in small:
         copy.wait()
     own = lax.axis_index("rows")
@@ -172,18 +182,17 @@
     z = apply_m(band_ref, b_ref[...])
 
     def before(g):
-        copy_of(g, coupling_hbm, coupling_ref, coupling_sem).wait()
-        copy_of(g, diagonal_hbm, diagonal_ref, diagonal_sem).wait()
+        (copy_of(g, coupling_hbm, coupling_ref, coupling_sem) if g < groups else diagonal_copy).wait()
 
     def tail():
         return pack([peak(b_ref[...]), jnp.maximum(peak(partial_ref[...]), peak(own_ref[...]))], width)
 
-    emit(z, tail, spread_ref, coupling_ref, diagonal_ref, partial_ref, own_ref, send_ref, before)
+    emit(z, tail, spread_ref, coupling_ref, diagonal_ref, (partial_ref, column_ref), own_ref, send_ref, before)
 
 
 def second_kernel(
     recv_ref, own_in, b_ref, band_ref, spread_ref, coupling_ref, diagonal_ref,
-    send_ref, own_ref, q_ref, scale_ref, partial_ref,
+    send_ref, own_ref, q_ref, scale_ref, partial_ref, column_ref,
 ):
     b = b_ref[...]
     rows, width = b.shape
@@ -195,7 +204,7 @@
     scale_ref[...] = jnp.broadcast_to(scale, (1, width))
     tail = pack([total(b * b), total(b * q)], width)
     z = apply_m(band_ref, scale * q)
-    emit(z, tail, spread_ref, coupling_ref, diagonal_ref, partial_ref, own_ref, send_ref)
+    emit(z, tail, spread_ref, coupling_ref, diagonal_ref, (partial_ref, column_ref), own_ref, send_ref)
 
 
 def scalars_of(recv_ref, rows, count, repeats):
@@ -205,7 +214,7 @@
 
 def third_kernel(
     recv_ref, own_in, b_ref, q_ref, scale_ref, band_ref, spread_ref, coupling_ref, diagonal_ref,
-    send_ref, own_ref, twice_ref, half_ref, u_ref, keep_ref, partial_ref, *, n_cols,
+    send_ref, own_ref, twice_ref, half_ref, u_ref, keep_ref, partial_ref, column_ref, *, n_cols,
 ):
     b, q = b_ref[...], q_ref[...]
     rows, width = b.shape
@@ -218,14 +227,14 @@
     twice_ref[...], half_ref[...], u_ref[...] = twice, half, u
     keep_ref[...] = pack([rho, alpha], width)
     z = apply_m(band_ref, alpha * twice)
-    emit(z, tail, spread_ref, coupling_ref, diagonal_ref, partial_ref, own_ref, send_ref)
+    emit(z, tail, spread_ref, coupling_ref, diagonal_ref, (partial_ref, column_ref), own_ref, send_ref)
 
 
 def fourth_kernel(
     recv_ref, own_in, b_ref, q_ref, twice_ref, half_ref, u_ref, keep_ref, band_ref, halves_ref, coupling_ref,
     diagonal_ref, *refs, n_rows, n_cols, n_sub,
 ):
-    parts, (three_ref, search_ref, done_ref, kept_ref, partial_ref, own_ref) = refs[:n_sub], refs[n_sub:]
+    parts, (three_ref, search_ref, done_ref, kept_ref, partial_ref, column_ref, own_ref) = refs[:n_sub], refs[n_sub:]
     b, q, twice, half = b_ref[...], q_ref[...], twice_ref[...], half_ref[...]
     rows, width = b.shape
     rho, alpha = keep_ref[:, 0:1], keep_ref[:, 1:2]
@@ -244,8 +253,7 @@
     first = lax.axis_index("cols") == 0
     tail = pack([jnp.where(first, total(b * image), 0.0)], width)
     z = apply_m(band_ref, alpha * image)
-    products(z, coupling_ref, diagonal_ref, partial_ref, own_ref)
-    out = jnp.dot(halves_ref[...], split3(partial_ref[...]), preferred_element_type=jnp.float32)
+    out = spread_products(z, halves_ref, coupling_ref, diagonal_ref, (partial_ref, column_ref), own_ref)
     size = parts[0].shape[0]
     for t, part_ref in enumerate(parts):
         part_ref[...] = out[t * size : (t + 1) * size]
@@ -345,14 +353,14 @@
     band_shape = ((2 * BAND + 1, rows, width), f32)
     spread_shape = ((devices * (rows + 1), 3 * slots * rows), jnp.bfloat16)
     halves_shape = ((n_sub * part_size, 3 * slots * rows), jnp.bfloat16)
-    scratch = [pltpu.VMEM((slots * rows, width), f32)]
+    scratch = [pltpu.VMEM((slots * rows, width), f32), pltpu.VMEM((rows, width, width), f32)]
 
     def exchange(send):
         send = send.reshape(devices, rows + 1, 1, width)
         return lax.all_to_all(send, PART, 0, 0, tiled=True).reshape(devices * (rows + 1), width)
 
     part, tile = column_part.T, column_tile.T
-    sems = [pltpu.SemaphoreType.DMA((n,)) for n in (4, rows // 8, rows // 8, rows // 8)]
+    sems = [pltpu.SemaphoreType.DMA((n,)) for n in (4, rows // 8, rows // 8)] + [pltpu.SemaphoreType.DMA]
     send, own, band, spread, halves, b, coupling, diagonal = call(
         functools.partial(first_kernel, sizes=sizes),
         [message, vec, band_shape, spread_shape, halves_shape, vec, (coupling.shape, f32), (diagonal.shape, f32)],

time: 56.8 us -> 56.7 us (level)
  no operation moved by 1% of the time
where the time goes in v6:
time: 56.7 us; the launch traced here: 56.4 us
  blocking collectives  35.6 us (63%)
  waiting for transfers between devices  8.51 us (15%)
  Pallas kernels  6.35 us (11%)
  starting transfers between devices  5.2 us (9%)
  between operations  0.69 us (1%)
    all_to_all x3, blocking collectives, exchange(): lax.all_to_all(send, PART, 0, 0, tiled=True)  35.6 us
    ppermute x6, waiting for transfers between devices, shifted(): lax.ppermute(x, axis, [(i, partner(i, step, count)) for i in range(count)])  8.51 us
    pallas_call x7, Pallas kernels, call(): pl.pallas_call(kernel, out_shape=[pltpu.VMEM(shape, kind) if space == plt...  6.35 us
    ppermute x6, starting transfers between devices, shifted(): lax.ppermute(x, axis, [(i, partner(i, step, count)) for i in range(count)])  5.2 us
  transfers between devices with their start and end apart: 6, of which 6 were waited for; matrix products, arithmetic and copies ran while one was open for 0% of the time, Pallas kernels for 0%

profile of v6, /device:TPU:0, one launch (start us, length us, event | category | flops | bytes accessed | tf_op | source)
XLA Modules:
  0.0 56.4 jit_solution(13685696886038542056)
XLA Ops:
  0.6 2.9 %shard_map.86 = (f32[272,128]{1,0:T(8,128)S(1)}, f32[16,128]{1,0:T(8,128)S(1)}, f32[9,16,128]{2,1,0:T(8,128)S(1)}, bf16[272,144]{1,0:T(8,128)(2,1)S(1)}, bf16[14...) custom-call(f32[16,128]{1,0:T(8,128)} %b_hbm.1, ...), custom_call_target="tpu_custom_call" | custom-call | tf_op jit(solution)/shard_map/pallas_call | solution.py:332
  3.5 14.8 %all_to_all.15 = f32[16,17,1,128]{3,2,1,0:T(1,128)S(1)} all-to-all(f32[16,17,1,128]{3,2,1,0:T(1,128)S(1)} %bitcast.12), channel_id=1, replica_groups=mesh['groups'=2,'rows'=4,'cols'=2,'sub'=2] {'rows','sub','cols'}, dimensions={0} | all-to-all | bytes 278528 | tf_op jit(solution)/shard_map/all_to_all | solution.py:360
  18.3 0.7 %shard_map.87 = (f32[272,128]{1,0:T(8,128)S(1)}, f32[16,128]{1,0:T(8,128)S(1)}, f32[16,128]{1,0:T(8,128)S(1)}, f32[1,128]{1,0:T(1,128)S(1)}) custom-call(f32[272,128]{1,0:T(8,128)S(1)} %bitcast.10, f32[16,128]{1,0:T(8,128)S(1)} %get-tuple-element.33.own_in, f32[16,128]{1,0:T(8,128)S(1)} %get-tuple-element.34.b_ref, ...), custom_call_target="tpu_custom_call" | custom-call | tf_op jit(solution)/shard_map/pallas_call | solution.py:332
  19.0 10.4 %all_to_all.16 = f32[16,17,1,128]{3,2,1,0:T(1,128)S(1)} all-to-all(f32[16,17,1,128]{3,2,1,0:T(1,128)S(1)} %bitcast.13), channel_id=1, replica_groups=mesh['groups'=2,'rows'=4,'cols'=2,'sub'=2] {'rows','sub','cols'}, dimensions={0} | all-to-all | bytes 278528 | tf_op jit(solution)/shard_map/all_to_all | solution.py:360
  29.4 0.7 %shard_map.88 = (f32[272,128]{1,0:T(8,128)S(1)}, f32[16,128]{1,0:T(8,128)S(1)}, f32[16,128]{1,0:T(8,128)S(1)}, f32[16,128]{1,0:T(8,128)S(1)}, f32[16,128]{1,0:T(8,128)S(1)}, /*index=5*/f32[1,128]{1,0:T(1,128)S(1)}) custom-call(f32[272,128]{1,0:T(8,128)S(1)} %bitcast.9, f32[16,128]{1,0:T(8,128)S(1)} %get-tuple-element.40.own_in, ...), custom_call_target="tpu_custom_call" | custom-call | tf_op jit(solution)/shard_map/pallas_call | solution.py:332
  30.2 10.4 %all_to_all.17 = f32[16,17,1,128]{3,2,1,0:T(1,128)S(1)} all-to-all(f32[16,17,1,128]{3,2,1,0:T(1,128)S(1)} %bitcast.11), channel_id=1, replica_groups=mesh['groups'=2,'rows'=4,'cols'=2,'sub'=2] {'rows','sub','cols'}, dimensions={0} | all-to-all | bytes 278528 | tf_op jit(solution)/shard_map/all_to_all | solution.py:360
  40.6 0.9 %shard_map.89 = (f32[72,128]{1,0:T(8,128)S(1)}, f32[72,128]{1,0:T(8,128)S(1)}, f32[48,128]{1,0:T(8,128)S(1)}, f32[16,128]{1,0:T(8,128)S(1)}, f32[16,128]{1,0:T(8,128)S(1)}, /*index=5*/f32[1,128]{1,0:T(1,128)S(1)}) custom-call(f32[272,128]{1,0:T(8,128)S(1)} %bitcast.8, f32[16,128]{1,0:T(8,128)S(1)} %get-tuple-element.44.own_in, ...), custom_call_target="tpu_custom_call" | custom-call | tf_op jit(solution)/shard_map/pallas_call | solution.py:332
  41.5 0.2 collective-permute-start
  41.7 1.1 %collective-permute-done = f32[72,128]{1,0:T(8,128)S(1)} collective-permute-done((f32[72,128]{1,0:T(8,128)S(1)}, f32[72,128]{1,0:T(8,128)S(1)}, u32[]{:S(2)}, u32[]{:S(2)}) %collective-permute-start) | collective-permute-done | bytes 36896 | tf_op jit(solution)/shard_map/ppermute | solution.py:318
  42.8 0.6 collective-permute-start.1
  43.4 3.4 %collective-permute-done.1 = f32[72,128]{1,0:T(8,128)S(1)} collective-permute-done((f32[72,128]{1,0:T(8,128)S(1)}, f32[72,128]{1,0:T(8,128)S(1)}, u32[]{:S(2)}, u32[]{:S(2)}) %collective-permute-start.1) | collective-permute-done | bytes 36896 | tf_op jit(solution)/shard_map/ppermute | solution.py:318
  46.8 1.7 %collective-permute-start.4 = (f32[120,128]{1,0:T(8,128)S(1)}, f32[120,128]{1,0:T(8,128)S(1)}, u32[]{:S(2)}, u32[]{:S(2)}) collective-permute-start(f32[120,128]{1,0:T(8,128)S(1)} %pad_maximum_fusion.mine_ref), channel_id=1, source_target_pairs={{0,12},{4,8},{8,4},{12,0},{1,13},{5,9},{9,5},{13,1},{2,14},{6,10},... | collective-permute-start | bytes 184328 | tf_op jit(solution)/shard_map/ppermute | solution.py:318
  48.5 0.0 collective-permute-start.3
  48.5 2.7 %collective-permute-start.2 = (f32[120,128]{1,0:T(8,128)S(1)}, f32[120,128]{1,0:T(8,128)S(1)}, u32[]{:S(2)}, u32[]{:S(2)}) collective-permute-start(f32[120,128]{1,0:T(8,128)S(1)} %pad_maximum_fusion.mine_ref), channel_id=1, source_target_pairs={{0,8},{4,12},{8,0},{12,4},{1,9},{5,13},{9,1},{13,5},{2,10},{6,14},... | collective-permute-start | bytes 184328 | tf_op jit(solution)/shard_map/ppermute | solution.py:318
  51.3 2.1 %collective-permute-done.4.refs_2_ = f32[120,128]{1,0:T(8,128)S(1)} collective-permute-done((f32[120,128]{1,0:T(8,128)S(1)}, f32[120,128]{1,0:T(8,128)S(1)}, u32[]{:S(2)}, u32[]{:S(2)}) %collective-permute-start.4) | collective-permute-done | bytes 61472 | tf_op jit(solution)/shard_map/ppermute | solution.py:318
  53.4 0.1 collective-permute-done.3.refs_1_
  53.5 0.7 %collective-permute-done.2.refs_0_ = f32[120,128]{1,0:T(8,128)S(1)} collective-permute-done((f32[120,128]{1,0:T(8,128)S(1)}, f32[120,128]{1,0:T(8,128)S(1)}, u32[]{:S(2)}, u32[]{:S(2)}) %collective-permute-start.2) | collective-permute-done | bytes 61472 | tf_op jit(solution)/shard_map/ppermute | solution.py:318
  54.2 0.2 shard_map.90
  54.5 0.0 collective-permute-start.5
  54.5 0.1 shard_map.91
  54.6 1.0 %collective-permute-done.5.refs_1_ = f32[1,128]{1,0:T(1,128)S(1)} collective-permute-done((f32[1,128]{1,0:T(1,128)S(1)}, f32[1,128]{1,0:T(1,128)S(1)}, u32[]{:S(2)}, u32[]{:S(2)}) %collective-permute-start.5) | collective-permute-done | bytes 544 | tf_op jit(solution)/shard_map/ppermute | solution.py:318
  55.6 0.8 %shard_map.92 = (f32[16,128]{1,0:T(8,128)}, f32[16,128]{1,0:T(8,128)}) custom-call(f32[16,128]{1,0:T(8,128)S(1)} %get-tuple-element.56.twice_ref, f32[16,128]{1,0:T(8,128)S(1)} %get-tuple-element.57.half_ref, f32[16,128]{1,0:T(8,128)S(1)} %get-tuple-element.59.half_hat_ref, f32[16,128]{1,0:T(8,128)S(1)} %get-tuple-element.60.sum_hat_ref, ...), custom_call_target="tpu_custom_call" | custom-call | tf_op jit(solution)/shard_map/pallas_call | solution.py:332
  (3 shorter events, 0.0 us)
Async XLA Ops:
  41.5 1.3 %collective-permute-start = (f32[72,128]{1,0:T(8,128)S(1)}, f32[72,128]{1,0:T(8,128)S(1)}, u32[]{:S(2)}, u32[]{:S(2)}) collective-permute-start(f32[72,128]{1,0:T(8,128)S(1)} %get-tuple-element.51), channel_id=1, source_target_pairs={{0,1},{1,0},{2,3},{3,2},{4,5},{5,4},{6,7},{7,6},{8,9},{9,8},{10,11... | collective-permute-start | bytes 110600 | tf_op jit(solution)/shard_map/ppermute | solution.py:318
  42.8 4.0 %collective-permute-start.1 = (f32[72,128]{1,0:T(8,128)S(1)}, f32[72,128]{1,0:T(8,128)S(1)}, u32[]{:S(2)}, u32[]{:S(2)}) collective-permute-start(f32[72,128]{1,0:T(8,128)S(1)} %add.6), channel_id=1, source_target_pairs={{0,2},{2,0},{1,3},{3,1},{4,6},{6,4},{5,7},{7,5},{8,10},{10,8},{9,1... | collective-permute-start | bytes 110600 | tf_op jit(solution)/shard_map/ppermute | solution.py:318
  46.8 6.6 %collective-permute-start.4 = (f32[120,128]{1,0:T(8,128)S(1)}, f32[120,128]{1,0:T(8,128)S(1)}, u32[]{:S(2)}, u32[]{:S(2)}) collective-permute-start(f32[120,128]{1,0:T(8,128)S(1)} %pad_maximum_fusion.mine_ref), channel_id=1, source_target_pairs={{0,12},{4,8},{8,4},{12,0},{1,13},{5,9},{9,5},{13,1},{2,14},{6,10},... | collective-permute-start | bytes 184328 | tf_op jit(solution)/shard_map/ppermute | solution.py:318
  48.5 4.9 %collective-permute-start.3 = (f32[120,128]{1,0:T(8,128)S(1)}, f32[120,128]{1,0:T(8,128)S(1)}, u32[]{:S(2)}, u32[]{:S(2)}) collective-permute-start(f32[120,128]{1,0:T(8,128)S(1)} %pad_maximum_fusion.mine_ref), channel_id=1, source_target_pairs={{0,4},{4,0},{8,12},{12,8},{1,5},{5,1},{9,13},{13,9},{2,6},{6,2},{1... | collective-permute-start | bytes 184328 | tf_op jit(solution)/shard_map/ppermute | solution.py:318
  48.5 5.7 %collective-permute-start.2 = (f32[120,128]{1,0:T(8,128)S(1)}, f32[120,128]{1,0:T(8,128)S(1)}, u32[]{:S(2)}, u32[]{:S(2)}) collective-permute-start(f32[120,128]{1,0:T(8,128)S(1)} %pad_maximum_fusion.mine_ref), channel_id=1, source_target_pairs={{0,8},{4,12},{8,0},{12,4},{1,9},{5,13},{9,1},{13,5},{2,10},{6,14},... | collective-permute-start | bytes 184328 | tf_op jit(solution)/shard_map/ppermute | solution.py:318
  54.5 1.2 %collective-permute-start.5 = (f32[1,128]{1,0:T(1,128)S(1)}, f32[1,128]{1,0:T(1,128)S(1)}, u32[]{:S(2)}, u32[]{:S(2)}) collective-permute-start(f32[1,128]{1,0:T(1,128)S(1)} %get-tuple-element.61.refs_0_), channel_id=1, source_target_pairs={{0,1},{1,0},{2,3},{3,2},{4,5},{5,4},{6,7},{7,6},{8,9},{9,8},{10,11... | collective-permute-start | bytes 1544 | tf_op jit(solution)/shard_map/ppermute | solution.py:318

commit v7 on v6

--- a/solution.py
+++ b/solution.py
@@ -225,8 +225,9 @@
     half = b - alpha * q
     tail = pack([total(twice * half), total(twice * twice), total(b * half), total(b * twice)], width)
     twice_ref[...], half_ref[...], u_ref[...] = twice, half, u
-    keep_ref[...] = pack([rho, alpha], width)
-    z = apply_m(band_ref, alpha * twice)
+    scale = scale_ref[:, 0:1]
+    keep_ref[...] = pack([rho, alpha, scale], width)
+    z = apply_m(band_ref, scale * twice)
     emit(z, tail, spread_ref, coupling_ref, diagonal_ref, (partial_ref, column_ref), own_ref, send_ref)
 
 
@@ -237,22 +238,22 @@
     parts, (three_ref, search_ref, done_ref, kept_ref, partial_ref, column_ref, own_ref) = refs[:n_sub], refs[n_sub:]
     b, q, twice, half = b_ref[...], q_ref[...], twice_ref[...], half_ref[...]
     rows, width = b.shape
-    rho, alpha = keep_ref[:, 0:1], keep_ref[:, 1:2]
+    rho, alpha, scale = (keep_ref[:, n : n + 1] for n in range(3))
     cross, square, b_half, b_twice = scalars_of(recv_ref, rows, 4, n_cols)
     omega = cross / square
     rho_next = b_half - omega * b_twice
     ratio = rho_next / rho
     beta = ratio * (alpha / omega)
-    a = twice - (omega / alpha) * chunks_of(recv_ref, own_in)
+    a = twice - (omega / scale) * chunks_of(recv_ref, own_in)
     residual = half - omega * twice
     image = a + beta * q - ratio * u_ref[...]
     three_ref[...] = jnp.concatenate([a, residual, image], axis=0)
     search_ref[...] = residual + beta * (b - omega * q)
     done_ref[...] = alpha * b + omega * half
-    kept_ref[...] = pack([rho_next, alpha], width)
+    kept_ref[...] = pack([rho_next, scale], width)
     first = lax.axis_index("cols") == 0
     tail = pack([jnp.where(first, total(b * image), 0.0)], width)
-    z = apply_m(band_ref, alpha * image)
+    z = apply_m(band_ref, scale * image)
     out = spread_products(z, halves_ref, coupling_ref, diagonal_ref, (partial_ref, column_ref), own_ref)
     size = parts[0].shape[0]
     for t, part_ref in enumerate(parts):
@@ -391,7 +392,7 @@
     summed = sum_over(summed, "cols")
     mine = jnp.concatenate([summed, three])
     others = [shifted(mine, "rows", step) for step in range(1, n_rows)]
-    order = [1, 0, *range(2, n_rows - 1)]
+    order = sorted(range(n_rows - 1), key=lambda n: (n > 1, -n if n < 2 else n))
     twice, half, total_search, dots = call(
         functools.partial(fifth_kernel, order=order, n_rows=n_rows), [vec] * 3 + [line],
         (mine, *(others[n] for n in order), kept, search, done), [pltpu.VMEM((part_size, width), f32)],

time: 56.7 us -> 56.7 us (level)
  no operation moved by 1% of the time
where the time goes in v7:
time: 56.7 us; the launch traced here: 56.4 us
  blocking collectives  35.6 us (63%)
  waiting for transfers between devices  8.51 us (15%)
  Pallas kernels  6.36 us (11%)
  starting transfers between devices  5.2 us (9%)
  between operations  0.69 us (1%)
    all_to_all x3, blocking collectives, exchange(): lax.all_to_all(send, PART, 0, 0, tiled=True)  35.6 us
    ppermute x6, waiting for transfers between devices, shifted(): lax.ppermute(x, axis, [(i, partner(i, step, count)) for i in range(count)])  8.51 us
    pallas_call x7, Pallas kernels, call(): pl.pallas_call(kernel, out_shape=[pltpu.VMEM(shape, kind) if space == plt...  6.36 us
    ppermute x6, starting transfers between devices, shifted(): lax.ppermute(x, axis, [(i, partner(i, step, count)) for i in range(count)])  5.2 us
  transfers between devices with their start and end apart: 6, of which 6 were waited for; matrix products, arithmetic and copies ran while one was open for 0% of the time, Pallas kernels for 0%

profile of v7, /device:TPU:0, one launch (start us, length us, event | category | flops | bytes accessed | tf_op | source)
XLA Modules:
  0.0 56.4 jit_solution(4017028061537032917)
XLA Ops:
  0.6 2.9 %shard_map.86 = (f32[272,128]{1,0:T(8,128)S(1)}, f32[16,128]{1,0:T(8,128)S(1)}, f32[9,16,128]{2,1,0:T(8,128)S(1)}, bf16[272,144]{1,0:T(8,128)(2,1)S(1)}, bf16[14...) custom-call(f32[16,128]{1,0:T(8,128)} %b_hbm.1, ...), custom_call_target="tpu_custom_call" | custom-call | tf_op jit(solution)/shard_map/pallas_call | solution.py:333
  3.5 14.8 %all_to_all.15 = f32[16,17,1,128]{3,2,1,0:T(1,128)S(1)} all-to-all(f32[16,17,1,128]{3,2,1,0:T(1,128)S(1)} %bitcast.12), channel_id=1, replica_groups=mesh['groups'=2,'rows'=4,'cols'=2,'sub'=2] {'rows','sub','cols'}, dimensions={0} | all-to-all | bytes 278528 | tf_op jit(solution)/shard_map/all_to_all | solution.py:361
  18.3 0.7 %shard_map.87 = (f32[272,128]{1,0:T(8,128)S(1)}, f32[16,128]{1,0:T(8,128)S(1)}, f32[16,128]{1,0:T(8,128)S(1)}, f32[1,128]{1,0:T(1,128)S(1)}) custom-call(f32[272,128]{1,0:T(8,128)S(1)} %bitcast.10, f32[16,128]{1,0:T(8,128)S(1)} %get-tuple-element.33.own_in, f32[16,128]{1,0:T(8,128)S(1)} %get-tuple-element.34.b_ref, ...), custom_call_target="tpu_custom_call" | custom-call | tf_op jit(solution)/shard_map/pallas_call | solution.py:333
  19.0 10.4 %all_to_all.16 = f32[16,17,1,128]{3,2,1,0:T(1,128)S(1)} all-to-all(f32[16,17,1,128]{3,2,1,0:T(1,128)S(1)} %bitcast.13), channel_id=1, replica_groups=mesh['groups'=2,'rows'=4,'cols'=2,'sub'=2] {'rows','sub','cols'}, dimensions={0} | all-to-all | bytes 278528 | tf_op jit(solution)/shard_map/all_to_all | solution.py:361
  29.4 0.7 %shard_map.88 = (f32[272,128]{1,0:T(8,128)S(1)}, f32[16,128]{1,0:T(8,128)S(1)}, f32[16,128]{1,0:T(8,128)S(1)}, f32[16,128]{1,0:T(8,128)S(1)}, f32[16,128]{1,0:T(8,128)S(1)}, /*index=5*/f32[1,128]{1,0:T(1,128)S(1)}) custom-call(f32[272,128]{1,0:T(8,128)S(1)} %bitcast.9, f32[16,128]{1,0:T(8,128)S(1)} %get-tuple-element.40.own_in, ...), custom_call_target="tpu_custom_call" | custom-call | tf_op jit(solution)/shard_map/pallas_call | solution.py:333
  30.2 10.4 %all_to_all.17 = f32[16,17,1,128]{3,2,1,0:T(1,128)S(1)} all-to-all(f32[16,17,1,128]{3,2,1,0:T(1,128)S(1)} %bitcast.11), channel_id=1, replica_groups=mesh['groups'=2,'rows'=4,'cols'=2,'sub'=2] {'rows','sub','cols'}, dimensions={0} | all-to-all | bytes 278528 | tf_op jit(solution)/shard_map/all_to_all | solution.py:361
  40.6 0.9 %shard_map.89 = (f32[72,128]{1,0:T(8,128)S(1)}, f32[72,128]{1,0:T(8,128)S(1)}, f32[48,128]{1,0:T(8,128)S(1)}, f32[16,128]{1,0:T(8,128)S(1)}, f32[16,128]{1,0:T(8,128)S(1)}, /*index=5*/f32[1,128]{1,0:T(1,128)S(1)}) custom-call(f32[272,128]{1,0:T(8,128)S(1)} %bitcast.8, f32[16,128]{1,0:T(8,128)S(1)} %get-tuple-element.44.own_in, ...), custom_call_target="tpu_custom_call" | custom-call | tf_op jit(solution)/shard_map/pallas_call | solution.py:333
  41.6 0.2 collective-permute-start
  41.7 1.1 %collective-permute-done = f32[72,128]{1,0:T(8,128)S(1)} collective-permute-done((f32[72,128]{1,0:T(8,128)S(1)}, f32[72,128]{1,0:T(8,128)S(1)}, u32[]{:S(2)}, u32[]{:S(2)}) %collective-permute-start) | collective-permute-done | bytes 36896 | tf_op jit(solution)/shard_map/ppermute | solution.py:319
  42.8 0.6 collective-permute-start.1
  43.4 3.4 %collective-permute-done.1 = f32[72,128]{1,0:T(8,128)S(1)} collective-permute-done((f32[72,128]{1,0:T(8,128)S(1)}, f32[72,128]{1,0:T(8,128)S(1)}, u32[]{:S(2)}, u32[]{:S(2)}) %collective-permute-start.1) | collective-permute-done | bytes 36896 | tf_op jit(solution)/shard_map/ppermute | solution.py:319
  46.8 1.7 %collective-permute-start.4 = (f32[120,128]{1,0:T(8,128)S(1)}, f32[120,128]{1,0:T(8,128)S(1)}, u32[]{:S(2)}, u32[]{:S(2)}) collective-permute-start(f32[120,128]{1,0:T(8,128)S(1)} %pad_maximum_fusion.mine_ref), channel_id=1, source_target_pairs={{0,12},{4,8},{8,4},{12,0},{1,13},{5,9},{9,5},{13,1},{2,14},{6,10},... | collective-permute-start | bytes 184328 | tf_op jit(solution)/shard_map/ppermute | solution.py:319
  48.6 0.0 collective-permute-start.3
  48.6 2.7 %collective-permute-start.2 = (f32[120,128]{1,0:T(8,128)S(1)}, f32[120,128]{1,0:T(8,128)S(1)}, u32[]{:S(2)}, u32[]{:S(2)}) collective-permute-start(f32[120,128]{1,0:T(8,128)S(1)} %pad_maximum_fusion.mine_ref), channel_id=1, source_target_pairs={{0,8},{4,12},{8,0},{12,4},{1,9},{5,13},{9,1},{13,5},{2,10},{6,14},... | collective-permute-start | bytes 184328 | tf_op jit(solution)/shard_map/ppermute | solution.py:319
  51.3 2.1 %collective-permute-done.4.refs_2_ = f32[120,128]{1,0:T(8,128)S(1)} collective-permute-done((f32[120,128]{1,0:T(8,128)S(1)}, f32[120,128]{1,0:T(8,128)S(1)}, u32[]{:S(2)}, u32[]{:S(2)}) %collective-permute-start.4) | collective-permute-done | bytes 61472 | tf_op jit(solution)/shard_map/ppermute | solution.py:319
  53.4 0.1 collective-permute-done.3.refs_1_
  53.5 0.7 %collective-permute-done.2.refs_0_ = f32[120,128]{1,0:T(8,128)S(1)} collective-permute-done((f32[120,128]{1,0:T(8,128)S(1)}, f32[120,128]{1,0:T(8,128)S(1)}, u32[]{:S(2)}, u32[]{:S(2)}) %collective-permute-start.2) | collective-permute-done | bytes 61472 | tf_op jit(solution)/shard_map/ppermute | solution.py:319
  54.2 0.2 shard_map.90
  54.5 0.0 collective-permute-start.5
  54.5 0.1 shard_map.91
  54.6 1.0 %collective-permute-done.5.refs_1_ = f32[1,128]{1,0:T(1,128)S(1)} collective-permute-done((f32[1,128]{1,0:T(1,128)S(1)}, f32[1,128]{1,0:T(1,128)S(1)}, u32[]{:S(2)}, u32[]{:S(2)}) %collective-permute-start.5) | collective-permute-done | bytes 544 | tf_op jit(solution)/shard_map/ppermute | solution.py:319
  55.6 0.8 %shard_map.92 = (f32[16,128]{1,0:T(8,128)}, f32[16,128]{1,0:T(8,128)}) custom-call(f32[16,128]{1,0:T(8,128)S(1)} %get-tuple-element.56.twice_ref, f32[16,128]{1,0:T(8,128)S(1)} %get-tuple-element.57.half_ref, f32[16,128]{1,0:T(8,128)S(1)} %get-tuple-element.59.half_hat_ref, f32[16,128]{1,0:T(8,128)S(1)} %get-tuple-element.60.sum_hat_ref, ...), custom_call_target="tpu_custom_call" | custom-call | tf_op jit(solution)/shard_map/pallas_call | solution.py:333
  (3 shorter events, 0.0 us)
Async XLA Ops:
  41.6 1.3 %collective-permute-start = (f32[72,128]{1,0:T(8,128)S(1)}, f32[72,128]{1,0:T(8,128)S(1)}, u32[]{:S(2)}, u32[]{:S(2)}) collective-permute-start(f32[72,128]{1,0:T(8,128)S(1)} %get-tuple-element.51), channel_id=1, source_target_pairs={{0,1},{1,0},{2,3},{3,2},{4,5},{5,4},{6,7},{7,6},{8,9},{9,8},{10,11... | collective-permute-start | bytes 110600 | tf_op jit(solution)/shard_map/ppermute | solution.py:319
  42.8 4.0 %collective-permute-start.1 = (f32[72,128]{1,0:T(8,128)S(1)}, f32[72,128]{1,0:T(8,128)S(1)}, u32[]{:S(2)}, u32[]{:S(2)}) collective-permute-start(f32[72,128]{1,0:T(8,128)S(1)} %add.6), channel_id=1, source_target_pairs={{0,2},{2,0},{1,3},{3,1},{4,6},{6,4},{5,7},{7,5},{8,10},{10,8},{9,1... | collective-permute-start | bytes 110600 | tf_op jit(solution)/shard_map/ppermute | solution.py:319
  46.8 6.6 %collective-permute-start.4 = (f32[120,128]{1,0:T(8,128)S(1)}, f32[120,128]{1,0:T(8,128)S(1)}, u32[]{:S(2)}, u32[]{:S(2)}) collective-permute-start(f32[120,128]{1,0:T(8,128)S(1)} %pad_maximum_fusion.mine_ref), channel_id=1, source_target_pairs={{0,12},{4,8},{8,4},{12,0},{1,13},{5,9},{9,5},{13,1},{2,14},{6,10},... | collective-permute-start | bytes 184328 | tf_op jit(solution)/shard_map/ppermute | solution.py:319
  48.6 4.9 %collective-permute-start.3 = (f32[120,128]{1,0:T(8,128)S(1)}, f32[120,128]{1,0:T(8,128)S(1)}, u32[]{:S(2)}, u32[]{:S(2)}) collective-permute-start(f32[120,128]{1,0:T(8,128)S(1)} %pad_maximum_fusion.mine_ref), channel_id=1, source_target_pairs={{0,4},{4,0},{8,12},{12,8},{1,5},{5,1},{9,13},{13,9},{2,6},{6,2},{1... | collective-permute-start | bytes 184328 | tf_op jit(solution)/shard_map/ppermute | solution.py:319
  48.6 5.7 %collective-permute-start.2 = (f32[120,128]{1,0:T(8,128)S(1)}, f32[120,128]{1,0:T(8,128)S(1)}, u32[]{:S(2)}, u32[]{:S(2)}) collective-permute-start(f32[120,128]{1,0:T(8,128)S(1)} %pad_maximum_fusion.mine_ref), channel_id=1, source_target_pairs={{0,8},{4,12},{8,0},{12,4},{1,9},{5,13},{9,1},{13,5},{2,10},{6,14},... | collective-permute-start | bytes 184328 | tf_op jit(solution)/shard_map/ppermute | solution.py:319
  54.5 1.2 %collective-permute-start.5 = (f32[1,128]{1,0:T(1,128)S(1)}, f32[1,128]{1,0:T(1,128)S(1)}, u32[]{:S(2)}, u32[]{:S(2)}) collective-permute-start(f32[1,128]{1,0:T(1,128)S(1)} %get-tuple-element.61.refs_0_), channel_id=1, source_target_pairs={{0,1},{1,0},{2,3},{3,2},{4,5},{5,4},{6,7},{7,6},{8,9},{9,8},{10,11... | collective-permute-start | bytes 1544 | tf_op jit(solution)/shard_map/ppermute | solution.py:319

commit v8 on v7

--- a/solution.py
+++ b/solution.py
@@ -198,10 +198,11 @@
     rows, width = b.shape
     top = pairwise(jnp.maximum, tails_of(recv_ref, rows))
     size, reach = top[:, 0:1], top[:, 1:2]
-    scale = jnp.where((size > 0) & (reach > 0), size / reach, 1.0)
+    good = (size > 0) & (reach > 0)
+    scale, back = jnp.where(good, size / reach, 1.0), jnp.where(good, reach / size, 1.0)
     q = chunks_of(recv_ref, own_in)
     q_ref[...] = q
-    scale_ref[...] = jnp.broadcast_to(scale, (1, width))
+    scale_ref[...] = pack([scale, back], width)
     tail = pack([total(b * b), total(b * q)], width)
     z = apply_m(band_ref, scale * q)
     emit(z, tail, spread_ref, coupling_ref, diagonal_ref, (partial_ref, column_ref), own_ref, send_ref)
@@ -220,13 +221,13 @@
     rows, width = b.shape
     rho, cross = scalars_of(recv_ref, rows, 2, n_cols)
     alpha = rho / cross
-    u = (alpha / scale_ref[:, 0:1]) * chunks_of(recv_ref, own_in)
+    scale, back = scale_ref[:, 0:1], scale_ref[:, 1:2]
+    u = (alpha * back) * chunks_of(recv_ref, own_in)
     twice = q - u
     half = b - alpha * q
     tail = pack([total(twice * half), total(twice * twice), total(b * half), total(b * twice)], width)
     twice_ref[...], half_ref[...], u_ref[...] = twice, half, u
-    scale = scale_ref[:, 0:1]
-    keep_ref[...] = pack([rho, alpha, scale], width)
+    keep_ref[...] = pack([rho, alpha, scale, back], width)
     z = apply_m(band_ref, scale * twice)
     emit(z, tail, spread_ref, coupling_ref, diagonal_ref, (partial_ref, column_ref), own_ref, send_ref)
 
@@ -238,19 +239,19 @@
     parts, (three_ref, search_ref, done_ref, kept_ref, partial_ref, column_ref, own_ref) = refs[:n_sub], refs[n_sub:]
     b, q, twice, half = b_ref[...], q_ref[...], twice_ref[...], half_ref[...]
     rows, width = b.shape
-    rho, alpha, scale = (keep_ref[:, n : n + 1] for n in range(3))
+    rho, alpha, scale, back = (keep_ref[:, n : n + 1] for n in range(4))
     cross, square, b_half, b_twice = scalars_of(recv_ref, rows, 4, n_cols)
     omega = cross / square
     rho_next = b_half - omega * b_twice
     ratio = rho_next / rho
     beta = ratio * (alpha / omega)
-    a = twice - (omega / scale) * chunks_of(recv_ref, own_in)
+    a = twice - (omega * back) * chunks_of(recv_ref, own_in)
     residual = half - omega * twice
     image = a + beta * q - ratio * u_ref[...]
     three_ref[...] = jnp.concatenate([a, residual, image], axis=0)
     search_ref[...] = residual + beta * (b - omega * q)
     done_ref[...] = alpha * b + omega * half
-    kept_ref[...] = pack([rho_next, scale], width)
+    kept_ref[...] = pack([rho_next, back], width)
     first = lax.axis_index("cols") == 0
     tail = pack([jnp.where(first, total(b * image), 0.0)], width)
     z = apply_m(band_ref, scale * image)
@@ -276,7 +277,7 @@
     full_ref[...] = full
     tail = full[n_rows * rows : n_rows * rows + 1]
     alpha = kept_ref[:, 0:1] / tail[:, 0:1]
-    factor = alpha / kept_ref[:, 1:2]
+    factor = alpha * kept_ref[:, 1:2]
     own = lax.axis_index("rows")
     cross = square = None
     for step, source in [(0, mine_ref)] + [(n + 1, other) for n, other in zip(order, others)]:

time: 56.7 us -> 56.7 us (level)
  no operation moved by 1% of the time
where the time goes in v8:
time: 56.7 us; the launch traced here: 56.4 us
  blocking collectives  35.6 us (63%)
  waiting for transfers between devices  8.51 us (15%)
  Pallas kernels  6.36 us (11%)
  starting transfers between devices  5.19 us (9%)
  between operations  0.69 us (1%)
    all_to_all x3, blocking collectives, exchange(): lax.all_to_all(send, PART, 0, 0, tiled=True)  35.6 us
    ppermute x6, waiting for transfers between devices, shifted(): lax.ppermute(x, axis, [(i, partner(i, step, count)) for i in range(count)])  8.51 us
    pallas_call x7, Pallas kernels, call(): pl.pallas_call(kernel, out_shape=[pltpu.VMEM(shape, kind) if space == plt...  6.36 us
    ppermute x6, starting transfers between devices, shifted(): lax.ppermute(x, axis, [(i, partner(i, step, count)) for i in range(count)])  5.19 us
  transfers between devices with their start and end apart: 6, of which 6 were waited for; matrix products, arithmetic and copies ran while one was open for 0% of the time, Pallas kernels for 0%

profile of v8, /device:TPU:0, one launch (start us, length us, event | category | flops | bytes accessed | tf_op | source)
XLA Modules:
  0.0 56.4 jit_solution(1677268372957722438)
XLA Ops:
  0.6 2.9 %shard_map.86 = (f32[272,128]{1,0:T(8,128)S(1)}, f32[16,128]{1,0:T(8,128)S(1)}, f32[9,16,128]{2,1,0:T(8,128)S(1)}, bf16[272,144]{1,0:T(8,128)(2,1)S(1)}, bf16[14...) custom-call(f32[16,128]{1,0:T(8,128)} %b_hbm.1, ...), custom_call_target="tpu_custom_call" | custom-call | tf_op jit(solution)/shard_map/pallas_call | solution.py:334
  3.5 14.8 %all_to_all.15 = f32[16,17,1,128]{3,2,1,0:T(1,128)S(1)} all-to-all(f32[16,17,1,128]{3,2,1,0:T(1,128)S(1)} %bitcast.12), channel_id=1, replica_groups=mesh['groups'=2,'rows'=4,'cols'=2,'sub'=2] {'rows','sub','cols'}, dimensions={0} | all-to-all | bytes 278528 | tf_op jit(solution)/shard_map/all_to_all | solution.py:362
  18.3 0.7 %shard_map.87 = (f32[272,128]{1,0:T(8,128)S(1)}, f32[16,128]{1,0:T(8,128)S(1)}, f32[16,128]{1,0:T(8,128)S(1)}, f32[1,128]{1,0:T(1,128)S(1)}) custom-call(f32[272,128]{1,0:T(8,128)S(1)} %bitcast.10, f32[16,128]{1,0:T(8,128)S(1)} %get-tuple-element.33.own_in, f32[16,128]{1,0:T(8,128)S(1)} %get-tuple-element.34.b_ref, ...), custom_call_target="tpu_custom_call" | custom-call | tf_op jit(solution)/shard_map/pallas_call | solution.py:334
  19.0 10.4 %all_to_all.16 = f32[16,17,1,128]{3,2,1,0:T(1,128)S(1)} all-to-all(f32[16,17,1,128]{3,2,1,0:T(1,128)S(1)} %bitcast.13), channel_id=1, replica_groups=mesh['groups'=2,'rows'=4,'cols'=2,'sub'=2] {'rows','sub','cols'}, dimensions={0} | all-to-all | bytes 278528 | tf_op jit(solution)/shard_map/all_to_all | solution.py:362
  29.4 0.7 %shard_map.88 = (f32[272,128]{1,0:T(8,128)S(1)}, f32[16,128]{1,0:T(8,128)S(1)}, f32[16,128]{1,0:T(8,128)S(1)}, f32[16,128]{1,0:T(8,128)S(1)}, f32[16,128]{1,0:T(8,128)S(1)}, /*index=5*/f32[1,128]{1,0:T(1,128)S(1)}) custom-call(f32[272,128]{1,0:T(8,128)S(1)} %bitcast.9, f32[16,128]{1,0:T(8,128)S(1)} %get-tuple-element.40.own_in, ...), custom_call_target="tpu_custom_call" | custom-call | tf_op jit(solution)/shard_map/pallas_call | solution.py:334
  30.2 10.4 %all_to_all.17 = f32[16,17,1,128]{3,2,1,0:T(1,128)S(1)} all-to-all(f32[16,17,1,128]{3,2,1,0:T(1,128)S(1)} %bitcast.11), channel_id=1, replica_groups=mesh['groups'=2,'rows'=4,'cols'=2,'sub'=2] {'rows','sub','cols'}, dimensions={0} | all-to-all | bytes 278528 | tf_op jit(solution)/shard_map/all_to_all | solution.py:362
  40.6 0.9 %shard_map.89 = (f32[72,128]{1,0:T(8,128)S(1)}, f32[72,128]{1,0:T(8,128)S(1)}, f32[48,128]{1,0:T(8,128)S(1)}, f32[16,128]{1,0:T(8,128)S(1)}, f32[16,128]{1,0:T(8,128)S(1)}, /*index=5*/f32[1,128]{1,0:T(1,128)S(1)}) custom-call(f32[272,128]{1,0:T(8,128)S(1)} %bitcast.8, f32[16,128]{1,0:T(8,128)S(1)} %get-tuple-element.44.own_in, ...), custom_call_target="tpu_custom_call" | custom-call | tf_op jit(solution)/shard_map/pallas_call | solution.py:334
  41.6 0.2 collective-permute-start
  41.7 1.1 %collective-permute-done = f32[72,128]{1,0:T(8,128)S(1)} collective-permute-done((f32[72,128]{1,0:T(8,128)S(1)}, f32[72,128]{1,0:T(8,128)S(1)}, u32[]{:S(2)}, u32[]{:S(2)}) %collective-permute-start) | collective-permute-done | bytes 36896 | tf_op jit(solution)/shard_map/ppermute | solution.py:320
  42.8 0.6 collective-permute-start.1
  43.4 3.4 %collective-permute-done.1 = f32[72,128]{1,0:T(8,128)S(1)} collective-permute-done((f32[72,128]{1,0:T(8,128)S(1)}, f32[72,128]{1,0:T(8,128)S(1)}, u32[]{:S(2)}, u32[]{:S(2)}) %collective-permute-start.1) | collective-permute-done | bytes 36896 | tf_op jit(solution)/shard_map/ppermute | solution.py:320
  46.8 1.7 %collective-permute-start.4 = (f32[120,128]{1,0:T(8,128)S(1)}, f32[120,128]{1,0:T(8,128)S(1)}, u32[]{:S(2)}, u32[]{:S(2)}) collective-permute-start(f32[120,128]{1,0:T(8,128)S(1)} %pad_maximum_fusion.mine_ref), channel_id=1, source_target_pairs={{0,12},{4,8},{8,4},{12,0},{1,13},{5,9},{9,5},{13,1},{2,14},{6,10},... | collective-permute-start | bytes 184328 | tf_op jit(solution)/shard_map/ppermute | solution.py:320
  48.6 0.0 collective-permute-start.3
  48.6 2.7 %collective-permute-start.2 = (f32[120,128]{1,0:T(8,128)S(1)}, f32[120,128]{1,0:T(8,128)S(1)}, u32[]{:S(2)}, u32[]{:S(2)}) collective-permute-start(f32[120,128]{1,0:T(8,128)S(1)} %pad_maximum_fusion.mine_ref), channel_id=1, source_target_pairs={{0,8},{4,12},{8,0},{12,4},{1,9},{5,13},{9,1},{13,5},{2,10},{6,14},... | collective-permute-start | bytes 184328 | tf_op jit(solution)/shard_map/ppermute | solution.py:320
  51.3 2.1 %collective-permute-done.4.refs_2_ = f32[120,128]{1,0:T(8,128)S(1)} collective-permute-done((f32[120,128]{1,0:T(8,128)S(1)}, f32[120,128]{1,0:T(8,128)S(1)}, u32[]{:S(2)}, u32[]{:S(2)}) %collective-permute-start.4) | collective-permute-done | bytes 61472 | tf_op jit(solution)/shard_map/ppermute | solution.py:320
  53.4 0.1 collective-permute-done.3.refs_1_
  53.5 0.7 %collective-permute-done.2.refs_0_ = f32[120,128]{1,0:T(8,128)S(1)} collective-permute-done((f32[120,128]{1,0:T(8,128)S(1)}, f32[120,128]{1,0:T(8,128)S(1)}, u32[]{:S(2)}, u32[]{:S(2)}) %collective-permute-start.2) | collective-permute-done | bytes 61472 | tf_op jit(solution)/shard_map/ppermute | solution.py:320
  54.2 0.2 shard_map.90
  54.5 0.0 collective-permute-start.5
  54.5 0.1 shard_map.91
  54.6 1.0 %collective-permute-done.5.refs_1_ = f32[1,128]{1,0:T(1,128)S(1)} collective-permute-done((f32[1,128]{1,0:T(1,128)S(1)}, f32[1,128]{1,0:T(1,128)S(1)}, u32[]{:S(2)}, u32[]{:S(2)}) %collective-permute-start.5) | collective-permute-done | bytes 544 | tf_op jit(solution)/shard_map/ppermute | solution.py:320
  55.6 0.8 %shard_map.92 = (f32[16,128]{1,0:T(8,128)}, f32[16,128]{1,0:T(8,128)}) custom-call(f32[16,128]{1,0:T(8,128)S(1)} %get-tuple-element.56.twice_ref, f32[16,128]{1,0:T(8,128)S(1)} %get-tuple-element.57.half_ref, f32[16,128]{1,0:T(8,128)S(1)} %get-tuple-element.59.half_hat_ref, f32[16,128]{1,0:T(8,128)S(1)} %get-tuple-element.60.sum_hat_ref, ...), custom_call_target="tpu_custom_call" | custom-call | tf_op jit(solution)/shard_map/pallas_call | solution.py:334
  (3 shorter events, 0.0 us)
Async XLA Ops:
  41.6 1.3 %collective-permute-start = (f32[72,128]{1,0:T(8,128)S(1)}, f32[72,128]{1,0:T(8,128)S(1)}, u32[]{:S(2)}, u32[]{:S(2)}) collective-permute-start(f32[72,128]{1,0:T(8,128)S(1)} %get-tuple-element.51), channel_id=1, source_target_pairs={{0,1},{1,0},{2,3},{3,2},{4,5},{5,4},{6,7},{7,6},{8,9},{9,8},{10,11... | collective-permute-start | bytes 110600 | tf_op jit(solution)/shard_map/ppermute | solution.py:320
  42.8 4.0 %collective-permute-start.1 = (f32[72,128]{1,0:T(8,128)S(1)}, f32[72,128]{1,0:T(8,128)S(1)}, u32[]{:S(2)}, u32[]{:S(2)}) collective-permute-start(f32[72,128]{1,0:T(8,128)S(1)} %add.6), channel_id=1, source_target_pairs={{0,2},{2,0},{1,3},{3,1},{4,6},{6,4},{5,7},{7,5},{8,10},{10,8},{9,1... | collective-permute-start | bytes 110600 | tf_op jit(solution)/shard_map/ppermute | solution.py:320
  46.8 6.6 %collective-permute-start.4 = (f32[120,128]{1,0:T(8,128)S(1)}, f32[120,128]{1,0:T(8,128)S(1)}, u32[]{:S(2)}, u32[]{:S(2)}) collective-permute-start(f32[120,128]{1,0:T(8,128)S(1)} %pad_maximum_fusion.mine_ref), channel_id=1, source_target_pairs={{0,12},{4,8},{8,4},{12,0},{1,13},{5,9},{9,5},{13,1},{2,14},{6,10},... | collective-permute-start | bytes 184328 | tf_op jit(solution)/shard_map/ppermute | solution.py:320
  48.6 4.9 %collective-permute-start.3 = (f32[120,128]{1,0:T(8,128)S(1)}, f32[120,128]{1,0:T(8,128)S(1)}, u32[]{:S(2)}, u32[]{:S(2)}) collective-permute-start(f32[120,128]{1,0:T(8,128)S(1)} %pad_maximum_fusion.mine_ref), channel_id=1, source_target_pairs={{0,4},{4,0},{8,12},{12,8},{1,5},{5,1},{9,13},{13,9},{2,6},{6,2},{1... | collective-permute-start | bytes 184328 | tf_op jit(solution)/shard_map/ppermute | solution.py:320
  48.6 5.7 %collective-permute-start.2 = (f32[120,128]{1,0:T(8,128)S(1)}, f32[120,128]{1,0:T(8,128)S(1)}, u32[]{:S(2)}, u32[]{:S(2)}) collective-permute-start(f32[120,128]{1,0:T(8,128)S(1)} %pad_maximum_fusion.mine_ref), channel_id=1, source_target_pairs={{0,8},{4,12},{8,0},{12,4},{1,9},{5,13},{9,1},{13,5},{2,10},{6,14},... | collective-permute-start | bytes 184328 | tf_op jit(solution)/shard_map/ppermute | solution.py:320
  54.5 1.2 %collective-permute-start.5 = (f32[1,128]{1,0:T(1,128)S(1)}, f32[1,128]{1,0:T(1,128)S(1)}, u32[]{:S(2)}, u32[]{:S(2)}) collective-permute-start(f32[1,128]{1,0:T(1,128)S(1)} %get-tuple-element.61.refs_0_), channel_id=1, source_target_pairs={{0,1},{1,0},{2,3},{3,2},{4,5},{5,4},{6,7},{7,6},{8,9},{9,8},{10,11... | collective-permute-start | bytes 1544 | tf_op jit(solution)/shard_map/ppermute | solution.py:320

commit v9 on v8

--- a/solution.py
+++ b/solution.py
@@ -244,7 +244,7 @@
     omega = cross / square
     rho_next = b_half - omega * b_twice
     ratio = rho_next / rho
-    beta = ratio * (alpha / omega)
+    beta = ratio * (alpha * (square / cross))
     a = twice - (omega * back) * chunks_of(recv_ref, own_in)
     residual = half - omega * twice
     image = a + beta * q - ratio * u_ref[...]

time: 56.7 us -> 56.6 us (level)
  no operation moved by 1% of the time
where the time goes in v9:
time: 56.6 us; the launch traced here: 56.3 us
  blocking collectives  35.6 us (63%)
  waiting for transfers between devices  8.51 us (15%)
  Pallas kernels  6.28 us (11%)
  starting transfers between devices  5.19 us (9%)
  between operations  0.69 us (1%)
    all_to_all x3, blocking collectives, exchange(): lax.all_to_all(send, PART, 0, 0, tiled=True)  35.6 us
    ppermute x6, waiting for transfers between devices, shifted(): lax.ppermute(x, axis, [(i, partner(i, step, count)) for i in range(count)])  8.51 us
    pallas_call x7, Pallas kernels, call(): pl.pallas_call(kernel, out_shape=[pltpu.VMEM(shape, kind) if space == plt...  6.28 us
    ppermute x6, starting transfers between devices, shifted(): lax.ppermute(x, axis, [(i, partner(i, step, count)) for i in range(count)])  5.19 us
  transfers between devices with their start and end apart: 6, of which 6 were waited for; matrix products, arithmetic and copies ran while one was open for 0% of the time, Pallas kernels for 0%

profile of v9, /device:TPU:0, one launch (start us, length us, event | category | flops | bytes accessed | tf_op | source)
XLA Modules:
  0.0 56.3 jit_solution(17982507339218255863)
XLA Ops:
  0.6 2.9 %shard_map.86 = (f32[272,128]{1,0:T(8,128)S(1)}, f32[16,128]{1,0:T(8,128)S(1)}, f32[9,16,128]{2,1,0:T(8,128)S(1)}, bf16[272,144]{1,0:T(8,128)(2,1)S(1)}, bf16[14...) custom-call(f32[16,128]{1,0:T(8,128)} %b_hbm.1, ...), custom_call_target="tpu_custom_call" | custom-call | tf_op jit(solution)/shard_map/pallas_call | solution.py:334
  3.5 14.8 %all_to_all.15 = f32[16,17,1,128]{3,2,1,0:T(1,128)S(1)} all-to-all(f32[16,17,1,128]{3,2,1,0:T(1,128)S(1)} %bitcast.12), channel_id=1, replica_groups=mesh['groups'=2,'rows'=4,'cols'=2,'sub'=2] {'rows','sub','cols'}, dimensions={0} | all-to-all | bytes 278528 | tf_op jit(solution)/shard_map/all_to_all | solution.py:362
  18.3 0.7 %shard_map.87 = (f32[272,128]{1,0:T(8,128)S(1)}, f32[16,128]{1,0:T(8,128)S(1)}, f32[16,128]{1,0:T(8,128)S(1)}, f32[1,128]{1,0:T(1,128)S(1)}) custom-call(f32[272,128]{1,0:T(8,128)S(1)} %bitcast.10, f32[16,128]{1,0:T(8,128)S(1)} %get-tuple-element.33.own_in, f32[16,128]{1,0:T(8,128)S(1)} %get-tuple-element.34.b_ref, ...), custom_call_target="tpu_custom_call" | custom-call | tf_op jit(solution)/shard_map/pallas_call | solution.py:334
  19.0 10.4 %all_to_all.16 = f32[16,17,1,128]{3,2,1,0:T(1,128)S(1)} all-to-all(f32[16,17,1,128]{3,2,1,0:T(1,128)S(1)} %bitcast.13), channel_id=1, replica_groups=mesh['groups'=2,'rows'=4,'cols'=2,'sub'=2] {'rows','sub','cols'}, dimensions={0} | all-to-all | bytes 278528 | tf_op jit(solution)/shard_map/all_to_all | solution.py:362
  29.4 0.7 %shard_map.88 = (f32[272,128]{1,0:T(8,128)S(1)}, f32[16,128]{1,0:T(8,128)S(1)}, f32[16,128]{1,0:T(8,128)S(1)}, f32[16,128]{1,0:T(8,128)S(1)}, f32[16,128]{1,0:T(8,128)S(1)}, /*index=5*/f32[1,128]{1,0:T(1,128)S(1)}) custom-call(f32[272,128]{1,0:T(8,128)S(1)} %bitcast.9, f32[16,128]{1,0:T(8,128)S(1)} %get-tuple-element.40.own_in, ...), custom_call_target="tpu_custom_call" | custom-call | tf_op jit(solution)/shard_map/pallas_call | solution.py:334
  30.2 10.4 %all_to_all.17 = f32[16,17,1,128]{3,2,1,0:T(1,128)S(1)} all-to-all(f32[16,17,1,128]{3,2,1,0:T(1,128)S(1)} %bitcast.11), channel_id=1, replica_groups=mesh['groups'=2,'rows'=4,'cols'=2,'sub'=2] {'rows','sub','cols'}, dimensions={0} | all-to-all | bytes 278528 | tf_op jit(solution)/shard_map/all_to_all | solution.py:362
  40.6 0.9 %shard_map.89 = (f32[72,128]{1,0:T(8,128)S(1)}, f32[72,128]{1,0:T(8,128)S(1)}, f32[48,128]{1,0:T(8,128)S(1)}, f32[16,128]{1,0:T(8,128)S(1)}, f32[16,128]{1,0:T(8,128)S(1)}, /*index=5*/f32[1,128]{1,0:T(1,128)S(1)}) custom-call(f32[272,128]{1,0:T(8,128)S(1)} %bitcast.8, f32[16,128]{1,0:T(8,128)S(1)} %get-tuple-element.44.own_in, ...), custom_call_target="tpu_custom_call" | custom-call | tf_op jit(solution)/shard_map/pallas_call | solution.py:334
  41.5 0.2 collective-permute-start
  41.7 1.1 %collective-permute-done = f32[72,128]{1,0:T(8,128)S(1)} collective-permute-done((f32[72,128]{1,0:T(8,128)S(1)}, f32[72,128]{1,0:T(8,128)S(1)}, u32[]{:S(2)}, u32[]{:S(2)}) %collective-permute-start) | collective-permute-done | bytes 36896 | tf_op jit(solution)/shard_map/ppermute | solution.py:320
  42.8 0.6 %collective-permute-start.1 = (f32[72,128]{1,0:T(8,128)S(1)}, f32[72,128]{1,0:T(8,128)S(1)}, u32[]{:S(2)}, u32[]{:S(2)}) collective-permute-start(f32[72,128]{1,0:T(8,128)S(1)} %add.6), channel_id=1, source_target_pairs={{0,2},{2,0},{1,3},{3,1},{4,6},{6,4},{5,7},{7,5},{8,10},{10,8},{9,1... | collective-permute-start | bytes 110600 | tf_op jit(solution)/shard_map/ppermute | solution.py:320
  43.3 3.4 %collective-permute-done.1 = f32[72,128]{1,0:T(8,128)S(1)} collective-permute-done((f32[72,128]{1,0:T(8,128)S(1)}, f32[72,128]{1,0:T(8,128)S(1)}, u32[]{:S(2)}, u32[]{:S(2)}) %collective-permute-start.1) | collective-permute-done | bytes 36896 | tf_op jit(solution)/shard_map/ppermute | solution.py:320
  46.7 1.7 %collective-permute-start.4 = (f32[120,128]{1,0:T(8,128)S(1)}, f32[120,128]{1,0:T(8,128)S(1)}, u32[]{:S(2)}, u32[]{:S(2)}) collective-permute-start(f32[120,128]{1,0:T(8,128)S(1)} %pad_maximum_fusion.mine_ref), channel_id=1, source_target_pairs={{0,12},{4,8},{8,4},{12,0},{1,13},{5,9},{9,5},{13,1},{2,14},{6,10},... | collective-permute-start | bytes 184328 | tf_op jit(solution)/shard_map/ppermute | solution.py:320
  48.5 0.0 collective-permute-start.3
  48.5 2.7 %collective-permute-start.2 = (f32[120,128]{1,0:T(8,128)S(1)}, f32[120,128]{1,0:T(8,128)S(1)}, u32[]{:S(2)}, u32[]{:S(2)}) collective-permute-start(f32[120,128]{1,0:T(8,128)S(1)} %pad_maximum_fusion.mine_ref), channel_id=1, source_target_pairs={{0,8},{4,12},{8,0},{12,4},{1,9},{5,13},{9,1},{13,5},{2,10},{6,14},... | collective-permute-start | bytes 184328 | tf_op jit(solution)/shard_map/ppermute | solution.py:320
  51.2 2.1 %collective-permute-done.4.refs_2_ = f32[120,128]{1,0:T(8,128)S(1)} collective-permute-done((f32[120,128]{1,0:T(8,128)S(1)}, f32[120,128]{1,0:T(8,128)S(1)}, u32[]{:S(2)}, u32[]{:S(2)}) %collective-permute-start.4) | collective-permute-done | bytes 61472 | tf_op jit(solution)/shard_map/ppermute | solution.py:320
  53.3 0.1 collective-permute-done.3.refs_1_
  53.4 0.7 %collective-permute-done.2.refs_0_ = f32[120,128]{1,0:T(8,128)S(1)} collective-permute-done((f32[120,128]{1,0:T(8,128)S(1)}, f32[120,128]{1,0:T(8,128)S(1)}, u32[]{:S(2)}, u32[]{:S(2)}) %collective-permute-start.2) | collective-permute-done | bytes 61472 | tf_op jit(solution)/shard_map/ppermute | solution.py:320
  54.2 0.2 shard_map.90
  54.4 0.0 collective-permute-start.5
  54.4 0.1 shard_map.91
  54.5 1.0 %collective-permute-done.5.refs_1_ = f32[1,128]{1,0:T(1,128)S(1)} collective-permute-done((f32[1,128]{1,0:T(1,128)S(1)}, f32[1,128]{1,0:T(1,128)S(1)}, u32[]{:S(2)}, u32[]{:S(2)}) %collective-permute-start.5) | collective-permute-done | bytes 544 | tf_op jit(solution)/shard_map/ppermute | solution.py:320
  55.5 0.8 %shard_map.92 = (f32[16,128]{1,0:T(8,128)}, f32[16,128]{1,0:T(8,128)}) custom-call(f32[16,128]{1,0:T(8,128)S(1)} %get-tuple-element.56.twice_ref, f32[16,128]{1,0:T(8,128)S(1)} %get-tuple-element.57.half_ref, f32[16,128]{1,0:T(8,128)S(1)} %get-tuple-element.59.half_hat_ref, f32[16,128]{1,0:T(8,128)S(1)} %get-tuple-element.60.sum_hat_ref, ...), custom_call_target="tpu_custom_call" | custom-call | tf_op jit(solution)/shard_map/pallas_call | solution.py:334
  (3 shorter events, 0.0 us)
Async XLA Ops:
  41.5 1.3 %collective-permute-start = (f32[72,128]{1,0:T(8,128)S(1)}, f32[72,128]{1,0:T(8,128)S(1)}, u32[]{:S(2)}, u32[]{:S(2)}) collective-permute-start(f32[72,128]{1,0:T(8,128)S(1)} %get-tuple-element.51), channel_id=1, source_target_pairs={{0,1},{1,0},{2,3},{3,2},{4,5},{5,4},{6,7},{7,6},{8,9},{9,8},{10,11... | collective-permute-start | bytes 110600 | tf_op jit(solution)/shard_map/ppermute | solution.py:320
  42.8 4.0 %collective-permute-start.1 = (f32[72,128]{1,0:T(8,128)S(1)}, f32[72,128]{1,0:T(8,128)S(1)}, u32[]{:S(2)}, u32[]{:S(2)}) collective-permute-start(f32[72,128]{1,0:T(8,128)S(1)} %add.6), channel_id=1, source_target_pairs={{0,2},{2,0},{1,3},{3,1},{4,6},{6,4},{5,7},{7,5},{8,10},{10,8},{9,1... | collective-permute-start | bytes 110600 | tf_op jit(solution)/shard_map/ppermute | solution.py:320
  46.7 6.6 %collective-permute-start.4 = (f32[120,128]{1,0:T(8,128)S(1)}, f32[120,128]{1,0:T(8,128)S(1)}, u32[]{:S(2)}, u32[]{:S(2)}) collective-permute-start(f32[120,128]{1,0:T(8,128)S(1)} %pad_maximum_fusion.mine_ref), channel_id=1, source_target_pairs={{0,12},{4,8},{8,4},{12,0},{1,13},{5,9},{9,5},{13,1},{2,14},{6,10},... | collective-permute-start | bytes 184328 | tf_op jit(solution)/shard_map/ppermute | solution.py:320
  48.5 4.9 %collective-permute-start.3 = (f32[120,128]{1,0:T(8,128)S(1)}, f32[120,128]{1,0:T(8,128)S(1)}, u32[]{:S(2)}, u32[]{:S(2)}) collective-permute-start(f32[120,128]{1,0:T(8,128)S(1)} %pad_maximum_fusion.mine_ref), channel_id=1, source_target_pairs={{0,4},{4,0},{8,12},{12,8},{1,5},{5,1},{9,13},{13,9},{2,6},{6,2},{1... | collective-permute-start | bytes 184328 | tf_op jit(solution)/shard_map/ppermute | solution.py:320
  48.5 5.7 %collective-permute-start.2 = (f32[120,128]{1,0:T(8,128)S(1)}, f32[120,128]{1,0:T(8,128)S(1)}, u32[]{:S(2)}, u32[]{:S(2)}) collective-permute-start(f32[120,128]{1,0:T(8,128)S(1)} %pad_maximum_fusion.mine_ref), channel_id=1, source_target_pairs={{0,8},{4,12},{8,0},{12,4},{1,9},{5,13},{9,1},{13,5},{2,10},{6,14},... | collective-permute-start | bytes 184328 | tf_op jit(solution)/shard_map/ppermute | solution.py:320
  54.4 1.2 %collective-permute-start.5 = (f32[1,128]{1,0:T(1,128)S(1)}, f32[1,128]{1,0:T(1,128)S(1)}, u32[]{:S(2)}, u32[]{:S(2)}) collective-permute-start(f32[1,128]{1,0:T(1,128)S(1)} %get-tuple-element.61.refs_0_), channel_id=1, source_target_pairs={{0,1},{1,0},{2,3},{3,2},{4,5},{5,4},{6,7},{7,6},{8,9},{9,8},{10,11... | collective-permute-start | bytes 1544 | tf_op jit(solution)/shard_map/ppermute | solution.py:320
